TPU v7x, 32 devices: a whole 2x2x4 slice. The times are simulated.
32 devices in a mesh: batch: 8 (over y, x, core), seq: 4 (over z).
Axes of the slice: x: 2, y: 2, z: 4, core: 2. Of those that a mesh axis runs over, the one named last changes fastest.
Arguments:
- tokens: bfloat16 [16, 1824, 768], P('batch', 'seq'), may hold values from -6 to 6
- cotangent: bfloat16 [16, 1824, 768], P('batch', 'seq'), may hold values from -6 to 6
- tags: int32 [16], P('batch'), may hold values from 0 to 21
- loss_weights: float32 [22], replicated, may hold values from 0.25 to 4
- w_qkv: float32 [768, 896], P('batch'), may hold values from -0.109375 to 0.109375
- m_qkv: float32 [768, 896], P('batch'), may hold values from -0.00061035156 to 0.00061035156
- v_qkv: float32 [768, 896], P('batch'), may hold values from 1.6676273e-10 to 6.670509e-10
- w_out: float32 [768, 768], P('batch'), may hold values from -1.75 to 1.75
- m_out: float32 [768, 768], P('batch'), may hold values from -0.00012207031 to 0.00012207031
- v_out: float32 [768, 768], P('batch'), may hold values from 5.8513238e-12 to 2.3405295e-11
- w_up: float32 [768, 3072], P('batch'), may hold values from -0.21650635 to 0.21650635
- m_up: float32 [768, 3072], P('batch'), may hold values from -0.00061035156 to 0.00061035156
- v_up: float32 [768, 3072], P('batch'), may hold values from 1.6676273e-10 to 6.670509e-10
- w_down: float32 [3072, 768], P('batch'), may hold values from -0.109375 to 0.109375
- m_down: float32 [3072, 768], P('batch'), may hold values from -0.00061035156 to 0.00061035156
- v_down: float32 [3072, 768], P('batch'), may hold values from 1.6676273e-10 to 6.670509e-10
- norm_params: float32 [4, 768], P(None, 'batch'), may hold values from -1 to 6, as said below
- m_norm: float32 [4, 768], P(None, 'batch'), may hold values from -0.001953125 to 0.001953125
- v_norm: float32 [4, 768], P(None, 'batch'), may hold values from 1.5008645e-09 to 6.003458e-09
Outputs:
- layer_out: bfloat16 [16, 1824, 768], P('batch', 'seq')
- input_grad: bfloat16 [16, 1824, 768], P('batch', 'seq')
- grad_norm: float32 [], replicated
- qkv_new: float32 [768, 896], P('batch')
- qkv_first: float32 [768, 896], P('batch')
- qkv_second: float32 [768, 896], P('batch')
- out_new: float32 [768, 768], P('batch')
- out_first: float32 [768, 768], P('batch')
- out_second: float32 [768, 768], P('batch')
- up_new: float32 [768, 3072], P('batch')
- up_first: float32 [768, 3072], P('batch')
- up_second: float32 [768, 3072], P('batch')
- down_new: float32 [3072, 768], P('batch')
- down_first: float32 [3072, 768], P('batch')
- down_second: float32 [3072, 768], P('batch')
- norm_new: float32 [4, 768], P(None, 'batch')
- norm_first: float32 [4, 768], P(None, 'batch')
- norm_second: float32 [4, 768], P(None, 'batch')
Inputs may be any that keep to these rules, and one draw needn't show every extreme that they name: `norm_params`: rows 0 and 2 are positive gains, rows 1 and 3 biases.
All inputs are finite; a program needn't handle non-finite values.
Results may differ from a plain program's by a relative error of at most 0.0055.
The roundings to bfloat16 on the way count: a program that leaves them out, or rounds other values in their place, can miss the bound.
Values may be sent and summed in bfloat16 or wider, within the bound.
No kernel may reach another device: no remote copies, remote signals or barrier semaphores. Data moves between devices by JAX's collectives and lax.ppermute only.
A program may use at most 192 MiB of HBM per device.

v0:
```python
import jax
import jax.numpy as jnp
from jax import lax
from jax.sharding import PartitionSpec as P

D = 768
H = 12
HD = 64
ROT = 16
STEP = 10


EPS_NORM = 1e-05
BETA_ONE = 0.9
BETA_TWO = 0.999
ADAM_EPS = 1e-08
CLIP_NORM = 1.0
RATE_SMALL = 0.02
RATE_LARGE = 0.2
RATE_NORM = 1.0
DECAY = 0.1
ROWS_FIRST = (((0,), (0,)), ((), ()))
COLS_LAST = (((1,), (1,)), ((), ()))


def for_sending(x):
    return jax.tree.map(lambda a: a.astype(jnp.bfloat16) if a.dtype == jnp.float32 else a, x)


def layer_norm_parts(values, gain, shift):
    mean = jnp.mean(values, -1, keepdims=True)
    centered = values - mean
    scale = lax.rsqrt(jnp.mean(centered * centered, -1, keepdims=True) + EPS_NORM)
    normed = centered * scale
    return (normed, scale, normed * gain + shift)


def norm_back(grad_out, normed, scale, gain):
    grad_normed = grad_out * gain
    inner = jnp.mean(grad_normed, -1, keepdims=True)
    along = jnp.mean(grad_normed * normed, -1, keepdims=True)
    return scale * (grad_normed - inner - normed * along)


def rotate(values, cosine, sine):
    half = ROT // 2
    front = values[..., :ROT]
    turned = jnp.concatenate([-front[..., half:], front[..., :half]], -1)
    return jnp.concatenate([front * cosine + turned * sine, values[..., ROT:]], -1)


def angles(first, count):
    place = (first + jnp.arange(count)).astype(jnp.float32)
    inverse = 10000.0 ** (-jnp.arange(0, ROT, 2).astype(jnp.float32) / ROT)
    turn = place[:, None] * inverse[None, :]
    turn = jnp.concatenate([turn, turn], -1)
    return (jnp.cos(turn), jnp.sin(turn))


def adam_update(weight, first, second, grad, rate, decay):
    first_new = BETA_ONE * first + (1.0 - BETA_ONE) * grad
    second_new = BETA_TWO * second + (1.0 - BETA_TWO) * grad * grad
    step_one = first_new / (1.0 - BETA_ONE**STEP)
    step_two = second_new / (1.0 - BETA_TWO**STEP)
    weight_new = weight - rate * (step_one / (jnp.sqrt(step_two) + ADAM_EPS) + decay * weight)
    return (weight_new, first_new, second_new)


def shards(
    tokens,
    cotangent,
    tags,
    loss_weights,
    w_qkv,
    m_qkv,
    v_qkv,
    w_out,
    m_out,
    v_out,
    w_up,
    m_up,
    v_up,
    w_down,
    m_down,
    v_down,
    norm_params,
    m_norm,
    v_norm,
):
    low_type = jnp.bfloat16
    wide_type = jnp.float32
    seq_count = lax.axis_size("seq")
    full_qkv, full_out, full_up, full_down, full_norm = (
        lax.all_gather(w_qkv.astype(low_type), "batch", axis=0, tiled=True),
        lax.all_gather(w_out.astype(low_type), "batch", axis=0, tiled=True),
        lax.all_gather(w_up.astype(low_type), "batch", axis=0, tiled=True),
        lax.all_gather(w_down.astype(low_type), "batch", axis=0, tiled=True),
        lax.all_gather(norm_params.astype(low_type), "batch", axis=1, tiled=True),
    )
    gains = full_norm.astype(wide_type)
    seq_rows, local_len, width = tokens.shape
    count = seq_rows * local_len
    flat = tokens.astype(wide_type).reshape(count, width)
    normed_one, scale_one, first = layer_norm_parts(flat, gains[0], gains[1])
    first_low = first.astype(low_type)
    normed_two, scale_two, second = layer_norm_parts(flat, gains[2], gains[3])
    second_low = second.astype(low_type)
    mixed = jnp.dot(first_low, full_qkv, preferred_element_type=wide_type)
    cosine, sine = angles(lax.axis_index("seq") * local_len, local_len)
    cos_tok = jnp.tile(cosine, (seq_rows, 1))
    sin_tok = jnp.tile(sine, (seq_rows, 1))
    query = rotate(mixed[:, :D].reshape(count, H, HD), cos_tok[:, None, :], sin_tok[:, None, :])
    key_rot = rotate(mixed[:, D : D + HD], cos_tok, sin_tok)
    query_low = query.reshape(seq_rows, local_len, D).astype(low_type)
    pair_low = (
        jnp.concatenate([key_rot, mixed[:, D + HD :]], -1)
        .reshape(seq_rows, local_len, 2 * HD)
        .astype(low_type)
    )
    local_heads = H // seq_count
    head_width = local_heads * HD
    query_heads = lax.all_to_all(query_low, "seq", split_axis=2, concat_axis=1, tiled=True)
    pairs = lax.all_gather(pair_low, "seq", axis=1, tiled=True)
    length = query_heads.shape[1]
    block = length // 2
    scale = HD ** (-0.5)

    def block_scores(query_row, pair, part):
        key_count = block * (part + 1)
        q_rows = query_row[part * block : (part + 1) * block].reshape(block * local_heads, HD)
        keys = pair[:key_count, :HD]
        values = pair[:key_count, HD:]
        raw = lax.dot_general(q_rows, keys, COLS_LAST, preferred_element_type=wide_type) * scale
        places = part * block + jnp.arange(block * local_heads) // local_heads
        causal = places[:, None] >= jnp.arange(key_count)[None, :]
        return (q_rows, keys, values, raw, causal)

    def forward_row(pieces):
        query_row, pair = pieces
        outputs = []
        totals = []
        for part in range(2):
            q_rows, keys, values, raw, causal = block_scores(query_row, pair, part)
            masked = jnp.where(causal, raw, -1e30)
            top = jnp.max(masked, -1, keepdims=True)
            expo = jnp.exp(masked - top)
            total = jnp.sum(expo, -1, keepdims=True)
            probs = (expo / total).astype(low_type)
            out_rows = jnp.dot(probs, values, preferred_element_type=wide_type)
            outputs.append(out_rows.astype(low_type).reshape(block, head_width))
            totals.append((top + jnp.log(total))[:, 0])
        return (jnp.concatenate(outputs, 0), jnp.stack(totals))

    heads_done, log_totals = lax.map(forward_row, (query_heads, pairs))
    attn_seq = jax.tree.map(
        lambda part, own: part.astype(own.dtype),
        lax.all_to_all(for_sending(heads_done), "seq", split_axis=1, concat_axis=2, tiled=True),
        heads_done,
    )
    attn_flat = attn_seq.reshape(count, D)
    attention = jnp.dot(attn_flat, full_out, preferred_element_type=wide_type)
    up_pre = jnp.dot(second_low, full_up, preferred_element_type=wide_type)
    active, gelu_back = jax.vjp(lambda values: jax.nn.gelu(values, approximate=False), up_pre)
    active_low = active.astype(low_type)
    feed = jnp.dot(active_low, full_down, preferred_element_type=wide_type)
    layer_out = (flat + attention + feed).astype(low_type).reshape(seq_rows, local_len, D)
    subsets = jnp.arange(loss_weights.shape[0])
    row_weight = jnp.sum(
        jnp.where(tags[:, None] == subsets[None, :], loss_weights[None, :], 0.0), -1
    )
    grad_y = (cotangent.astype(wide_type) * row_weight[:, None, None]).reshape(count, D)
    grad_low = grad_y.astype(low_type)
    grad_down = lax.dot_general(active_low, grad_low, ROWS_FIRST, preferred_element_type=wide_type)
    grad_out_w = lax.dot_general(attn_flat, grad_low, ROWS_FIRST, preferred_element_type=wide_type)
    grad_active = lax.dot_general(grad_low, full_down, COLS_LAST, preferred_element_type=wide_type)
    grad_up_pre = gelu_back(grad_active)[0].astype(low_type)
    grad_up = lax.dot_general(second_low, grad_up_pre, ROWS_FIRST, preferred_element_type=wide_type)
    grad_second = lax.dot_general(grad_up_pre, full_up, COLS_LAST, preferred_element_type=wide_type)
    grad_heads_seq = (
        lax.dot_general(grad_low, full_out, COLS_LAST, preferred_element_type=wide_type)
        .astype(low_type)
        .reshape(seq_rows, local_len, D)
    )
    grad_heads = lax.all_to_all(grad_heads_seq, "seq", split_axis=2, concat_axis=1, tiled=True)

    def backward_row(pieces):
        query_row, pair, grad_row, lse_row = pieces
        query_parts = []
        pair_grad = jnp.zeros((length, 2 * HD), wide_type)
        for part in range(2):
            q_rows, keys, values, raw, causal = block_scores(query_row, pair, part)
            key_count = keys.shape[0]
            probs = jnp.where(causal, jnp.exp(raw - lse_row[part][:, None]), 0.0)
            grad_rows = grad_row[part * block : (part + 1) * block].reshape(block * local_heads, HD)
            grad_probs = lax.dot_general(
                grad_rows, values, COLS_LAST, preferred_element_type=wide_type
            )
            inner = jnp.sum(probs * grad_probs, -1, keepdims=True)
            grad_scores = (probs * (grad_probs - inner)).astype(low_type)
            grad_query = jnp.dot(grad_scores, keys, preferred_element_type=wide_type) * scale
            grad_key = (
                lax.dot_general(grad_scores, q_rows, ROWS_FIRST, preferred_element_type=wide_type)
                * scale
            )
            grad_value = lax.dot_general(
                probs.astype(low_type), grad_rows, ROWS_FIRST, preferred_element_type=wide_type
            )
            update = jnp.concatenate([grad_key, grad_value], -1)
            pair_grad = pair_grad + jnp.pad(update, ((0, length - key_count), (0, 0)))
            query_parts.append(grad_query.astype(low_type).reshape(block, head_width))
        return (jnp.concatenate(query_parts, 0), pair_grad)

    query_grads, pair_grads = lax.map(backward_row, (query_heads, pairs, grad_heads, log_totals))
    grad_query_seq = jax.tree.map(
        lambda part, own: part.astype(own.dtype),
        lax.all_to_all(for_sending(query_grads), "seq", split_axis=1, concat_axis=2, tiled=True),
        query_grads,
    )
    grad_pair = lax.psum_scatter(pair_grads, "seq", scatter_dimension=1, tiled=True)
    grad_pair = (
        lax.optimization_barrier(grad_pair.astype(low_type))
        .astype(wide_type)
        .reshape(count, 2 * HD)
    )
    grad_query = rotate(
        grad_query_seq.astype(wide_type).reshape(count, H, HD),
        cos_tok[:, None, :],
        -sin_tok[:, None, :],
    )
    grad_key = rotate(grad_pair[:, :HD], cos_tok, -sin_tok)
    grad_mixed = jnp.concatenate(
        [grad_query.reshape(count, D), grad_key, grad_pair[:, HD:]], -1
    ).astype(low_type)
    grad_qkv = lax.dot_general(first_low, grad_mixed, ROWS_FIRST, preferred_element_type=wide_type)
    grad_first = lax.dot_general(grad_mixed, full_qkv, COLS_LAST, preferred_element_type=wide_type)
    grad_input = (
        grad_y
        + norm_back(grad_first, normed_one, scale_one, gains[0])
        + norm_back(grad_second, normed_two, scale_two, gains[2])
    )
    input_grad = grad_input.astype(low_type).reshape(seq_rows, local_len, D)
    grad_norm_params = jnp.stack(
        [
            jnp.sum(grad_first * normed_one, 0),
            jnp.sum(grad_first, 0),
            jnp.sum(grad_second * normed_two, 0),
            jnp.sum(grad_second, 0),
        ]
    )
    sum_qkv, sum_out, sum_up, sum_down, sum_norm = (
        lax.psum_scatter(grad_qkv, "batch", scatter_dimension=0, tiled=True),
        lax.psum_scatter(grad_out_w, "batch", scatter_dimension=0, tiled=True),
        lax.psum_scatter(grad_up, "batch", scatter_dimension=0, tiled=True),
        lax.psum_scatter(grad_down, "batch", scatter_dimension=0, tiled=True),
        lax.psum_scatter(grad_norm_params, "batch", scatter_dimension=1, tiled=True),
    )
    summed = lax.psum((sum_qkv, sum_out, sum_up, sum_down, sum_norm), "seq")
    local_squares = jnp.float32(0.0)
    for grad in summed:
        local_squares = local_squares + jnp.sum(grad * grad)
    total_squares = lax.psum(local_squares, "batch")
    grad_norm = jnp.sqrt(total_squares)
    factor = CLIP_NORM / jnp.maximum(grad_norm, CLIP_NORM)
    masters = (w_qkv, w_out, w_up, w_down, norm_params)
    firsts = (m_qkv, m_out, m_up, m_down, m_norm)
    seconds = (v_qkv, v_out, v_up, v_down, v_norm)
    rates = (RATE_SMALL, RATE_LARGE, RATE_SMALL, RATE_SMALL, RATE_NORM)
    decays = (DECAY, DECAY, DECAY, DECAY, 0.0)
    results = []
    for index in range(5):
        results.extend(
            adam_update(
                masters[index],
                firsts[index],
                seconds[index],
                summed[index] * factor,
                rates[index],
                decays[index],
            )
        )
    return (
        layer_out,
        input_grad,
        grad_norm,
        results[0],
        results[1],
        results[2],
        results[3],
        results[4],
        results[5],
        results[6],
        results[7],
        results[8],
        results[9],
        results[10],
        results[11],
        results[12],
        results[13],
        results[14],
    )


def solution(mesh):
    in_specs = (
        P("batch", "seq", None),
        P("batch", "seq", None),
        P("batch"),
        P(),
        P("batch", None),
        P("batch", None),
        P("batch", None),
        P("batch", None),
        P("batch", None),
        P("batch", None),
        P("batch", None),
        P("batch", None),
        P("batch", None),
        P("batch", None),
        P("batch", None),
        P("batch", None),
        P(None, "batch"),
        P(None, "batch"),
        P(None, "batch"),
    )
    out_specs = (
        P("batch", "seq", None),
        P("batch", "seq", None),
        P(),
        P("batch", None),
        P("batch", None),
        P("batch", None),
        P("batch", None),
        P("batch", None),
        P("batch", None),
        P("batch", None),
        P("batch", None),
        P("batch", None),
        P("batch", None),
        P("batch", None),
        P("batch", None),
        P(None, "batch"),
        P(None, "batch"),
        P(None, "batch"),
    )
    return jax.shard_map(shards, mesh=mesh, in_specs=in_specs, out_specs=out_specs, check_vma=False)
```

profile of v0, /device:TPU:0, one launch (start us, length us, event | category | flops | bytes accessed | tf_op | source)
XLA Modules:
  0.0 1049.3 jit_solution(6613265956624384278)
XLA Ops:
  14.1 10.4 all-gather
  100.3 43.3 %all_gather.20 = bf16[2,1824,128]{2,1,0:T(8,128)(2,1)} all-gather(bf16[2,456,128]{2,1,0:T(8,128)(2,1)S(1)} %bitcast.183), channel_id=1, replica_groups=mesh['batch'=8,'seq'=4] {'seq'}, dimensions={1}, use_global_device_ids=true | all-gather | bytes 1167360 | tf_op jit(solution)/shard_map/all_gather | solution.py:123
  151.6 84.9 %while.28 = (s32[]{:T(128)}, bf16[2,1824,192]{2,1,0:T(8,128)(2,1)}, f32[2,2,2736]{2,1,0:T(2,128)}, bf16[2,1824,192]{2,1,0:T(8,128)(2,1)}, bf16[2,1824,128]{2,1,0:T(8,128)(2,1)}, /*index=5*/s32[]{:T(128)}, s32[]{:T(128)}, s32[]{}) while((s32[]{:T(128)}, bf16[2,1824,192]{2,1,0:T(8,128)(2,1)}, f32[2,2,2736]{2,1,0:T(2,128)}, ...), condition=%wide.region_7.8_spmd, body=%wide.region_2.7_spmd.sunk | while | flops 2000478464 | bytes 101778040 | solution.py:154
  236.4 14.9 %copy.150 = bf16[2,1824,192]{2,0,1:T(2,128)(2,1)} copy(bf16[2,1824,192]{2,1,0:T(8,128)(2,1)} %get-tuple-element.177) | data formatting | bytes 2801664 | tf_op jit(solution)/shard_map/while | solution.py:154
  257.6 232.7 %while.29 = (s32[]{:T(128)}, bf16[2,1824,192]{2,1,0:T(8,128)(2,1)}, f32[2,1824,128]{2,0,1:T(2,128)}, bf16[2,1824,192]{2,1,0:T(8,128)(2,1)}, bf16[2,1824,128]{2,1...) while((s32[]{:T(128)}, bf16[2,1824,192]{2,1,0:T(8,128)(2,1)}, ...), condition=%wide.region_12.13_spmd, body=%wide.region_9.12_spmd.sunk | while | flops 4869421056 | bytes 350656032 | solution.py:213
  274.4 10.5 %multiply_convert_fusion.6 = bf16[2736,912]{0,1:T(8,128)(2,1)} fusion(f32[2736,912]{0,1:T(8,128)} %copy-done, f32[2736,912]{0,1:T(8,128)} %copy-done.1, f32[2736]{0:T(1024)} %get-tuple-element.437), kind=kLoop, calls=%fused_computation.45.clone.1 | loop fusion | flops 7485696 | bytes 24963264 | tf_op jit(solution)/shard_map/while/body/eval_jaxpr/convert_element_type | solution.py:199
  300.4 18.0 %multiply_reduce_fusion.15 = (f32[2736]{0:T(1024)S(1)}, f32[2736,1824]{0,1:T(8,128)}) fusion(f32[2736,1824]{0,1:T(8,128)} %fusion.189, f32[2736]{0:T(1024)S(1)} %get-tuple-element.429, bf16[2736,64]{1,0:T(8,128)(2,1)S(1)} %reshape.423, bf16[1824,128]{1,0:T(8,128)(2,1)S(1)} %dynamic-slice_bitcast_fusion.5, s32[2736]{0:T(1024)S(1)} %broadcast_add_fusion.5), kind=kOutput, calls=%fused_computation.40.clone.1 | convolution fusion | flops 668719424 | bytes 40773696 | tf_op jit(solution)/shard_map/while/body/eval_jaxpr/dot_general | solution.py:133
  328.3 13.5 %multiply_convert_fusion.5 = bf16[2736,1824]{0,1:T(8,128)(2,1)S(1)} fusion(f32[2736,1824]{0,1:T(8,128)} %get-tuple-element.431, f32[2736,1824]{0,1:T(8,128)} %fusion.189, f32[2736]{0:T(1024)S(1)} %get-tuple-element.432), kind=kLoop, calls=%fused_computation.39.clone.1 | loop fusion | flops 14971392 | bytes 49915584 | tf_op jit(solution)/shard_map/while/body/eval_jaxpr/convert_element_type | solution.py:199
  350.1 23.7 %dynamic_update_slice.37 = f32[2,1824,128]{2,0,1:T(2,128)} dynamic-update-slice(f32[2,1824,128]{2,0,1:T(2,128)} %get-tuple-element.475, f32[1,1824,128]{2,0,1:T(1,128)S(1)} %copy.198, s32[]{:T(128)S(6)} %copy.215, s32[]{:T(128)} %constant.139.clone.1..sunk.1, s32[]{:T(128)} %constant.139.clone.1..sunk.1) | dynamic-update-slice | bytes 1867780 | tf_op jit(solution)/shard_map/while/body/jit(dynamic_update_index_in_dim)/dynamic_update_slice | solution.py:213
  390.4 10.5 %multiply_convert_fusion.6 = bf16[2736,912]{0,1:T(8,128)(2,1)} fusion(f32[2736,912]{0,1:T(8,128)} %copy-done, f32[2736,912]{0,1:T(8,128)} %copy-done.1, f32[2736]{0:T(1024)} %get-tuple-element.437), kind=kLoop, calls=%fused_computation.45.clone.1 | loop fusion | flops 7485696 | bytes 24963264 | tf_op jit(solution)/shard_map/while/body/eval_jaxpr/convert_element_type | solution.py:199
  416.4 18.0 %multiply_reduce_fusion.15 = (f32[2736]{0:T(1024)S(1)}, f32[2736,1824]{0,1:T(8,128)}) fusion(f32[2736,1824]{0,1:T(8,128)} %fusion.189, f32[2736]{0:T(1024)S(1)} %get-tuple-element.429, bf16[2736,64]{1,0:T(8,128)(2,1)S(1)} %reshape.423, bf16[1824,128]{1,0:T(8,128)(2,1)S(1)} %dynamic-slice_bitcast_fusion.5, s32[2736]{0:T(1024)S(1)} %broadcast_add_fusion.5), kind=kOutput, calls=%fused_computation.40.clone.1 | convolution fusion | flops 668719424 | bytes 40773696 | tf_op jit(solution)/shard_map/while/body/eval_jaxpr/dot_general | solution.py:133
  444.3 13.5 %multiply_convert_fusion.5 = bf16[2736,1824]{0,1:T(8,128)(2,1)S(1)} fusion(f32[2736,1824]{0,1:T(8,128)} %get-tuple-element.431, f32[2736,1824]{0,1:T(8,128)} %fusion.189, f32[2736]{0:T(1024)S(1)} %get-tuple-element.432), kind=kLoop, calls=%fused_computation.39.clone.1 | loop fusion | flops 14971392 | bytes 49915584 | tf_op jit(solution)/shard_map/while/body/eval_jaxpr/convert_element_type | solution.py:199
  466.1 23.7 %dynamic_update_slice.37 = f32[2,1824,128]{2,0,1:T(2,128)} dynamic-update-slice(f32[2,1824,128]{2,0,1:T(2,128)} %get-tuple-element.475, f32[1,1824,128]{2,0,1:T(1,128)S(1)} %copy.198, s32[]{:T(128)S(6)} %copy.215, s32[]{:T(128)} %constant.139.clone.1..sunk.1, s32[]{:T(128)} %constant.139.clone.1..sunk.1) | dynamic-update-slice | bytes 1867780 | tf_op jit(solution)/shard_map/while/body/jit(dynamic_update_index_in_dim)/dynamic_update_slice | solution.py:213
  490.2 14.9 %copy.157 = bf16[2,1824,192]{2,0,1:T(2,128)(2,1)} copy(bf16[2,1824,192]{2,1,0:T(8,128)(2,1)} %get-tuple-element.179) | data formatting | bytes 2801664 | tf_op jit(solution)/shard_map/while | solution.py:213
  526.6 84.1 %all-reduce.7 = bf16[2,1824,128]{2,0,1:T(2,128)(2,1)S(1)} all-reduce(f32[2,1824,128]{2,0,1:T(2,128)} %get-tuple-element.180), channel_id=2, replica_groups=mesh['batch'=8,'seq'=4] {'seq'}, use_global_device_ids=true, to_apply=%region_13.14.clone | all-reduce | flops 466944 | bytes 2801664
  635.4 33.3 %add_convert_fusion = (bf16[912,3072]{1,0:T(8,128)(2,1)}, f32[912,3072]{1,0:T(8,128)S(1)}) fusion(f32[912,3072]{1,0:T(8,128)} %fusion.80, bf16[912,768]{1,0:T(8,128)(2,1)S(1)} %copy-done.32, bf16[3072,768]{1,0:T(8,128)(2,1)} %all-gather.12.cloned.1.call-done), kind=kOutput, calls=%fused_computation.88 | convolution fusion | flops 4505075712 | bytes 34136064 | tf_op jit(solution)/shard_map/dot_general | solution.py:175
  685.8 10.6 %fusion.83 = f32[768,3072]{1,0:T(8,128)} fusion(bf16[912,768]{1,0:T(8,128)(2,1)S(1)} %copy-done.28, bf16[912,3072]{1,0:T(8,128)(2,1)} %get-tuple-element.294), kind=kOutput, calls=%fused_computation.210 | convolution fusion | flops 4303355904 | bytes 16441344 | tf_op jit(solution)/shard_map/dot_general | solution.py:177
  701.8 12.2 %multiply_reduce_fusion.2 = (f32[768]{0:T(1024)S(1)}, f32[768]{0:T(1024)S(1)}, f32[912]{0:T(1024)S(1)}, f32[912]{0:T(1024)S(1)}, f32[912]{0:T(1024)S(1)}, /*inde...) fusion(bf16[2,456,768]{2,1,0:T(8,128)(2,1)S(1)} %copy-done.7, f32[912]{0:T(1024)S(1)} %copy-done.49, ...), kind=kOutput, calls=%fused_computation.116 | convolution fusion | flops 4315254784 | bytes 20168064 | tf_op jit(solution)/shard_map/dot_general | solution.py:178
  715.1 46.1 %reduce-scatter.14.cloned.1.call-done = f32[384,768]{1,0:T(8,128)} async-done(((f32[3072,768]{1,0:T(8,128)}), f32[384,768]{1,0:T(8,128)}) %reduce-scatter.14.cloned.1.call-update) | async-done | bytes 1179664 | tf_op jit(solution)/shard_map/reduce_scatter | solution.py:254
  761.2 80.0 %reduce-scatter.12.cloned.1.call-done = f32[96,3072]{1,0:T(8,128)} async-done(((f32[768,3072]{1,0:T(8,128)}), f32[96,3072]{1,0:T(8,128)}) %reduce-scatter.12.cloned.1.call-update) | async-done | bytes 1179664 | tf_op jit(solution)/shard_map/reduce_scatter | solution.py:253
  856.0 22.7 %reduce-scatter.16.cloned.1.call-done = f32[96,4]{1,0:T(8,128)} async-done(((f32[768,4]{1,0:T(8,128)}), f32[96,4]{1,0:T(8,128)}) %reduce-scatter.16.cloned.1.call-update) | async-done | bytes 1552
  879.6 12.1 %psum.46 = f32[4,96]{1,0:T(4,128)S(1)} all-reduce(f32[4,96]{1,0:T(4,128)S(1)} %copy.166), channel_id=1, replica_groups=mesh['batch'=8,'seq'=4] {'seq'}, use_global_device_ids=true, to_apply=%region_35.36 | all-reduce | flops 384 | bytes 3072 | tf_op jit(solution)/shard_map/psum | solution.py:257
  892.3 106.5 %all-reduce.6.cloned.1.call-done = (f32[96,896]{1,0:T(8,128)}, f32[96,768]{1,0:T(8,128)}, f32[96,3072]{1,0:T(8,128)}, f32[384,768]{1,0:T(8,128)}) async-done(((f32[96,896]{1,0:T(8,128)}, f32[96,768]{1,0:T(8,128)}, f32[96,3072]{1,0:T(8,128)}, f32[384,768]{1,0:T(8,128)}), (f32[96,896]{1,0:T(8,128)}, f32[96,768]{1,0:T(8,128)}, f32[96,3072]{1,0:T(8,128)}, f32[384,768]{1,0:T(8,128)})) %all-reduce.6.cloned.1.call-update) | async-done | bytes 2998288 | tf_op jit(solution)/shard_map/psum | solution.py:257
  1014.4 14.2 %psum.47 = f32[]{:T(128)} all-reduce(f32[]{:T(128)S(6)} %add.299), channel_id=1, replica_groups=mesh['batch'=8,'seq'=4] {'batch'}, use_global_device_ids=true, to_apply=%region_37.38 | all-reduce | flops 1 | bytes 8 | tf_op jit(solution)/shard_map/psum | solution.py:261
  (353 shorter events, 389.7 us)
Async XLA Ops:
  7.2 30.1 %all-gather.8.cloned.1.call-start = ((), (), s32[]{:S(2)}) async-start(), calls=%async_computation.10 | async-start | bytes 1327104 | tf_op jit(solution)/shard_map/all_gather | solution.py:95
  9.0 55.7 %all-gather.6.cloned.1.call-start = ((), (), s32[]{:S(2)}) async-start(), calls=%async_computation.9 | async-start | bytes 1548288 | tf_op jit(solution)/shard_map/all_gather | solution.py:94
  10.8 614.7 %all-gather.10.cloned.1.call-start = ((), (), s32[]{:S(2)}) async-start(), calls=%async_computation.11 | async-start | bytes 5308416 | tf_op jit(solution)/shard_map/all_gather | solution.py:96
  13.5 38.0 %copy-start.46 = (f32[912]{0:T(1024)}, f32[912]{0:T(1024)S(1)}, u32[]{:S(2)}) copy-start(f32[912]{0:T(1024)S(1)} %div.176) | copy-start | bytes 10948
  14.1 37.4 %copy-start.48 = (f32[912]{0:T(1024)}, f32[912]{0:T(1024)S(1)}, u32[]{:S(2)}) copy-start(f32[912]{0:T(1024)S(1)} %rsqrt.13) | copy-start | bytes 10948
  46.0 42.1 %all-to-all-start.2 = ((bf16[2,456,768]{1,0,2:T(2,128)(2,1)}), bf16[2,456,768]{1,0,2:T(2,128)(2,1)}, u32[]{:S(2)}, u32[]{:S(2)}) async-start(bf16[2,456,768]{1,0,2:T(2,128)(2,1)} %copy.152), calls=%async_computation.2 | async-start | bytes 3145728 | tf_op jit(solution)/shard_map/all_to_all | solution.py:184
  50.9 45.5 %copy-start.17 = (f32[456,16]{1,0:T(8,128)}, f32[456,16]{1,0:T(8,128)S(1)}, u32[]{:S(2)}) copy-start(f32[456,16]{1,0:T(8,128)S(1)} %copy.143) | copy-start | bytes 87556
  51.0 45.4 %copy-start.19 = (f32[456,16]{1,0:T(8,128)}, f32[456,16]{1,0:T(8,128)S(1)}, u32[]{:S(2)}) copy-start(f32[456,16]{1,0:T(8,128)S(1)} %copy.145) | copy-start | bytes 87556
  51.4 23.6 %copy-start.37 = (f32[912,16]{0,1:T(8,128)}, f32[912,16]{0,1:T(8,128)S(1)}, u32[]{:S(2)}) copy-start(f32[912,16]{0,1:T(8,128)S(1)} %copy.144) | copy-start | bytes 175108
  88.1 59.5 %all-to-all-start = ((bf16[2,456,768]{1,0,2:T(2,128)(2,1)}), bf16[2,456,768]{1,0,2:T(2,128)(2,1)S(1)}, u32[]{:S(2)}, u32[]{:S(2)}) async-start(bf16[2,456,768]{1,0,2:T(2,128)(2,1)} %convert_element_type.164), calls=%async_computation | async-start | bytes 3145728 | tf_op jit(solution)/shard_map/all_to_all | solution.py:122
  91.6 543.8 %all-gather.12.cloned.1.call-start = ((), (), s32[]{:S(2)}) async-start(), calls=%async_computation.12 | async-start | bytes 5308416 | tf_op jit(solution)/shard_map/all_gather | solution.py:97
  251.3 253.8 %all-to-all-start.1 = ((bf16[2,1824,192]{2,0,1:T(2,128)(2,1)}), bf16[2,1824,192]{2,0,1:T(2,128)(2,1)}, u32[]{:S(2)}, u32[]{:S(2)}) async-start(bf16[2,1824,192]{2,0,1:T(2,128)(2,1)} %copy.150), calls=%async_computation.1 | async-start | bytes 3735552 | tf_op jit(solution)/shard_map/all_to_all | solution.py:157
  505.1 107.4 %all-to-all-start.3 = ((bf16[2,1824,192]{2,0,1:T(2,128)(2,1)}), bf16[2,1824,192]{2,0,1:T(2,128)(2,1)S(1)}, u32[]{:S(2)}, u32[]{:S(2)}) async-start(bf16[2,1824,192]{2,0,1:T(2,128)(2,1)} %copy.157), calls=%async_computation.3 | async-start | bytes 3735552 | tf_op jit(solution)/shard_map/all_to_all | solution.py:216
  510.2 204.9 %reduce-scatter.10.cloned.1.call-start = ((), (), s32[]{:S(2)}) async-start(), calls=%async_computation.14 | async-start | bytes 2654208 | tf_op jit(solution)/shard_map/reduce_scatter | solution.py:252
  526.6 188.5 %reduce-scatter.8.cloned.1.call-start = ((), (), s32[]{:S(2)}) async-start(), calls=%async_computation.13 | async-start | bytes 3096576 | tf_op jit(solution)/shard_map/reduce_scatter | solution.py:251
  625.4 135.7 %reduce-scatter.14.cloned.1.call-start = ((), (), s32[]{:S(2)}) async-start(), calls=%async_computation.16 | async-start | bytes 10616832 | tf_op jit(solution)/shard_map/reduce_scatter | solution.py:254
  684.5 156.8 %reduce-scatter.12.cloned.1.call-start = ((), (), s32[]{:S(2)}) async-start(), calls=%async_computation.15 | async-start | bytes 10616832 | tf_op jit(solution)/shard_map/reduce_scatter | solution.py:253
  696.5 182.2 %reduce-scatter.16.cloned.1.call-start = ((), (), s32[]{:S(2)}) async-start(), calls=%async_computation.17 | async-start | bytes 442368
  714.0 127.3 %copy-start.5 = (f32[2,456,768]{2,1,0:T(8,128)S(1)}, f32[2,456,768]{2,1,0:T(8,128)}, u32[]{:S(2)}) copy-start(f32[2,456,768]{2,1,0:T(8,128)} %copy-done.4) | copy-start | bytes 8404996
  715.0 283.8 %all-reduce.6.cloned.1.call-start = ((), (), s32[]{:S(2)}) async-start(), calls=%async_computation.18 | async-start | bytes 5996544 | tf_op jit(solution)/shard_map/psum | solution.py:257
  856.0 153.6 %copy-start.8 = (bf16[2,456,768]{2,1,0:T(8,128)(2,1)S(1)}, bf16[2,456,768]{2,1,0:T(8,128)(2,1)}, u32[]{:S(2)}) copy-start(bf16[2,456,768]{2,1,0:T(8,128)(2,1)} %param.23) | copy-start | bytes 4202500
  856.0 153.7 %copy-start.23 = (bf16[912,768]{0,1:T(8,128)(2,1)S(1)}, bf16[912,768]{0,1:T(8,128)(2,1)}, u32[]{:S(2)}) copy-start(bf16[912,768]{0,1:T(8,128)(2,1)} %reshape.387) | copy-start | bytes 4202500
  1009.7 22.6 %copy-start.33 = (f32[96,896]{1,0:T(8,128)S(1)}, f32[96,896]{1,0:T(8,128)}, u32[]{:S(2)}) copy-start(f32[96,896]{1,0:T(8,128)} %param.27) | copy-start | bytes 1032196
  1014.4 20.2 %copy-start.16 = (f32[384,768]{1,0:T(8,128)S(1)}, f32[384,768]{1,0:T(8,128)}, u32[]{:S(2)}) copy-start(f32[384,768]{1,0:T(8,128)} %get-tuple-element.278) | copy-start | bytes 3538948
  (54 other events, 323.2 us)
Sparse Core Ops, SparseCore 0:
  10.5 26.8 all-gather.7
  39.8 24.8 all-gather.5
  67.2 38.9 all-gather.9
  108.4 38.9 all-gather.11
  526.7 42.8 reduce-scatter.9
  625.6 44.3 reduce-scatter.7
  684.6 76.5 reduce-scatter.13
  764.7 76.4 reduce-scatter.11
  844.8 33.8 reduce-scatter.15
  881.2 117.5 all-reduce.5
where the time goes:
time: 1060 us; the launch traced here: 1050 us
  waiting for transfers between devices  283 us (27%)
  matrix products  261 us (25%)
  local copies, waits for them, and re-layouts  171 us (16%)
  blocking collectives  164 us (15%)
  other arithmetic  128 us (12%)
  between operations  21.3 us (2%)
  starting transfers between devices  18.7 us (2%)
    psum x1, waiting for transfers between devices, shards(): summed = lax.psum((sum_qkv, sum_out, sum_up, sum_down, sum_norm), 'seq')  106 us
    unnamed x1, blocking collectives  84.1 us
    reduce_scatter x1, waiting for transfers between devices, shards(): lax.psum_scatter(grad_up, 'batch', scatter_dimension=0, tiled=True)  80 us
    dot_general x8, matrix products, block_scores(): lax.dot_general(q_rows, keys, COLS_LAST, preferred_element_type=wide_type)  65.2 us
    dynamic_update_slice x4, local copies, waits for them, and re-layouts, shards(): lax.map(backward_row, (query_heads, pairs, grad_heads, log_totals))  49.2 us
    convert_element_type x4, other arithmetic, backward_row(): grad_scores = (probs * (grad_probs - inner)).astype(low_type)  48.1 us
    reduce_scatter x1, waiting for transfers between devices, shards(): lax.psum_scatter(grad_down, 'batch', scatter_dimension=0, tiled=True)  46.1 us
    all_gather x1, blocking collectives, shards(): pairs = lax.all_gather(pair_low, 'seq', axis=1, tiled=True)  43.3 us
  transfers between devices with their start and end apart: 14, of which 7 were waited for; matrix products, arithmetic and copies ran while one was open for 49% of the time, Pallas kernels for 0%

commit v1 on v0

v1 whole, which is shorter than its diff:
```python
import functools

import jax
import jax.numpy as jnp
from jax import lax
from jax.experimental import pallas as pl
from jax.experimental.pallas import tpu as pltpu
from jax.sharding import PartitionSpec as P

D = 768
H = 12
HD = 64
ROT = 16
STEP = 10


EPS_NORM = 1e-05
BETA_ONE = 0.9
BETA_TWO = 0.999
ADAM_EPS = 1e-08
CLIP_NORM = 1.0
RATE_SMALL = 0.02
RATE_LARGE = 0.2
RATE_NORM = 1.0
DECAY = 0.1
ROWS_FIRST = (((0,), (0,)), ((), ()))
COLS_LAST = (((1,), (1,)), ((), ()))


def layer_norm_parts(values, gain, shift):
    mean = jnp.mean(values, -1, keepdims=True)
    centered = values - mean
    scale = lax.rsqrt(jnp.mean(centered * centered, -1, keepdims=True) + EPS_NORM)
    normed = centered * scale
    return (normed, scale, normed * gain + shift)


def norm_back(grad_out, normed, scale, gain):
    grad_normed = grad_out * gain
    inner = jnp.mean(grad_normed, -1, keepdims=True)
    along = jnp.mean(grad_normed * normed, -1, keepdims=True)
    return scale * (grad_normed - inner - normed * along)


def rotate(values, cosine, sine):
    half = ROT // 2
    front = values[..., :ROT]
    turned = jnp.concatenate([-front[..., half:], front[..., :half]], -1)
    return jnp.concatenate([front * cosine + turned * sine, values[..., ROT:]], -1)


def angles(first, count):
    place = (first + jnp.arange(count)).astype(jnp.float32)
    inverse = 10000.0 ** (-jnp.arange(0, ROT, 2).astype(jnp.float32) / ROT)
    turn = place[:, None] * inverse[None, :]
    turn = jnp.concatenate([turn, turn], -1)
    return (jnp.cos(turn), jnp.sin(turn))


def adam_update(weight, first, second, grad, rate, decay):
    first_new = BETA_ONE * first + (1.0 - BETA_ONE) * grad
    second_new = BETA_TWO * second + (1.0 - BETA_TWO) * grad * grad
    step_one = first_new / (1.0 - BETA_ONE**STEP)
    step_two = second_new / (1.0 - BETA_TWO**STEP)
    weight_new = weight - rate * (step_one / (jnp.sqrt(step_two) + ADAM_EPS) + decay * weight)
    return (weight_new, first_new, second_new)


BF = jnp.bfloat16
F32 = jnp.float32
ROWS = 128
KEYS = 256


def attention_body(
    place,
    q_ref,
    do_ref,
    kv_ref,
    o_ref,
    dq_ref,
    dkv_ref,
    k_rows,
    v_rows,
    k_cols,
    v_cols,
    scores,
    out_acc,
    dq_acc,
    dkv_acc,
    *,
    local,
):
    step = pl.program_id(1)
    chunks = scores.shape[0]
    wide = H * ROWS

    @pl.when(step == 0)
    def _():
        def prepare(j, carry):
            rows = pl.ds(pl.multiple_of(j * KEYS, KEYS), KEYS)
            pair = kv_ref[0, rows, :]
            k_rows[rows, :] = pair[:, :HD]
            v_rows[rows, :] = pair[:, HD:]
            turned = pair.T
            k_cols[j] = turned[:HD]
            v_cols[j] = turned[HD:]
            dkv_acc[rows, :] = jnp.zeros((KEYS, 2 * HD), F32)
            return carry

        lax.fori_loop(0, chunks, prepare, 0)

    start = place[0] * local + step * ROWS
    last = jnp.minimum(start + ROWS - 1, (place[0] + 1) * local - 1)
    open_chunks = (start + 1) // KEYS
    all_chunks = last // KEYS + 1

    def heads_in_columns(x):
        turned = [x[:, 2 * HD * p : 2 * HD * (p + 1)].T for p in range(H // 2)]
        return jnp.concatenate([t[a : a + HD] for t in turned for a in (0, HD)], 1)

    def heads_in_rows(x):
        return jnp.concatenate([x[:, HD * h : HD * (h + 1)] for h in range(H)], 0)

    def heads_side_by_side(t):
        return jnp.concatenate(
            [
                jnp.concatenate(
                    [
                        t[:, 2 * p * ROWS : (2 * p + 1) * ROWS],
                        t[:, (2 * p + 1) * ROWS : (2 * p + 2) * ROWS],
                    ],
                    0,
                ).T
                for p in range(H // 2)
            ],
            1,
        )

    q = q_ref[0]
    do = do_ref[0]
    q_cols = heads_in_columns(q)
    do_cols = heads_in_columns(do)
    blank = jnp.zeros((wide, HD), BF)
    q_side = jnp.concatenate([heads_in_rows(q), blank], 1)
    do_side = jnp.concatenate([blank, heads_in_rows(do)], 1)
    out_acc[...] = jnp.zeros_like(out_acc)
    dq_acc[...] = jnp.zeros_like(dq_acc)
    lane = lax.broadcasted_iota(jnp.int32, (1, wide), 1)
    query_at = start + (lane & (ROWS - 1))

    def score_pass(masked):
        def one(j, top):
            rows = pl.ds(pl.multiple_of(j * KEYS, KEYS), KEYS)
            raw = jnp.dot(k_rows[rows, :], q_cols, preferred_element_type=F32)
            if masked:
                key_at = j * KEYS + lax.broadcasted_iota(jnp.int32, (KEYS, wide), 0)
                raw = jnp.where(key_at <= query_at, raw, -1e30)
            scores[j] = raw
            return jnp.maximum(top, jnp.max(raw.reshape(KEYS // 8, 8, wide), 0))

        return one

    top = jnp.full((8, wide), -1e30, F32)
    top = lax.fori_loop(0, open_chunks, score_pass(False), top)
    top = lax.fori_loop(open_chunks, all_chunks, score_pass(True), top)
    top = jnp.max(top, 0, keepdims=True)

    def value_pass(j, total):
        expo = jnp.exp(scores[j] - top)
        scores[j] = expo
        out_acc[...] += jnp.dot(v_cols[j], expo.astype(BF), preferred_element_type=F32)
        return total + jnp.sum(expo.reshape(KEYS // 8, 8, wide), 0)

    total = lax.fori_loop(0, all_chunks, value_pass, jnp.zeros((8, wide), F32))
    share = 1.0 / jnp.sum(total, 0, keepdims=True)
    out = out_acc[...] * share
    inner = jnp.sum(out * do_cols.astype(F32), 0, keepdims=True)

    def back_pass(j, carry):
        rows = pl.ds(pl.multiple_of(j * KEYS, KEYS), KEYS)
        grad_probs = jnp.dot(v_rows[rows, :], do_cols, preferred_element_type=F32)
        probs = scores[j] * share
        grad_scores = (probs * (grad_probs - inner)).astype(BF)
        dkv_acc[rows, :] += jnp.dot(
            grad_scores, q_side, preferred_element_type=F32
        ) + jnp.dot(probs.astype(BF), do_side, preferred_element_type=F32)
        dq_acc[...] += jnp.dot(k_cols[j], grad_scores, preferred_element_type=F32)
        return carry

    lax.fori_loop(0, all_chunks, back_pass, 0)
    o_ref[0] = heads_side_by_side(out).astype(BF)
    dq_ref[0] = (heads_side_by_side(dq_acc[...]) * HD ** (-0.5)).astype(BF)

    @pl.when(step == pl.num_programs(1) - 1)
    def _():
        dkv_ref[0] = dkv_acc[...].astype(BF)


def attention(place, q, do, kv, local):
    batch, rows, _ = q.shape
    keys = kv.shape[1]
    chunks = keys // KEYS
    wide = H * ROWS
    by_row = pl.BlockSpec((1, ROWS, D), lambda b, i, p: (b, i, 0))
    by_seq = pl.BlockSpec((1, keys, 2 * HD), lambda b, i, p: (b, 0, 0))
    return pl.pallas_call(
        functools.partial(attention_body, local=local),
        grid_spec=pltpu.PrefetchScalarGridSpec(
            num_scalar_prefetch=1,
            grid=(batch, rows // ROWS),
            in_specs=[by_row, by_row, by_seq],
            out_specs=[by_row, by_row, by_seq],
            scratch_shapes=[
                pltpu.VMEM((keys, HD), BF),
                pltpu.VMEM((keys, HD), BF),
                pltpu.VMEM((chunks, HD, KEYS), BF),
                pltpu.VMEM((chunks, HD, KEYS), BF),
                pltpu.VMEM((chunks, KEYS, wide), F32),
                pltpu.VMEM((HD, wide), F32),
                pltpu.VMEM((HD, wide), F32),
                pltpu.VMEM((keys, 2 * HD), F32),
            ],
        ),
        out_shape=[
            jax.ShapeDtypeStruct(q.shape, BF),
            jax.ShapeDtypeStruct(q.shape, BF),
            jax.ShapeDtypeStruct(kv.shape, BF),
        ],
        compiler_params=pltpu.CompilerParams(
            dimension_semantics=("arbitrary", "arbitrary"), vmem_limit_bytes=48 << 20
        ),
    )(place, q, do, kv)


def shift(x, by, count):
    return lax.ppermute(x, "seq", [(s, s + by) for s in range(count) if 0 <= s + by < count])


def shards(
    tokens,
    cotangent,
    tags,
    loss_weights,
    w_qkv,
    m_qkv,
    v_qkv,
    w_out,
    m_out,
    v_out,
    w_up,
    m_up,
    v_up,
    w_down,
    m_down,
    v_down,
    norm_params,
    m_norm,
    v_norm,
):
    seq_count = lax.axis_size("seq")
    seq_at = lax.axis_index("seq")
    seq_rows, local_len, width = tokens.shape
    count = seq_rows * local_len
    part = w_qkv.shape[0]

    small = jnp.concatenate(
        [w_qkv[:, D:], norm_params.T, jnp.zeros((part, 2 * HD - 4), F32)], 1
    ).astype(BF)
    small = lax.all_gather(small, "batch", axis=0, tiled=True)
    middle = jnp.concatenate([w_qkv[:, :D], w_out], 1).astype(BF)
    middle = lax.all_gather(middle, "batch", axis=0, tiled=True)
    full_up = lax.all_gather(w_up.astype(BF), "batch", axis=0, tiled=True)
    full_down = lax.all_gather(w_down.astype(BF), "batch", axis=0, tiled=True)
    full_kv = small[:, : 2 * HD]
    gains = small[:, 2 * HD : 2 * HD + 4].T.astype(F32)
    full_q = middle[:, :D]
    full_out = middle[:, D:]

    flat = tokens.astype(F32).reshape(count, width)
    normed_one, scale_one, first = layer_norm_parts(flat, gains[0], gains[1])
    first_low = first.astype(BF)
    _, _, second = layer_norm_parts(flat, gains[2], gains[3])
    second_low = second.astype(BF)

    cosine, sine = angles(seq_at * local_len, local_len)
    cos_tok = jnp.tile(cosine, (seq_rows, 1))
    sin_tok = jnp.tile(sine, (seq_rows, 1))

    mixed_kv = jnp.dot(first_low, full_kv, preferred_element_type=F32)
    key_rot = rotate(mixed_kv[:, :HD], cos_tok, sin_tok)
    pair = jnp.concatenate([key_rot, mixed_kv[:, HD:]], -1).astype(BF)
    pair = pair.reshape(seq_rows, local_len, 2 * HD)
    arrived = [pair] + [shift(pair, by, seq_count) for by in range(1, seq_count)]
    pairs = []
    for owner in range(seq_count):
        piece = jnp.zeros_like(pair)
        for by in range(seq_count):
            piece = jnp.where(seq_at - by == owner, arrived[by], piece)
        pairs.append(piece)
    keys = -(-seq_count * local_len // KEYS) * KEYS
    pairs.append(jnp.zeros((seq_rows, keys - seq_count * local_len, 2 * HD), BF))
    pairs = jnp.concatenate(pairs, 1)

    mixed_q = jnp.dot(first_low, full_q, preferred_element_type=F32)
    query = rotate(mixed_q.reshape(count, H, HD), cos_tok[:, None, :], sin_tok[:, None, :])
    query = query.reshape(seq_rows, local_len, D).astype(BF) * BF(HD ** (-0.5))
    subsets = jnp.arange(loss_weights.shape[0])
    row_weight = jnp.sum(
        jnp.where(tags[:, None] == subsets[None, :], loss_weights[None, :], 0.0), -1
    )
    grad_y = (cotangent.astype(F32) * row_weight[:, None, None]).reshape(count, D)
    grad_low = grad_y.astype(BF)
    grad_heads = (
        lax.dot_general(grad_low, full_out, COLS_LAST, preferred_element_type=F32)
        .astype(BF)
        .reshape(seq_rows, local_len, D)
    )
    rows = -(-local_len // ROWS) * ROWS
    pad = ((0, 0), (0, rows - local_len), (0, 0))
    heads, grad_query, grad_pairs = attention(
        jnp.reshape(seq_at, (1,)).astype(jnp.int32),
        jnp.pad(query, pad),
        jnp.pad(grad_heads, pad),
        pairs,
        local_len,
    )
    heads = heads[:, :local_len].reshape(count, D)
    grad_query = grad_query[:, :local_len].reshape(count, D)

    def piece_for(by):
        at = jnp.maximum(seq_at - by, 0) * local_len
        return lax.dynamic_slice_in_dim(grad_pairs, at, local_len, 1)

    grad_pair = piece_for(0).astype(F32)
    for by in range(1, seq_count):
        grad_pair = grad_pair + shift(piece_for(by), -by, seq_count).astype(F32)
    grad_pair = grad_pair.astype(BF).astype(F32).reshape(count, 2 * HD)

    up_pre = jnp.dot(second_low, full_up, preferred_element_type=F32)
    active, gelu_back = jax.vjp(lambda values: jax.nn.gelu(values, approximate=False), up_pre)
    active_low = active.astype(BF)
    attention_out = jnp.dot(heads, full_out, preferred_element_type=F32)
    feed = jnp.dot(active_low, full_down, preferred_element_type=F32)
    layer_out = (flat + attention_out + feed).astype(BF).reshape(seq_rows, local_len, D)
    grad_down = lax.dot_general(active_low, grad_low, ROWS_FIRST, preferred_element_type=F32)
    grad_active = lax.dot_general(grad_low, full_down, COLS_LAST, preferred_element_type=F32)
    grad_up_pre = gelu_back(grad_active)[0].astype(BF)
    grad_up = lax.dot_general(second_low, grad_up_pre, ROWS_FIRST, preferred_element_type=F32)
    grad_second = lax.dot_general(grad_up_pre, full_up, COLS_LAST, preferred_element_type=F32)

    grad_out_w = lax.dot_general(heads, grad_low, ROWS_FIRST, preferred_element_type=F32)
    grad_query = rotate(
        grad_query.astype(F32).reshape(count, H, HD),
        cos_tok[:, None, :],
        -sin_tok[:, None, :],
    )
    grad_key = rotate(grad_pair[:, :HD], cos_tok, -sin_tok)
    grad_mixed = jnp.concatenate(
        [grad_query.reshape(count, D), grad_key, grad_pair[:, HD:]], -1
    ).astype(BF)
    full_qkv = jnp.concatenate([full_q, full_kv], 1)
    grad_qkv = lax.dot_general(first_low, grad_mixed, ROWS_FIRST, preferred_element_type=F32)
    grad_first = lax.dot_general(grad_mixed, full_qkv, COLS_LAST, preferred_element_type=F32)
    normed_two, scale_two, _ = layer_norm_parts(flat, gains[2], gains[3])
    grad_input = (
        grad_y
        + norm_back(grad_first, normed_one, scale_one, gains[0])
        + norm_back(grad_second, normed_two, scale_two, gains[2])
    )
    input_grad = grad_input.astype(BF).reshape(seq_rows, local_len, D)
    grad_norm_params = jnp.stack(
        [
            jnp.sum(grad_first * normed_one, 0),
            jnp.sum(grad_first, 0),
            jnp.sum(grad_second * normed_two, 0),
            jnp.sum(grad_second, 0),
        ]
    )

    tail = jnp.concatenate(
        [grad_qkv, grad_out_w, grad_norm_params.T, jnp.zeros((D, 2 * HD - 4), F32)], 1
    )
    sums = [
        lax.psum_scatter(g, "batch", scatter_dimension=0, tiled=True)
        for g in (grad_down.astype(BF), grad_up.astype(BF), tail)
    ]
    sum_down, sum_up, tail = [lax.psum(g, "seq").astype(F32) for g in sums]
    qkv_width = w_qkv.shape[1]
    summed = (
        tail[:, :qkv_width],
        tail[:, qkv_width : qkv_width + D],
        sum_up,
        sum_down,
        tail[:, qkv_width + D : qkv_width + D + 4].T,
    )
    local_squares = jnp.float32(0.0)
    for grad in summed:
        local_squares = local_squares + jnp.sum(grad * grad)
    total_squares = lax.psum(local_squares, "batch")
    grad_norm = jnp.sqrt(total_squares)
    factor = CLIP_NORM / jnp.maximum(grad_norm, CLIP_NORM)
    masters = (w_qkv, w_out, w_up, w_down, norm_params)
    firsts = (m_qkv, m_out, m_up, m_down, m_norm)
    seconds = (v_qkv, v_out, v_up, v_down, v_norm)
    rates = (RATE_SMALL, RATE_LARGE, RATE_SMALL, RATE_SMALL, RATE_NORM)
    decays = (DECAY, DECAY, DECAY, DECAY, 0.0)
    results = []
    for index in range(5):
        results.extend(
            adam_update(
                masters[index],
                firsts[index],
                seconds[index],
                summed[index] * factor,
                rates[index],
                decays[index],
            )
        )
    return (layer_out, input_grad, grad_norm, *results)


def solution(mesh):
    in_specs = (
        P("batch", "seq", None),
        P("batch", "seq", None),
        P("batch"),
        P(),
        P("batch", None),
        P("batch", None),
        P("batch", None),
        P("batch", None),
        P("batch", None),
        P("batch", None),
        P("batch", None),
        P("batch", None),
        P("batch", None),
        P("batch", None),
        P("batch", None),
        P("batch", None),
        P(None, "batch"),
        P(None, "batch"),
        P(None, "batch"),
    )
    out_specs = (
        P("batch", "seq", None),
        P("batch", "seq", None),
        P(),
        P("batch", None),
        P("batch", None),
        P("batch", None),
        P("batch", None),
        P("batch", None),
        P("batch", None),
        P("batch", None),
        P("batch", None),
        P("batch", None),
        P("batch", None),
        P("batch", None),
        P("batch", None),
        P(None, "batch"),
        P(None, "batch"),
        P(None, "batch"),
    )
    return jax.shard_map(shards, mesh=mesh, in_specs=in_specs, out_specs=out_specs, check_vma=False)
```

time: 1060 us -> 598 us (0.56)
  matrix products: 261 us -> 101 us
  blocking collectives: 164 us -> 25.5 us
  local copies, waits for them, and re-layouts: 171 us -> 69 us
  other arithmetic: 128 us -> 51.1 us
  Pallas kernels: 0 us -> 28.6 us
    dot_general x37 -> x10, matrix products: 239 us -> 83.5 us  [the longest x1 33.5 us: shards(): lax.dot_general(grad_low, full_down, COLS_LAST, preferred_element_type=F32)]
    reduce_scatter x4 -> x2, waiting for transfers between devices: 126 us -> 0.04 us  [shards(): lax.psum_scatter(g, 'batch', scatter_dimension=0, tiled=True)]
    unnamed x1 -> x0, blocking collectives: 84.1 us -> none
    ppermute x0 -> x6, waiting for transfers between devices: none -> 82.1 us  [shift(): lax.ppermute(x, 'seq', [(s, s + by) for s in range(count) if 0 <= s + by...]
    dynamic_update_slice x4 -> x0, local copies, waits for them, and re-layouts: 49.2 us -> none  [shards(): lax.map(backward_row, (query_heads, pairs, grad_heads, log_totals))]
    convert_element_type x14 -> x9, other arithmetic: 67.1 us -> 20.3 us  [the longest x1 8.66 us: shards(): active_low = active.astype(BF)]
    all_gather x2 -> x1, blocking collectives: 53.6 us -> 11.2 us  [shards(): small = lax.all_gather(small, 'batch', axis=0, tiled=True)]
    while x20 -> x0, local copies, waits for them, and re-layouts: 39 us -> none  [the longest x2 17.2 us: shards(): lax.map(backward_row, (query_heads, pairs, grad_heads, log_totals))]
  transfers between devices with their start and end apart: 14 -> 14, of which waited for: 7 -> 7; matrix products, arithmetic and copies ran while one was open for 49% -> 29% of each run, Pallas kernels for 0% -> 5%
where the time goes in v1:
time: 598 us; the launch traced here: 587 us
  waiting for transfers between devices  277 us (46%)
  matrix products  101 us (17%)
  local copies, waits for them, and re-layouts  69 us (12%)
  other arithmetic  51.1 us (9%)
  Pallas kernels  28.6 us (5%)
  blocking collectives  25.5 us (4%)
  between operations  20.7 us (3%)
  starting transfers between devices  14.6 us (2%)
    psum x2, waiting for transfers between devices, shards(): sum_down, sum_up, tail = [lax.psum(g, 'seq').astype(F32) for g in sums]  97.8 us
    ppermute x6, waiting for transfers between devices, shift(): lax.ppermute(x, 'seq', [(s, s + by) for s in range(count) if 0 <= s + by...  82.1 us
    unnamed x9, waiting for transfers between devices  44.8 us
    dot_general x1, matrix products, shards(): lax.dot_general(grad_low, full_down, COLS_LAST, preferred_element_type=F32)  33.5 us
    unnamed x151, local copies, waits for them, and re-layouts  33.3 us
    all_gather x1, waiting for transfers between devices, shards(): full_down = lax.all_gather(w_down.astype(BF), 'batch', axis=0, tiled=True)  31.8 us
    pallas_call x1, Pallas kernels, attention(): pl.pallas_call(functools.partial(attention_body, local=local), grid_spec=...  28.6 us
    all_gather x1, waiting for transfers between devices, shards(): full_up = lax.all_gather(w_up.astype(BF), 'batch', axis=0, tiled=True)  20 us
  transfers between devices with their start and end apart: 14, of which 7 were waited for; matrix products, arithmetic and copies ran while one was open for 29% of the time, Pallas kernels for 5%

profile of v1, /device:TPU:0, one launch (start us, length us, event | category | flops | bytes accessed | tf_op | source)
XLA Modules:
  0.0 586.8 jit_solution(1509120598030632035)
XLA Ops:
  13.3 11.2 %all_gather.12 = bf16[768,256]{1,0:T(8,128)(2,1)S(1)} all-gather(bf16[96,256]{1,0:T(8,128)(2,1)S(1)} %maximum_maximum_fusion), channel_id=1, replica_groups=mesh['batch'=8,'seq'=4] {'batch'}, dimensions={0}, use_global_device_ids=true | all-gather | bytes 442368 | tf_op jit(solution)/shard_map/all_gather | solution.py:270
  32.2 20.0 %all-gather.6.cloned.1.call-done = bf16[768,3072]{1,0:T(8,128)(2,1)} async-done(((bf16[96,3072]{1,0:T(8,128)(2,1)}), bf16[768,3072]{1,0:T(8,128)(2,1)}) %all-gather.6.cloned.1.call-update) | async-done | bytes 4718608 | tf_op jit(solution)/shard_map/all_gather | solution.py:273
  52.2 9.6 %fusion.63 = f32[912,3072]{1,0:T(8,128)} fusion(bf16[912,768]{1,0:T(8,128)(2,1)S(1)} %get-tuple-element.176, bf16[768,3072]{1,0:T(8,128)(2,1)} %all-gather.6.cloned.1.call-done), kind=kOutput, calls=%fused_computation.157 | convolution fusion | flops 4303355904 | bytes 17326080 | tf_op jit(solution)/shard_map/dot_general | solution.py:340
  61.9 31.8 %all-gather.8.cloned.1.call-done = bf16[3072,768]{1,0:T(8,128)(2,1)} async-done(((bf16[384,768]{1,0:T(8,128)(2,1)}), bf16[3072,768]{1,0:T(8,128)(2,1)}) %all-gather.8.cloned.1.call-update) | async-done | bytes 4718608 | tf_op jit(solution)/shard_map/all_gather | solution.py:274
  93.6 33.5 %add_convert_fusion = (bf16[912,3072]{1,0:T(8,128)(2,1)S(1)}, f32[912,3072]{1,0:T(8,128)}) fusion(f32[912,3072]{1,0:T(8,128)} %fusion.63, bf16[912,768]{1,0:T(8,128)(2,1)S(1)} %copy-done.32, bf16[3072,768]{1,0:T(8,128)(2,1)} %all-gather.8.cloned.1.call-done), kind=kOutput, calls=%fused_computation.2 | convolution fusion | flops 4505075712 | bytes 34136064 | tf_op jit(solution)/shard_map/dot_general | solution.py:347
  129.6 6.8 %convolution_convert_fusion.1 = bf16[768,3072]{1,0:T(8,128)(2,1)} fusion(bf16[912,768]{1,0:T(8,128)(2,1)S(1)} %copy-done.29, bf16[912,3072]{1,0:T(8,128)(2,1)S(1)} %get-tuple-element.169), kind=kOutput, calls=%fused_computation.18 | convolution fusion | flops 4305715200 | bytes 11722752 | tf_op jit(solution)/shard_map/dot_general | solution.py:349
  139.8 5.3 collective-permute-start
  146.4 3.5 collective-permute-start.2
  160.8 8.7 %multiply_convert_fusion = bf16[912,3072]{1,0:T(8,128)(2,1)S(1)} fusion(f32[912,3072]{1,0:T(8,128)} %get-tuple-element.170, f32[912,3072]{1,0:T(8,128)} %fusion.63), kind=kLoop, calls=%fused_computation.3 | loop fusion | flops 8404992 | bytes 28016640 | tf_op jit(solution)/shard_map/convert_element_type | solution.py:342
  171.9 6.9 %convolution_convert_fusion = bf16[3072,768]{1,0:T(8,128)(2,1)} fusion(bf16[912,3072]{1,0:T(8,128)(2,1)S(1)} %multiply_convert_fusion, bf16[912,768]{1,0:T(8,128)(2,1)S(1)} %copy-done.33), kind=kOutput, calls=%fused_computation.17 | convolution fusion | flops 4305715200 | bytes 11722752 | tf_op jit(solution)/shard_map/dot_general | solution.py:346
  191.6 3.7 copy.172
  201.0 28.6 %shard_map.322 = (bf16[2,512,768]{2,1,0:T(8,128)(2,1)S(1)}, bf16[2,512,768]{2,1,0:T(8,128)(2,1)S(1)}, bf16[2,2048,128]{2,1,0:T(8,128)(2,1)S(1)}) custom-call(s32[1]{0:T(128)} %bitcast.1.place, bf16[2,512,768]{2,1,0:T(8,128)(2,1)} %pad.7.q_ref, bf16[2,512,768]{2,1,0:T(8,128)(2,1)} %pad.8.do_ref, ...), custom_call_target="tpu_custom_call" | custom-call | tf_op jit(solution)/shard_map/pallas_call | solution.py:207
  246.8 79.4 %collective-permute-done.5 = bf16[2,456,128]{2,1,0:T(8,128)(2,1)S(1)} collective-permute-done((bf16[2,456,128]{2,1,0:T(8,128)(2,1)S(1)}, bf16[2,456,128]{2,1,0:T(8,128)(2,1)S(1)}, u32[]{:S(2)}, u32[]{:S(2)}) %collective-permute-start.5) | collective-permute-done | bytes 233504 | tf_op jit(solution)/shard_map/ppermute | solution.py:237
  329.6 3.8 fusion.20
  337.5 12.0 %multiply_reduce_fusion = (f32[768]{0:T(1024)S(1)}, f32[768]{0:T(1024)S(1)}, f32[912]{0:T(1024)}, f32[912]{0:T(1024)}, f32[912]{0:T(1024)S(1)}, /*index=5*/f32[9...) fusion(bf16[2,456,768]{2,1,0:T(8,128)(2,1)S(1)} %copy-done.4, f32[912]{0:T(1024)S(1)} %copy-done.57, ...), kind=kOutput, calls=%fused_computation.36 | convolution fusion | flops 4315254784 | bytes 20168064 | tf_op jit(solution)/shard_map/dot_general | solution.py:350
  349.7 6.3 %concatenate.78 = f32[768,1792]{1,0:T(8,128)} concatenate(f32[768,896]{1,0:T(8,128)} %fusion.36, f32[768,768]{1,0:T(8,128)} %convolution_bitcast_fusion, f32[768,4]{1,0:T(8,128)S(1)} %bitcast.90, f32[768,124]{1,0:T(8,128)S(1)} %broadcast_in_dim.22), dimensions={1} | concatenate | bytes 11010048 | tf_op jit(solution)/shard_map/concatenate | solution.py:381
  365.4 10.6 %fusion.64 = f32[912,768]{1,0:T(8,128)} fusion(bf16[912,3072]{1,0:T(8,128)(2,1)} %copy-done.7, bf16[3072,768]{1,0:T(8,128)(2,1)} %all-gather.8.cloned.1.call-done), kind=kOutput, calls=%fused_computation.158 | convolution fusion | flops 4303355904 | bytes 13123584 | tf_op jit(solution)/shard_map/dot_general | solution.py:344
  376.0 44.7 %reduce-scatter.10.cloned.1.call-done = f32[96,1792]{1,0:T(8,128)} async-done(((f32[768,1792]{1,0:T(8,128)}), f32[96,1792]{1,0:T(8,128)}) %reduce-scatter.10.cloned.1.call-update) | async-done | bytes 688144
  423.1 5.1 fusion.7
  428.2 51.4 %all-reduce.8.cloned.1.call-done = (bf16[96,3072]{1,0:T(8,128)(2,1)}, bf16[384,768]{1,0:T(8,128)(2,1)}) async-done(((bf16[96,3072]{1,0:T(8,128)(2,1)}, bf16[384,768]{1,0:T(8,128)(2,1)}), (bf16[96,3072]{1,0:T(8,128)(2,1)}, bf16[384,768]{1,0:T(8,128)(2,1)})) %all-reduce.8.cloned.1.call-update) | async-done | bytes 1179664 | tf_op jit(solution)/shard_map/psum | solution.py:388
  483.5 46.5 %all-reduce.6.cloned.1.call-done = f32[96,1792]{0,1:T(8,128)} async-done(((f32[96,1792]{0,1:T(8,128)}), f32[96,1792]{0,1:T(8,128)}) %all-reduce.6.cloned.1.call-update) | async-done | bytes 688144 | tf_op jit(solution)/shard_map/psum | solution.py:388
  538.0 5.0 fusion.16
  543.0 14.3 %psum.31 = f32[]{:T(128)} all-reduce(f32[]{:T(128)S(6)} %add.229), channel_id=1, replica_groups=mesh['batch'=8,'seq'=4] {'batch'}, use_global_device_ids=true, to_apply=%region_22.23 | all-reduce | flops 1 | bytes 8 | tf_op jit(solution)/shard_map/psum | solution.py:400
  571.1 4.2 multiply_subtract_fusion.1
  (276 shorter events, 113.4 us)
Async XLA Ops:
  7.2 45.0 %all-gather.6.cloned.1.call-start = ((), (), s32[]{:S(2)}) async-start(), calls=%async_computation.4 | async-start | bytes 5308416 | tf_op jit(solution)/shard_map/all_gather | solution.py:273
  9.6 84.1 %all-gather.8.cloned.1.call-start = ((), (), s32[]{:S(2)}) async-start(), calls=%async_computation.5 | async-start | bytes 5308416 | tf_op jit(solution)/shard_map/all_gather | solution.py:274
  10.5 169.8 %all-gather.4.cloned.1.call-start = ((), (), s32[]{:S(2)}) async-start(), calls=%async_computation.3 | async-start | bytes 2654208 | tf_op jit(solution)/shard_map/all_gather | solution.py:272
  11.5 353.9 %reduce-scatter.6.cloned.1.call-start = ((), (), s32[]{:S(2)}) async-start(), calls=%async_computation.7 | async-start | bytes 5308416 | tf_op jit(solution)/shard_map/reduce_scatter | solution.py:385
  12.5 16.9 %copy-start.54 = (f32[912]{0:T(1024)}, f32[912]{0:T(1024)S(1)}, u32[]{:S(2)}) copy-start(f32[912]{0:T(1024)S(1)} %div.108) | copy-start | bytes 10948
  13.1 16.2 %copy-start.56 = (f32[912]{0:T(1024)}, f32[912]{0:T(1024)S(1)}, u32[]{:S(2)}) copy-start(f32[912]{0:T(1024)S(1)} %rsqrt.15) | copy-start | bytes 10948
  32.2 29.7 %copy-start.28 = (bf16[912,768]{1,0:T(8,128)(2,1)}, bf16[912,768]{1,0:T(8,128)(2,1)S(1)}, u32[]{:S(2)}) copy-start(bf16[912,768]{1,0:T(8,128)(2,1)S(1)} %get-tuple-element.176) | copy-start | bytes 4202500
  52.2 41.4 %copy-start.32 = (bf16[912,768]{1,0:T(8,128)(2,1)S(1)}, bf16[912,768]{1,0:T(8,128)(2,1)}, u32[]{:S(2)}) copy-start(bf16[912,768]{1,0:T(8,128)(2,1)} %bitcast_convert_fusion) | copy-start | bytes 4202500
  93.6 35.9 %copy-start.29 = (bf16[912,768]{1,0:T(8,128)(2,1)S(1)}, bf16[912,768]{1,0:T(8,128)(2,1)}, u32[]{:S(2)}) copy-start(bf16[912,768]{1,0:T(8,128)(2,1)} %copy-done.28) | copy-start | bytes 4202500
  136.4 228.9 %reduce-scatter.8.cloned.1.call-start = ((), (), s32[]{:S(2)}) async-start(), calls=%async_computation.8 | async-start | bytes 5308416 | tf_op jit(solution)/shard_map/reduce_scatter | solution.py:385
  138.7 16.1 %copy-start.3 = (bf16[2,456,768]{2,1,0:T(8,128)(2,1)S(1)}, bf16[2,456,768]{2,1,0:T(8,128)(2,1)}, u32[]{:S(2)}) copy-start(bf16[2,456,768]{2,1,0:T(8,128)(2,1)} %param.19) | copy-start | bytes 4202500
  138.7 16.0 %copy-start.45 = (f32[2,456]{1,0:T(2,128)S(1)}, f32[2,456]{1,0:T(2,128)}, u32[]{:S(2)}) copy-start(f32[2,456]{1,0:T(2,128)} %copy-done.44) | copy-start | bytes 10948
  139.8 16.6 %collective-permute-start = (bf16[2,456,128]{2,1,0:T(8,128)(2,1)S(1)}, bf16[2,456,128]{2,1,0:T(8,128)(2,1)S(1)}, u32[]{:S(2)}, u32[]{:S(2)}) collective-permute-start(bf16[2,456,128]{2,1,0:T(8,128)(2,1)S(1)} %pad_maximum_fusion.5), channel_id=1, source_target_pairs={{0,3},{4,7},{8,11},{12,15},{16,19},{20,23},{24,27},{28,31}} | collective-permute-start | bytes 700424 | tf_op jit(solution)/shard_map/ppermute | solution.py:237
  145.1 11.4 %collective-permute-start.1 = (bf16[2,456,128]{2,1,0:T(8,128)(2,1)S(1)}, bf16[2,456,128]{2,1,0:T(8,128)(2,1)S(1)}, u32[]{:S(2)}, u32[]{:S(2)}) collective-permute-start(bf16[2,456,128]{2,1,0:T(8,128)(2,1)S(1)} %pad_maximum_fusion.5), channel_id=1, source_target_pairs={{0,2},{1,3},{4,6},{5,7},{8,10},{9,11},{12,14},{13,15},{16,18},{17,... | collective-permute-start | bytes 700424 | tf_op jit(solution)/shard_map/ppermute | solution.py:237
  146.4 14.1 %collective-permute-start.2 = (bf16[2,456,128]{2,1,0:T(8,128)(2,1)S(1)}, bf16[2,456,128]{2,1,0:T(8,128)(2,1)}, u32[]{:S(2)}, u32[]{:S(2)}) collective-permute-start(bf16[2,456,128]{2,1,0:T(8,128)(2,1)S(1)} %pad_maximum_fusion.5), channel_id=1, source_target_pairs={{0,1},{1,2},{2,3},{4,5},{5,6},{6,7},{8,9},{9,10},{10,11},{12,13},{... | collective-permute-start | bytes 700424 | tf_op jit(solution)/shard_map/ppermute | solution.py:237
  178.9 241.9 %reduce-scatter.10.cloned.1.call-start = ((), (), s32[]{:S(2)}) async-start(), calls=%async_computation.9 | async-start | bytes 6193152
  238.1 88.1 %collective-permute-start.5 = (bf16[2,456,128]{2,1,0:T(8,128)(2,1)S(1)}, bf16[2,456,128]{2,1,0:T(8,128)(2,1)S(1)}, u32[]{:S(2)}, u32[]{:S(2)}) collective-permute-start(bf16[2,456,128]{2,1,0:T(8,128)(2,1)S(1)} %get-tuple-element.179), channel_id=1, source_target_pairs={{3,0},{7,4},{11,8},{15,12},{19,16},{23,20},{27,24},{31,28}} | collective-permute-start | bytes 700424 | tf_op jit(solution)/shard_map/ppermute | solution.py:237
  239.4 86.8 %collective-permute-start.4 = (bf16[2,456,128]{2,1,0:T(8,128)(2,1)S(1)}, bf16[2,456,128]{2,1,0:T(8,128)(2,1)S(1)}, u32[]{:S(2)}, u32[]{:S(2)}) collective-permute-start(bf16[2,456,128]{2,1,0:T(8,128)(2,1)S(1)} %get-tuple-element.180), channel_id=1, source_target_pairs={{2,0},{3,1},{6,4},{7,5},{10,8},{11,9},{14,12},{15,13},{18,16},{19,... | collective-permute-start | bytes 700424 | tf_op jit(solution)/shard_map/ppermute | solution.py:237
  240.7 85.5 %collective-permute-start.3 = (bf16[2,456,128]{2,1,0:T(8,128)(2,1)S(1)}, bf16[2,456,128]{2,1,0:T(8,128)(2,1)S(1)}, u32[]{:S(2)}, u32[]{:S(2)}) collective-permute-start(bf16[2,456,128]{2,1,0:T(8,128)(2,1)S(1)} %get-tuple-element.178), channel_id=1, source_target_pairs={{1,0},{2,1},{3,2},{5,4},{6,5},{7,6},{9,8},{10,9},{11,10},{13,12},{... | collective-permute-start | bytes 700424 | tf_op jit(solution)/shard_map/ppermute | solution.py:237
  246.8 80.7 %copy-start.14 = (f32[456,16]{1,0:T(8,128)S(1)}, f32[456,16]{1,0:T(8,128)}, u32[]{:S(2)}) copy-start(f32[456,16]{1,0:T(8,128)} %copy-done.13) | copy-start | bytes 87556
  356.1 123.5 %all-reduce.8.cloned.1.call-start = ((), (), s32[]{:S(2)}) async-start(), calls=%async_computation.10 | async-start | bytes 2359296 | tf_op jit(solution)/shard_map/psum | solution.py:388
  365.4 164.6 %all-reduce.6.cloned.1.call-start = ((), (), s32[]{:S(2)}) async-start(), calls=%async_computation.6 | async-start | bytes 1835008 | tf_op jit(solution)/shard_map/psum | solution.py:388
  376.0 47.1 %copy-start.5 = (bf16[2,456,768]{2,1,0:T(8,128)(2,1)S(1)}, bf16[2,456,768]{2,1,0:T(8,128)(2,1)}, u32[]{:S(2)}) copy-start(bf16[2,456,768]{2,1,0:T(8,128)(2,1)} %param.19) | copy-start | bytes 4202500
  538.0 20.0 %copy-start.19 = (f32[96,1792]{0,1:T(8,128)S(1)}, f32[96,1792]{0,1:T(8,128)}, u32[]{:S(2)}) copy-start(f32[96,1792]{0,1:T(8,128)} %all-reduce.6.cloned.1.call-done) | copy-start | bytes 2064388
  (60 other events, 282.1 us)
Sparse Core Ops, SparseCore 0:
  10.5 41.6 all-gather.5
  54.7 38.9 all-gather.7
  96.1 29.0 all-gather.3
  136.5 53.8 reduce-scatter.5
  194.2 53.8 reduce-scatter.7
  356.2 64.5 reduce-scatter.9
  423.3 56.2 all-reduce.7
  482.7 47.2 all-reduce.5

commit v2 on v1

v2 whole, which is shorter than its diff:
```python
import functools
import math

import jax
import jax.numpy as jnp
from jax import lax
from jax.experimental import pallas as pl
from jax.experimental.pallas import tpu as pltpu
from jax.sharding import PartitionSpec as P

D = 768
H = 12
HD = 64
ROT = 16
STEP = 10


EPS_NORM = 1e-05
BETA_ONE = 0.9
BETA_TWO = 0.999
ADAM_EPS = 1e-08
CLIP_NORM = 1.0
RATE_SMALL = 0.02
RATE_LARGE = 0.2
RATE_NORM = 1.0
DECAY = 0.1
ROWS_FIRST = (((0,), (0,)), ((), ()))
COLS_LAST = (((1,), (1,)), ((), ()))


def angles(first, count):
    place = (first + jnp.arange(count)).astype(jnp.float32)
    inverse = 10000.0 ** (-jnp.arange(0, ROT, 2).astype(jnp.float32) / ROT)
    turn = place[:, None] * inverse[None, :]
    turn = jnp.concatenate([turn, turn], -1)
    return (jnp.cos(turn), jnp.sin(turn))


def adam_update(weight, first, second, grad, rate, decay):
    first_new = BETA_ONE * first + (1.0 - BETA_ONE) * grad
    second_new = BETA_TWO * second + (1.0 - BETA_TWO) * grad * grad
    step_one = first_new / (1.0 - BETA_ONE**STEP)
    step_two = second_new / (1.0 - BETA_TWO**STEP)
    weight_new = weight - rate * (step_one / (jnp.sqrt(step_two) + ADAM_EPS) + decay * weight)
    return (weight_new, first_new, second_new)


BF = jnp.bfloat16
F32 = jnp.float32
ROWS = 128
KEYS = 384
VMEM_BYTES = 60 << 20


def attention_body(
    place,
    q_ref,
    do_ref,
    *refs,
    local,
    devices,
):
    kv_refs, refs = refs[:devices], refs[-10 - devices :]
    o_ref, dq_ref, dkv_refs = refs[0], refs[1], refs[2 : 2 + devices]
    k_rows, v_rows, k_cols, v_cols, scores, out_acc, dq_acc, dkv_acc = refs[-8:]
    step = pl.program_id(0)
    chunks = scores.shape[0]
    wide = H * ROWS

    @pl.when(step == 0)
    def _():
        dkv_acc[...] = jnp.zeros_like(dkv_acc)
        for by, kv_ref in enumerate(kv_refs):

            @pl.when(place[0] >= by)
            def _(by=by, kv_ref=kv_ref):
                rows = pl.ds(pl.multiple_of((place[0] - by) * local, 8), local)
                dkv_acc[rows, :] = kv_ref[...].astype(F32)

        def prepare(j, carry):
            rows = pl.ds(pl.multiple_of(j * KEYS, KEYS), KEYS)
            pair = dkv_acc[rows, :].astype(BF)
            k_rows[rows, :] = pair[:, :HD]
            v_rows[rows, :] = pair[:, HD:]
            turned = pair.T
            k_cols[j] = turned[:HD]
            v_cols[j] = turned[HD:]
            dkv_acc[rows, :] = jnp.zeros((KEYS, 2 * HD), F32)
            return carry

        lax.fori_loop(0, chunks, prepare, 0)

    start = place[0] * local + step * ROWS
    last = jnp.minimum(start + ROWS - 1, (place[0] + 1) * local - 1)
    open_chunks = (start + 1) // KEYS
    all_chunks = last // KEYS + 1

    def heads_in_columns(x):
        turned = [x[:, 2 * HD * p : 2 * HD * (p + 1)].T for p in range(H // 2)]
        return jnp.concatenate([t[a : a + HD] for t in turned for a in (0, HD)], 1)

    def heads_in_rows(x):
        return jnp.concatenate([x[:, HD * h : HD * (h + 1)] for h in range(H)], 0)

    def heads_side_by_side(t):
        return jnp.concatenate(
            [
                jnp.concatenate(
                    [
                        t[:, 2 * p * ROWS : (2 * p + 1) * ROWS],
                        t[:, (2 * p + 1) * ROWS : (2 * p + 2) * ROWS],
                    ],
                    0,
                ).T
                for p in range(H // 2)
            ],
            1,
        )

    real = lax.broadcasted_iota(jnp.int32, (ROWS, D), 0) < local - step * ROWS
    q = jnp.where(real, q_ref[0], 0.0).astype(BF)
    do = jnp.where(real, do_ref[0], 0.0).astype(BF)
    q_cols = heads_in_columns(q)
    do_cols = heads_in_columns(do)
    blank = jnp.zeros((wide, HD), BF)
    q_side = jnp.concatenate([heads_in_rows(q), blank], 1)
    do_side = jnp.concatenate([blank, heads_in_rows(do)], 1)
    out_acc[...] = jnp.zeros_like(out_acc)
    dq_acc[...] = jnp.zeros_like(dq_acc)
    lane = lax.broadcasted_iota(jnp.int32, (1, wide), 1)
    query_at = start + (lane & (ROWS - 1))

    open_pairs, all_pairs, odd = open_chunks // 2, all_chunks // 2, all_chunks % 2

    def key_rows(j, count):
        return pl.ds(pl.multiple_of(j * KEYS, KEYS), count * KEYS)

    def columns(ref, j, count):
        return jnp.concatenate([ref[j + c] for c in range(count)], 1)

    def score_step(j, top, count, masked):
        raw = jnp.dot(k_rows[key_rows(j, count), :], q_cols, preferred_element_type=F32)
        if masked:
            key_at = j * KEYS + lax.broadcasted_iota(jnp.int32, (count * KEYS, wide), 0)
            raw = jnp.where(key_at <= query_at, raw, -1e30)
        scores[pl.ds(j, count)] = raw.reshape(count, KEYS, wide)
        return jnp.maximum(top, jnp.max(raw.reshape(count * KEYS // 8, 8, wide), 0))

    def value_step(j, total, count):
        expo = jnp.exp(scores[pl.ds(j, count)].reshape(count * KEYS, wide) - top)
        scores[pl.ds(j, count)] = expo.reshape(count, KEYS, wide)
        out_acc[...] += jnp.dot(
            columns(v_cols, j, count), expo.astype(BF), preferred_element_type=F32
        )
        return total + jnp.sum(expo.reshape(count * KEYS // 8, 8, wide), 0)

    def back_step(j, count):
        rows = key_rows(j, count)
        grad_probs = jnp.dot(v_rows[rows, :], do_cols, preferred_element_type=F32)
        probs = scores[pl.ds(j, count)].reshape(count * KEYS, wide) * share
        grad_scores = (probs * (grad_probs - inner)).astype(BF)
        dkv_acc[rows, :] += jnp.dot(
            grad_scores, q_side, preferred_element_type=F32
        ) + jnp.dot(probs.astype(BF), do_side, preferred_element_type=F32)
        dq_acc[...] += jnp.dot(
            columns(k_cols, j, count), grad_scores, preferred_element_type=F32
        )

    top = jnp.full((8, wide), -1e30, F32)
    top = lax.fori_loop(0, open_pairs, lambda p, t: score_step(2 * p, t, 2, False), top)
    top = lax.fori_loop(open_pairs, all_pairs, lambda p, t: score_step(2 * p, t, 2, True), top)
    top = lax.fori_loop(0, odd, lambda p, t: score_step(2 * all_pairs, t, 1, True), top)
    top = jnp.max(top, 0, keepdims=True)

    total = jnp.zeros((8, wide), F32)
    total = lax.fori_loop(0, all_pairs, lambda p, t: value_step(2 * p, t, 2), total)
    total = lax.fori_loop(0, odd, lambda p, t: value_step(2 * all_pairs, t, 1), total)
    share = 1.0 / jnp.sum(total, 0, keepdims=True)
    out = out_acc[...] * share
    inner = jnp.sum(out * do_cols.astype(F32), 0, keepdims=True)

    def back_pair(p, carry):
        back_step(2 * p, 2)
        return carry

    lax.fori_loop(0, all_pairs, back_pair, 0)

    @pl.when(odd != 0)
    def _():
        back_step(2 * all_pairs, 1)

    o_ref[0] = heads_side_by_side(out).astype(BF)
    dq_ref[0] = (heads_side_by_side(dq_acc[...]) * HD ** (-0.5)).astype(BF)

    @pl.when(step == pl.num_programs(0) - 1)
    def _():
        for by, dkv_ref in enumerate(dkv_refs):
            owner = jnp.maximum(place[0] - by, 0)
            rows = pl.ds(pl.multiple_of(owner * local, 8), local)
            dkv_ref[...] = dkv_acc[rows, :].astype(BF)


def attention(place, q, do, kv, at, earlier=()):
    local = q.shape[1]
    devices = len(kv)
    keys = devices * local
    chunks = -(-keys // KEYS)
    steps = -(-local // ROWS)
    wide = H * ROWS
    by_row = pl.BlockSpec((1, ROWS, D), lambda i, p: (at, i, 0))
    pairs = pl.BlockSpec((local, 2 * HD), lambda i, p: (0, 0))
    return pl.pallas_call(
        functools.partial(attention_body, local=local, devices=devices),
        grid_spec=pltpu.PrefetchScalarGridSpec(
            num_scalar_prefetch=1,
            grid=(steps,),
            in_specs=[by_row] * 2
            + [pairs] * devices
            + [pl.BlockSpec(memory_space=pl.ANY)] * len(earlier),
            out_specs=[by_row] * 2 + [pairs] * devices,
            scratch_shapes=[
                pltpu.VMEM((chunks * KEYS, HD), BF),
                pltpu.VMEM((chunks * KEYS, HD), BF),
                pltpu.VMEM((chunks, HD, KEYS), BF),
                pltpu.VMEM((chunks, HD, KEYS), BF),
                pltpu.VMEM((chunks, KEYS, wide), F32),
                pltpu.VMEM((HD, wide), F32),
                pltpu.VMEM((HD, wide), F32),
                pltpu.VMEM((chunks * KEYS, 2 * HD), F32),
            ],
        ),
        out_shape=[jax.ShapeDtypeStruct(q.shape, BF)] * 2
        + [jax.ShapeDtypeStruct((local, 2 * HD), BF)] * devices,
        input_output_aliases={3 + devices: 0, 4 + devices: 1} if earlier else {},
        compiler_params=pltpu.CompilerParams(
            dimension_semantics=("arbitrary",), vmem_limit_bytes=VMEM_BYTES
        ),
        cost_estimate=pl.CostEstimate(
            flops=12 * local * D * keys,
            transcendentals=local * H * keys,
            bytes_accessed=8 * local * D,
        ),
    )(place, q, do, *kv, *earlier)


def feed_body(*refs, block, direct):
    h_ref, dy_ref, up_ref, down_ref, f_ref, da_ref = refs[:6]
    goal_down, goal_up = (refs[6], refs[6]) if direct else refs[6:8]
    h_cols, made_down, made_up, sem = refs[-4:]
    step, last = pl.program_id(0), pl.num_programs(0) - 1
    slot = step % 2
    width = h_ref.shape[1]

    def copies(c, at):
        if direct:
            owners, rows = made_down.shape[1], made_down.shape[2]
            part = made_up.shape[2]
            there = (
                goal_down.at[pl.ds(c * owners, owners), pl.ds(0, rows), :],
                goal_up.at[:, pl.ds(pl.multiple_of(rows + c * part, part), part), :],
            )
        else:
            span = pl.ds(pl.multiple_of(c * width, width), width)
            there = (goal_down.at[span, :], goal_up.at[:, span])
        return [
            pltpu.make_async_copy(made_down.at[at], there[0], sem.at[0, at]),
            pltpu.make_async_copy(made_up.at[at], there[1], sem.at[1, at]),
        ]

    @pl.when(step == 0)
    def _():
        h_cols[...] = h_ref[...].T

    up = up_ref[...].reshape(width, width)
    down = down_ref[...].reshape(width, width)
    for r in range(0, h_ref.shape[0], block):
        rows = pl.ds(r, block)
        pre = jnp.dot(h_ref[rows, :], up, preferred_element_type=F32)
        grad = lax.dot_general(dy_ref[rows, :], down, COLS_LAST, preferred_element_type=F32)
        below = 0.5 + 0.5 * lax.erf(pre * 0.5**0.5)
        bell = jnp.exp(pre * pre * -0.5) * (2.0 * math.pi) ** -0.5
        f_ref[rows, :] = (pre * below).astype(BF)
        da_ref[rows, :] = (grad * (below + pre * bell)).astype(BF)

    @pl.when(step >= 2)
    def _():
        for copy in copies(step - 2, slot):
            copy.wait()

    grad = lax.dot_general(f_ref[...], dy_ref[...], ROWS_FIRST, preferred_element_type=F32)
    made_down[slot] = grad.astype(BF).reshape(made_down.shape[1:])
    grad = jnp.dot(h_cols[...], da_ref[...], preferred_element_type=F32)
    made_up[slot] = grad.astype(BF).reshape(made_up.shape[1:])
    for copy in copies(step, slot):
        copy.start()

    @pl.when(step == last)
    def _():
        for copy in copies(step - 1, 1 - slot) + copies(step, slot):
            copy.wait()


def feed_weights(packed):
    owners, eight, width = packed.shape
    part = eight // 8
    if part % 16 == 0:
        return (packed, packed), (
            pl.BlockSpec((owners, part, width), lambda c: (0, 4 + c, 0)),
            pl.BlockSpec((owners // 4, 4 * part, width), lambda c: (c, 0, 0)),
        )
    down = packed[:, : 4 * part].reshape(4 * width, width)
    up = packed[:, 4 * part :].reshape(owners, 4, part, width)
    up = up.transpose(0, 2, 1, 3).reshape(width, 4 * width)
    return (up, down), (
        pl.BlockSpec((width, width), lambda c: (0, c)),
        pl.BlockSpec((width, width), lambda c: (c, 0)),
    )


def feed_forward(h, dy, weights, specs, owners):
    count, width = h.shape
    part = width // owners
    hidden = 4 * width
    direct = part % 16 == 0
    whole = pl.BlockSpec((count, width), lambda c: (0, 0))
    column = pl.BlockSpec((count, width), lambda c: (0, c))
    anywhere = pl.BlockSpec(memory_space=pl.ANY)
    if direct:
        made = [(owners // 4, 4 * part, width), (owners, part, width)]
        goals = [jax.ShapeDtypeStruct((owners, 8 * part, width), BF)]
    else:
        made = [(width, width)] * 2
        goals = [
            jax.ShapeDtypeStruct((hidden, width), BF),
            jax.ShapeDtypeStruct((width, hidden), BF),
        ]
    f, da, *grads = pl.pallas_call(
        functools.partial(feed_body, block=count // 3, direct=direct),
        grid=(4,),
        in_specs=[whole, whole, *specs],
        out_specs=[column, column] + [anywhere] * len(goals),
        out_shape=[jax.ShapeDtypeStruct((count, hidden), BF)] * 2 + goals,
        scratch_shapes=[pltpu.VMEM((width, count), BF)]
        + [pltpu.VMEM((2, *shape), BF) for shape in made]
        + [pltpu.SemaphoreType.DMA((2, 2))],
        compiler_params=pltpu.CompilerParams(
            dimension_semantics=("arbitrary",), vmem_limit_bytes=VMEM_BYTES
        ),
        cost_estimate=pl.CostEstimate(
            flops=8 * count * width * hidden,
            transcendentals=2 * count * hidden,
            bytes_accessed=4 * (count + 2 * width) * (hidden + width),
        ),
    )(h, dy, *weights)
    if direct:
        return f, da, grads[0]
    down, up = grads
    up = up.reshape(owners, part, 4, width).transpose(0, 2, 1, 3)
    packed = jnp.concatenate(
        [down.reshape(owners, 4 * part, width), up.reshape(owners, 4 * part, width)], 1
    )
    return f, da, packed


def turn(x, tables, sign=1.0):
    cosine, ahead, behind = tables
    half = ROT // 2
    return (
        x * cosine
        + pltpu.roll(x, 2 * HD - half, 1) * (sign * ahead)
        + pltpu.roll(x, half, 1) * (sign * behind)
    )


def key_only(tables):
    cosine, ahead, behind = tables
    first = lax.broadcasted_iota(jnp.int32, cosine.shape, 1) < HD
    return jnp.where(first, cosine, 1.0), jnp.where(first, ahead, 0.0), jnp.where(first, behind, 0.0)


def turn_tables(first, count):
    cosine, sine = angles(first, count)
    half = ROT // 2
    rest = jnp.zeros((count, HD - ROT), F32)
    none = jnp.zeros((count, half), F32)
    cosine = jnp.concatenate([cosine, rest + 1.0], 1)
    ahead = jnp.concatenate([-sine[:, :half], none, rest], 1)
    behind = jnp.concatenate([none, sine[:, half:], rest], 1)
    return [jnp.concatenate([t, t], 1) for t in (cosine, ahead, behind)]


def normed_rows(x):
    mean = jnp.mean(x, -1, keepdims=True)
    centered = x - mean
    scale = lax.rsqrt(jnp.mean(centered * centered, -1, keepdims=True) + EPS_NORM)
    return centered * scale, scale


def norm_rows_of(small_ref):
    return small_ref[:, pl.ds(2 * HD, 2 * HD)].astype(F32).T


def entry_body(x_ref, small_ref, cos_ref, ahead_ref, behind_ref, h1_ref, h2_ref, kv_ref, *, block):
    params = norm_rows_of(small_ref)
    weight = small_ref[:, pl.ds(0, 2 * HD)]
    for r in range(0, x_ref.shape[1], block):
        rows = pl.ds(r, block)
        normed, _ = normed_rows(x_ref[0, rows, :].astype(F32))
        first = (normed * params[0:1] + params[1:2]).astype(BF)
        h1_ref[0, rows, :] = first
        h2_ref[0, rows, :] = (normed * params[2:3] + params[3:4]).astype(BF)
        pair = jnp.dot(first, weight, preferred_element_type=F32)
        tables = key_only([t[rows, :] for t in (cos_ref, ahead_ref, behind_ref)])
        kv_ref[0, rows, :] = turn(pair, tables).astype(BF)


def entry(x, small, tables):
    batch, local, width = x.shape
    rows = pl.BlockSpec((1, local, width), lambda b: (b, 0, 0))
    table = pl.BlockSpec((local, 2 * HD), lambda b: (0, 0))
    return pl.pallas_call(
        functools.partial(entry_body, block=local // 3),
        grid=(batch,),
        in_specs=[rows, pl.BlockSpec(small.shape, lambda b: (0, 0)), table, table, table],
        out_specs=[rows, rows, pl.BlockSpec((1, local, 2 * HD), lambda b: (b, 0, 0))],
        out_shape=[jax.ShapeDtypeStruct(x.shape, BF)] * 2
        + [jax.ShapeDtypeStruct((batch, local, 2 * HD), BF)],
        compiler_params=pltpu.CompilerParams(
            dimension_semantics=("arbitrary",), vmem_limit_bytes=VMEM_BYTES
        ),
        cost_estimate=pl.CostEstimate(
            flops=4 * batch * local * width * HD,
            transcendentals=batch * local,
            bytes_accessed=8 * batch * local * width,
        ),
    )(x, small, *tables)


def query_body(h_ref, dy_ref, weight_ref, cos_ref, ahead_ref, behind_ref, q_ref, do_ref):
    mixed = jnp.dot(h_ref[0], weight_ref[:, pl.ds(0, D)], preferred_element_type=F32)
    tables = cos_ref[...], ahead_ref[...], behind_ref[...]
    for c in range(0, D, 2 * HD):
        q = turn(mixed[:, c : c + 2 * HD], tables).astype(BF)
        q_ref[0, :, pl.ds(c, 2 * HD)] = q * BF(HD ** (-0.5))
    do_ref[0] = lax.dot_general(
        dy_ref[0], weight_ref[:, pl.ds(D, D)], COLS_LAST, preferred_element_type=F32
    ).astype(BF)


def queries(h, dy, middle, tables):
    batch, local, width = h.shape
    rows = pl.BlockSpec((1, local, width), lambda b: (b, 0, 0))
    table = pl.BlockSpec((local, 2 * HD), lambda b: (0, 0))
    return pl.pallas_call(
        query_body,
        grid=(batch,),
        in_specs=[rows, rows, pl.BlockSpec(middle.shape, lambda b: (0, 0)), table, table, table],
        out_specs=[rows, rows],
        out_shape=[jax.ShapeDtypeStruct(h.shape, BF)] * 2,
        compiler_params=pltpu.CompilerParams(
            dimension_semantics=("arbitrary",), vmem_limit_bytes=VMEM_BYTES
        ),
        cost_estimate=pl.CostEstimate(
            flops=4 * batch * local * width * width,
            transcendentals=0,
            bytes_accessed=8 * batch * local * width,
        ),
    )(h, dy, middle, *tables)


def back_body(
    core_of, weight_of, x_ref, cot_ref, h_ref, o_ref, dq_ref, dh2_ref, middle_ref, small_ref,
    cos_ref, ahead_ref, behind_ref, *refs, devices,
):
    pair_refs, refs = refs[: devices * weight_of.shape[0]], refs[devices * weight_of.shape[0] :]
    dx_ref, *grad_refs, acc, norm_acc, pair_acc = refs
    b, last = pl.program_id(0), pl.num_programs(0) - 1
    tables = cos_ref[...], ahead_ref[...], behind_ref[...]
    params = norm_rows_of(small_ref)
    dy = cot_ref[0].astype(F32) * weight_of[b]
    dy_low = dy.astype(BF)
    for at in range(weight_of.shape[0]):

        @pl.when(b == at)
        def _(parts=pair_refs[devices * at : devices * (at + 1)]):
            total = parts[0][...].astype(F32)
            for part in parts[1:]:
                total = total + part[...].astype(F32)
            pair_acc[...] = total.astype(BF).astype(F32)

    pair = turn(pair_acc[...], key_only(tables), -1.0).astype(BF)
    turned = [
        turn(dq_ref[0, :, pl.ds(c, 2 * HD)].astype(F32), tables, -1.0).astype(BF)
        for c in range(0, D, 2 * HD)
    ]
    dz = jnp.concatenate(turned + [pair], 1)
    wide = dz.shape[1]
    made = lax.dot_general(h_ref[0], dz, ROWS_FIRST, preferred_element_type=F32)
    made_out = lax.dot_general(o_ref[0], dy_low, ROWS_FIRST, preferred_element_type=F32)

    @pl.when(b == 0)
    def _():
        acc[:, pl.ds(0, wide)] = made
        acc[:, pl.ds(wide, D)] = made_out
        norm_acc[...] = jnp.zeros_like(norm_acc)

    @pl.when(b > 0)
    def _():
        acc[:, pl.ds(0, wide)] += made
        acc[:, pl.ds(wide, D)] += made_out

    weights = jnp.concatenate([middle_ref[:, pl.ds(0, D)], small_ref[:, pl.ds(0, 2 * HD)]], 1)
    dh1 = lax.dot_general(dz, weights, COLS_LAST, preferred_element_type=F32)
    dh2 = dh2_ref[0]
    normed, scale = normed_rows(x_ref[0].astype(F32))
    norm_acc[0:1] += jnp.sum(dh1 * normed, 0, keepdims=True)
    norm_acc[1:2] += jnp.sum(dh1, 0, keepdims=True)
    norm_acc[2:3] += jnp.sum(dh2 * normed, 0, keepdims=True)
    norm_acc[3:4] += jnp.sum(dh2, 0, keepdims=True)
    inner = dh1 * params[0:1] + dh2 * params[2:3]
    inner = inner - jnp.mean(inner, -1, keepdims=True) - normed * jnp.mean(
        inner * normed, -1, keepdims=True
    )
    dx_ref[0] = (dy + scale * inner).astype(BF)

    @pl.when(b == last)
    def _():
        acc[:, pl.ds(wide + D, 2 * HD)] = norm_acc[...].T
        if len(grad_refs) == 1:
            grad_refs[0][...] = acc[...].astype(BF)
            return
        send_ref, keep_ref = grad_refs
        pairs, part, _ = send_ref.shape
        for p in range(pairs):
            for ref, core in ((send_ref, 1 - core_of[0]), (keep_ref, core_of[0])):
                rows = pl.ds(pl.multiple_of((2 * p + core) * part, part), part)
                ref[p] = acc[rows, :].astype(ref.dtype)


def back(core, row_weight, owners, x, cot, h, o, dq, pairs, dh2, middle, small, tables):
    batch, local, width = x.shape
    rows = pl.BlockSpec((1, local, width), lambda b, *s: (b, 0, 0))
    table = pl.BlockSpec((local, 2 * HD), lambda b, *s: (0, 0))
    columns = 2 * width + 4 * HD
    part = width // owners
    if part % 16 == 0:
        half = (owners // 2, part, columns)
        made = [jax.ShapeDtypeStruct(half, BF), jax.ShapeDtypeStruct(half, F32)]
    else:
        made = [jax.ShapeDtypeStruct((width, columns), BF)]
    return pl.pallas_call(
        functools.partial(back_body, devices=len(pairs[0])),
        grid_spec=pltpu.PrefetchScalarGridSpec(
            num_scalar_prefetch=2,
            grid=(batch,),
            in_specs=[rows] * 6
            + [pl.BlockSpec(w.shape, lambda b, *s: (0, 0)) for w in (middle, small)]
            + [table] * (3 + sum(len(parts) for parts in pairs)),
            out_specs=[rows]
            + [pl.BlockSpec(m.shape, lambda b, *s, n=len(m.shape): (0,) * n) for m in made],
            scratch_shapes=[
                pltpu.VMEM((width, columns), F32),
                pltpu.VMEM((2 * HD, width), F32),
                pltpu.VMEM((local, 2 * HD), F32),
            ],
        ),
        out_shape=[jax.ShapeDtypeStruct(x.shape, BF), *made],
        compiler_params=pltpu.CompilerParams(
            dimension_semantics=("arbitrary",), vmem_limit_bytes=VMEM_BYTES
        ),
        cost_estimate=pl.CostEstimate(
            flops=6 * batch * local * width * width,
            transcendentals=batch * local,
            bytes_accessed=16 * batch * local * width,
        ),
    )(
        core, row_weight, x, cot, h, o, dq, dh2, middle, small, *tables,
        *[part for parts in pairs for part in parts],
    )


def sum_body(a_ref, w_ref, out_ref):
    width = out_ref.shape[1]
    part = lax.dot_general(
        a_ref[...], w_ref[...].reshape(width, width), COLS_LAST, preferred_element_type=F32
    )

    @pl.when(pl.program_id(0) == 0)
    def _():
        out_ref[...] = part

    @pl.when(pl.program_id(0) > 0)
    def _():
        out_ref[...] += part


def up_back(da, weights, specs):
    count, hidden = da.shape
    width = hidden // 4
    return pl.pallas_call(
        sum_body,
        grid=(4,),
        in_specs=[pl.BlockSpec((count, width), lambda c: (0, c)), specs[0]],
        out_specs=pl.BlockSpec((count, width), lambda c: (0, 0)),
        out_shape=jax.ShapeDtypeStruct((count, width), F32),
        compiler_params=pltpu.CompilerParams(
            dimension_semantics=("arbitrary",), vmem_limit_bytes=VMEM_BYTES
        ),
        cost_estimate=pl.CostEstimate(
            flops=2 * count * width * hidden,
            transcendentals=0,
            bytes_accessed=2 * count * hidden + 4 * count * width + 2 * width * hidden,
        ),
    )(da, weights[0])


def output_body(x_ref, o_ref, out_w_ref, f_ref, w_ref, y_ref, acc):
    step, last = pl.program_id(0), pl.num_programs(0) - 1
    width = acc.shape[1]
    part = jnp.dot(f_ref[...], w_ref[...].reshape(width, width), preferred_element_type=F32)

    @pl.when(step == 0)
    def _():
        heads = jnp.dot(o_ref[...], out_w_ref[...], preferred_element_type=F32)
        acc[...] = x_ref[...].astype(F32) + heads + part

    @pl.when(step > 0)
    def _():
        acc[...] += part

    @pl.when(step == last)
    def _():
        y_ref[...] = acc[...].astype(BF)


def output(x, o, middle, f, weights, specs):
    count, hidden = f.shape
    width = hidden // 4
    whole = pl.BlockSpec((count, width), lambda c: (0, 0))
    return pl.pallas_call(
        output_body,
        grid=(4,),
        in_specs=[
            whole,
            whole,
            pl.BlockSpec((width, width), lambda c: (0, 1)),
            pl.BlockSpec((count, width), lambda c: (0, c)),
            specs[1],
        ],
        out_specs=whole,
        out_shape=jax.ShapeDtypeStruct((count, width), BF),
        scratch_shapes=[pltpu.VMEM((count, width), F32)],
        compiler_params=pltpu.CompilerParams(
            dimension_semantics=("arbitrary",), vmem_limit_bytes=VMEM_BYTES
        ),
        cost_estimate=pl.CostEstimate(
            flops=2 * count * width * (hidden + width),
            transcendentals=0,
            bytes_accessed=2 * (count + width) * hidden + 6 * count * width,
        ),
    )(x, o, middle, f, weights[1])


def adam_store(weight_ref, first_ref, second_ref, grad, outs, rate, decay):
    results = adam_update(weight_ref[...], first_ref[...], second_ref[...], grad, rate, decay)
    for out_ref, result in zip(outs, results):
        out_ref[...] = result


def adam_body(seq_at, factor_ref, up_grad_ref, down_grad_ref, *refs):
    parts, refs, joined = refs[:4], refs[4:-1], refs[-1]
    factor = factor_ref[0, 0]
    qkv, out, up, down, norm = [refs[3 * i : 3 * i + 3] for i in range(5)]
    outs = refs[15:]
    qkv_out, out_out, up_out, down_out, norm_out = [outs[3 * i : 3 * i + 3] for i in range(5)]
    adam_store(*up, up_grad_ref[...].astype(F32) * factor, up_out, RATE_SMALL, DECAY)
    adam_store(*down, down_grad_ref[...].astype(F32) * factor, down_out, RATE_SMALL, DECAY)

    @pl.when(pl.program_id(0) == pl.num_programs(0) - 1)
    def _():
        for mask, ref in enumerate(parts):
            joined[seq_at[0] ^ mask] = unpack_quarter(ref)
        rest = joined[...].reshape(-1, joined.shape[2])
        wide = qkv[0].shape[1]
        adam_store(*qkv, rest[:, :wide] * factor, qkv_out, RATE_SMALL, DECAY)
        adam_store(*out, rest[:, wide : wide + D] * factor, out_out, RATE_LARGE, DECAY)
        grad = rest[:, wide + D :].T[:4] * factor
        adam_store(*norm, grad, norm_out, RATE_NORM, 0.0)


def adam_all(seq_at, factor, feed, rest, qkv, out, up, down, norm):
    part, hidden = up[0].shape
    width = hidden // 4
    column = pl.BlockSpec((part, width), lambda c, p: (0, c))
    row = pl.BlockSpec((part, width), lambda c, p: (c, 0))

    def whole(x):
        return pl.BlockSpec(x.shape, lambda c, p: (0, 0))

    states = [*qkv, *out, *up, *down, *norm]
    specs = (
        [whole(x) for x in qkv + out] + [column] * 3 + [row] * 3 + [whole(x) for x in norm]
    )
    return pl.pallas_call(
        adam_body,
        grid_spec=pltpu.PrefetchScalarGridSpec(
            num_scalar_prefetch=1,
            grid=(4,),
            in_specs=[
                pl.BlockSpec(memory_space=pltpu.SMEM),
                pl.BlockSpec((part, width), lambda c, p: (4 + c, 0)),
                row,
                *[whole(x) for x in rest],
                *specs,
            ],
            out_specs=specs,
            scratch_shapes=[pltpu.VMEM((4, rest[0].shape[0], rest[0].shape[1] - 2 * HD), F32)],
        ),
        out_shape=[jax.ShapeDtypeStruct(x.shape, F32) for x in states],
        compiler_params=pltpu.CompilerParams(
            dimension_semantics=("arbitrary",), vmem_limit_bytes=VMEM_BYTES
        ),
    )(seq_at, factor, feed, feed, *rest, *states)


def swap(x, axis, mask):
    return lax.ppermute(x, axis, [(i, i ^ mask) for i in range(lax.axis_size(axis))])


def local_call(body, at, inputs, shapes, scratch=()):
    return pl.pallas_call(
        body,
        grid_spec=pltpu.PrefetchScalarGridSpec(
            num_scalar_prefetch=1,
            grid=(1,),
            in_specs=[pl.BlockSpec(a.shape, lambda i, p, n=a.ndim: (0,) * n) for a in inputs],
            out_specs=[pl.BlockSpec(s, lambda i, p, n=len(s): (0,) * n) for s, _ in shapes],
            scratch_shapes=list(scratch),
        ),
        out_shape=[jax.ShapeDtypeStruct(s, kind) for s, kind in shapes],
        compiler_params=pltpu.CompilerParams(
            dimension_semantics=("arbitrary",), vmem_limit_bytes=VMEM_BYTES // 3
        ),
    )(at, *inputs)


def split_chips(at, keep, came, send_left, send_right, keep_left, keep_right):
    x, y = at[0], at[1]
    half = send_left.shape[2]
    left, right = pl.ds(0, half), pl.ds(half, half)
    for i in range(2):
        for ref, block, columns in (
            (send_left, 2 * i + 1 - x, left),
            (keep_left, 2 * i + x, left),
            (send_right, 2 * (1 - y) + i, right),
            (keep_right, 2 * y + i, right),
        ):
            total = keep[block, :, columns] + came[block, :, columns].astype(F32)
            ref[i] = total.astype(ref.dtype)


def split_last(at, left, right, a, b, send_left, send_right, keep_left, keep_right):
    x, y = at[0], at[1]
    for ref, keep, came, block in (
        (send_left, left, a, 1 - y),
        (keep_left, left, a, y),
        (send_right, right, b, 1 - x),
        (keep_right, right, b, x),
    ):
        ref[...] = (keep[block] + came[block].astype(F32)).astype(ref.dtype)


def split_seq(at, left, right, a, b, one, two, three, keep, total):
    half = left.shape[1]
    quarters, rows, _ = total.shape
    total[:, :, pl.ds(0, half)] = (left[...] + a[...].astype(F32)).reshape(quarters, rows, half)
    total[:, :, pl.ds(half, half)] = (right[...] + b[...].astype(F32)).reshape(quarters, rows, half)
    seq = at[2]
    keep[...] = total[seq]
    for mask, ref in ((1, one), (2, two), (3, three)):
        ref[...] = total[seq ^ mask].astype(BF)


def pack_quarter(at, keep, one, two, three, packed):
    total = keep[...]
    for ref in (one, two, three):
        total = total + ref[...].astype(F32)
    wide = total.shape[1]
    packed[:, pl.ds(0, wide)] = total.astype(BF)
    pair = total[:, D : D + 2 * HD]
    packed[:, pl.ds(wide, 2 * HD)] = (pair - pair.astype(BF).astype(F32)).astype(BF)


def unpack_quarter(ref):
    wide = ref.shape[1] - 2 * HD
    pair = pl.ds(D, 2 * HD)
    after = D + 2 * HD
    return jnp.concatenate(
        [
            ref[:, pl.ds(0, D)].astype(F32),
            ref[:, pair].astype(F32) + ref[:, pl.ds(wide, 2 * HD)].astype(F32),
            ref[:, pl.ds(after, wide - after)].astype(F32),
        ],
        1,
    )


def add_squares(at, *refs):
    *quarters, feed, squares = refs
    total = jnp.zeros(squares.shape, F32)
    for grad in [unpack_quarter(ref) for ref in quarters] + [feed[...].astype(F32)]:
        parts = jnp.sum(jnp.square(grad), 0, keepdims=True)
        for c in range(0, grad.shape[1], 2 * HD):
            total = total + parts[:, c : c + 2 * HD]
    squares[...] = total


def beside(sends, work=lambda: (), inputs=()):
    flat, inputs = lax.optimization_barrier(([x for x, _, _ in sends], inputs))
    came = [swap(x, axis, mask) for x, (_, axis, mask) in zip(flat, sends)]
    return lax.optimization_barrier((came, work(*inputs)))


def batch_sum(at, send, keep, work, inputs):
    (came,), _ = beside([(send, "batch", 1)])
    _, r, c = keep.shape
    two, one, quarter = (2, r, c // 2), (r, c // 2), (r // 4, c)
    send_left, send_right, left, right = local_call(
        split_chips, at, [keep, came], [(two, BF), (two, BF), (two, F32), (two, F32)]
    )
    (a, b), _ = beside([(send_left, "batch", 2), (send_right, "batch", 4)])
    send_left, send_right, left, right = local_call(
        split_last, at, [left, right, a, b], [(one, BF), (one, BF), (one, F32), (one, F32)]
    )
    (a, b), _ = beside([(send_left, "batch", 4), (send_right, "batch", 2)])
    *sends, keep = local_call(
        split_seq,
        at,
        [left, right, a, b],
        [(quarter, BF)] * 3 + [(quarter, F32)],
        [pltpu.VMEM((4, *quarter), F32)],
    )
    came, result = beside([(x, "seq", m + 1) for m, x in enumerate(sends)], work, inputs)
    (own,) = local_call(pack_quarter, at, [keep, *came], [((r // 4, c + 2 * HD), BF)])
    came, _ = beside([(own, "seq", mask) for mask in (1, 2, 3)])
    return [own, *came], result


def shift(x, by):
    count = lax.axis_size("seq")
    return lax.ppermute(x, "seq", [(s, s + by) for s in range(count) if 0 <= s + by < count])


def shards(
    tokens,
    cotangent,
    tags,
    loss_weights,
    w_qkv,
    m_qkv,
    v_qkv,
    w_out,
    m_out,
    v_out,
    w_up,
    m_up,
    v_up,
    w_down,
    m_down,
    v_down,
    norm_params,
    m_norm,
    v_norm,
):
    owners = lax.axis_size("batch")
    seq_count = lax.axis_size("seq")
    seq_at = lax.axis_index("seq")
    seq_rows, local, width = tokens.shape
    count = seq_rows * local
    part = w_qkv.shape[0]
    fence = lax.optimization_barrier

    small = jnp.concatenate(
        [w_qkv[:, D:], norm_params.T, jnp.zeros((part, 2 * HD - 4), F32)], 1
    ).astype(BF)
    small = lax.all_gather(small, "batch", axis=0, tiled=True)
    middle = jnp.concatenate([w_qkv[:, :D], w_out], 1).astype(BF)
    middle = lax.all_gather(middle, "batch", axis=0, tiled=True)
    packed = jnp.concatenate([w_down] + [w_up[:, D * i : D * (i + 1)] for i in range(4)], 0)
    packed, small = fence((packed.astype(BF), small))
    packed = lax.all_gather(packed, "batch", axis=0, tiled=True).reshape(owners, 8 * part, D)
    weights, specs = feed_weights(packed)

    tables = turn_tables(seq_at * local, local)
    subsets = jnp.arange(loss_weights.shape[0])
    row_weight = jnp.sum(
        jnp.where(tags[:, None] == subsets[None, :], loss_weights[None, :], 0.0), -1
    )
    grad_low = (cotangent.astype(F32) * row_weight[:, None, None]).astype(BF)

    first_low, second_low, pair = entry(tokens, small, tables)
    query, grad_heads = queries(first_low, grad_low, middle, tables)

    def gather_pair(own):
        return [own] + [shift(own, by) for by in range(1, seq_count)]

    arrived, query = fence((gather_pair(pair[0]), query))
    place = jnp.reshape(seq_at, (1,)).astype(jnp.int32)

    state, came = (), []
    for at in range(seq_rows):
        if at == seq_rows // 2:
            second_low, state = fence((second_low, state))
            active_low, grad_up_pre, grad_feed = feed_forward(
                second_low.reshape(count, D), grad_low.reshape(count, D), weights, specs, owners
            )
            feed_sum = lax.psum_scatter(
                grad_feed.reshape(owners * 8 * part, D), "batch", scatter_dimension=0, tiled=True
            )
            state, grad_up_pre = fence((state, grad_up_pre))
        keys = arrived
        if at + 1 < seq_rows:
            own, keys = fence((pair[at + 1], keys))
            arrived = gather_pair(own)
        heads, grad_query, *grad_pair = attention(place, query, grad_heads, keys, at, state)
        state = heads, grad_query
        came.append([shift(g, -by) if by else g for by, g in enumerate(grad_pair)])
        if at + 1 < seq_rows:
            arrived, state = fence((arrived, state))
    heads, grad_query = state

    grad_up_pre, heads = fence((grad_up_pre, heads))
    grad_second = up_back(grad_up_pre, weights, specs)
    came, grad_second, feed_sum = fence((came, grad_second, feed_sum))
    feed_sum = lax.psum(feed_sum, "seq")

    def input_side():
        return back(
            jnp.reshape(lax.axis_index("batch") % 2, (1,)),
            row_weight,
            owners,
            tokens,
            cotangent,
            first_low,
            heads,
            grad_query,
            came,
            grad_second.reshape(seq_rows, local, D),
            middle,
            small,
            tables,
        )

    def output_side(x, o, w, f):
        return output(x, o, w, f, weights, specs)

    output_inputs = tokens.reshape(count, D), heads.reshape(count, D), middle, active_low

    if owners == 8 and seq_count == 4:
        batch_at = lax.axis_index("batch")
        at = jnp.stack([(batch_at // 2) % 2, batch_at // 4, seq_at])

        def rest_of_layer(_, carry):
            input_grad, send, keep = input_side()
            parts, layer_out = batch_sum(at, send, keep, output_side, output_inputs)
            return input_grad, layer_out, parts

        quarter = (part // 4, w_qkv.shape[1] + D + 4 * HD)
        unused = (
            second_low,
            query.reshape(count, D),
            [jnp.zeros(quarter, BF)] * 4,
        )
        once = 1 + jnp.minimum(tags[0], 0)
        input_grad, layer_out, rest = lax.fori_loop(0, once, rest_of_layer, unused)
        feed_sum, rest = fence((feed_sum, rest))
        (squares,) = local_call(add_squares, at, [*rest, feed_sum], [((1, 2 * HD), F32)])
        total_squares = lax.psum(jnp.sum(squares), "batch")
    else:
        input_grad, rest = input_side()
        layer_out = output_side(*output_inputs)
        rest = lax.psum_scatter(rest.astype(F32), "batch", scatter_dimension=0, tiled=True)
        rest = lax.psum(rest, "seq")
        squares = [jnp.sum(jnp.square(x.astype(F32))) for x in (rest, feed_sum)]
        total_squares = lax.psum(sum(squares), "batch")
    layer_out = layer_out.reshape(seq_rows, local, D)
    grad_norm = jnp.sqrt(total_squares)
    factor = CLIP_NORM / jnp.maximum(grad_norm, CLIP_NORM)
    states = (
        (w_qkv, m_qkv, v_qkv),
        (w_out, m_out, v_out),
        (w_up, m_up, v_up),
        (w_down, m_down, v_down),
        (norm_params, m_norm, v_norm),
    )
    if isinstance(rest, list):
        results = adam_all(at[2:], factor.reshape(1, 1), feed_sum, rest, *states)
    else:
        qkv_width = w_qkv.shape[1]
        down_sum, up_sum = feed_sum[: 4 * part], feed_sum[4 * part :]
        up_sum = up_sum.astype(F32).reshape(4, part, D).transpose(1, 0, 2)
        grads = (
            rest[:, :qkv_width],
            rest[:, qkv_width : qkv_width + D],
            up_sum.reshape(part, 4 * D),
            down_sum.astype(F32),
            rest[:, qkv_width + D : qkv_width + D + 4].T,
        )
        rates = (RATE_SMALL, RATE_LARGE, RATE_SMALL, RATE_SMALL, RATE_NORM)
        decays = (DECAY, DECAY, DECAY, DECAY, 0.0)
        results = []
        for three, grad, rate, decay in zip(states, grads, rates, decays):
            results.extend(adam_update(*three, grad * factor, rate, decay))
    return (layer_out, input_grad, grad_norm, *results)


def solution(mesh):
    in_specs = (
        P("batch", "seq", None),
        P("batch", "seq", None),
        P("batch"),
        P(),
        P("batch", None),
        P("batch", None),
        P("batch", None),
        P("batch", None),
        P("batch", None),
        P("batch", None),
        P("batch", None),
        P("batch", None),
        P("batch", None),
        P("batch", None),
        P("batch", None),
        P("batch", None),
        P(None, "batch"),
        P(None, "batch"),
        P(None, "batch"),
    )
    out_specs = (
        P("batch", "seq", None),
        P("batch", "seq", None),
        P(),
        P("batch", None),
        P("batch", None),
        P("batch", None),
        P("batch", None),
        P("batch", None),
        P("batch", None),
        P("batch", None),
        P("batch", None),
        P("batch", None),
        P("batch", None),
        P("batch", None),
        P("batch", None),
        P(None, "batch"),
        P(None, "batch"),
        P(None, "batch"),
    )
    return jax.shard_map(shards, mesh=mesh, in_specs=in_specs, out_specs=out_specs, check_vma=False)
```

time: 598 us -> 322 us (0.54)
  waiting for transfers between devices: 277 us -> 91.7 us
  matrix products: 101 us -> 0 us
  Pallas kernels: 28.6 us -> 122 us
  local copies, waits for them, and re-layouts: 69 us -> 11.7 us
  other arithmetic: 51.1 us -> 6.73 us
  starting transfers between devices: 14.6 us -> 43.6 us
    dot_general x13 -> x0, matrix products: 101 us -> none  [the longest x1 33.5 us: shards(): lax.dot_general(grad_low, full_down, COLS_LAST, preferred_element_type=F32)]
    psum x2 -> x1, waiting for transfers between devices: 97.8 us -> 0.01 us  [shards(): feed_sum = lax.psum(feed_sum, 'seq')]
    pallas_call x1 -> x14, Pallas kernels: 28.6 us -> 122 us  [the longest x2 34.6 us: attention(): pl.pallas_call(functools.partial(attention_body, local=local, devices=dev...]
    ppermute x6 -> x12, waiting for transfers between devices: 82.1 us -> 31.6 us  [shift(): lax.ppermute(x, 'seq', [(s, s + by) for s in range(count) if 0 <= s + by...]
    unnamed x9 -> x4, waiting for transfers between devices: 44.8 us -> 0.07 us
    unnamed x151 -> x41, local copies, waits for them, and re-layouts: 33.3 us -> 2.94 us
    all_gather x2 -> x1, waiting for transfers between devices: 51.8 us -> 28.2 us  [shards(): lax.all_gather(packed, 'batch', axis=0, tiled=True)]
    ppermute x0 -> x11, waiting for transfers between devices: none -> 22.7 us  [swap(): lax.ppermute(x, axis, [(i, i ^ mask) for i in range(lax.axis_size(axis))])]
  transfers between devices with their start and end apart: 14 -> 27, of which waited for: 7 -> 13; matrix products, arithmetic and copies ran while one was open for 29% -> 3% of each run, Pallas kernels for 5% -> 27%
where the time goes in v2:
time: 322 us; the launch traced here: 316 us
  Pallas kernels  122 us (38%)
  waiting for transfers between devices  91.7 us (28%)
  starting transfers between devices  43.6 us (14%)
  blocking collectives  23.6 us (7%)
  between operations  16.6 us (5%)
  local copies, waits for them, and re-layouts  11.7 us (4%)
  other arithmetic  6.73 us (2%)
    pallas_call x2, Pallas kernels, attention(): pl.pallas_call(functools.partial(attention_body, local=local, devices=dev...  34.6 us
    ppermute x12, waiting for transfers between devices, shift(): lax.ppermute(x, 'seq', [(s, s + by) for s in range(count) if 0 <= s + by...  31.6 us
    all_gather x1, waiting for transfers between devices, shards(): lax.all_gather(packed, 'batch', axis=0, tiled=True)  28.2 us
    ppermute x12, starting transfers between devices, shift(): lax.ppermute(x, 'seq', [(s, s + by) for s in range(count) if 0 <= s + by...  26.2 us
    pallas_call x1, Pallas kernels, feed_forward(): pl.pallas_call(functools.partial(feed_body, block=count // 3, direct=dire...  26 us
    ppermute x11, waiting for transfers between devices, swap(): lax.ppermute(x, axis, [(i, i ^ mask) for i in range(lax.axis_size(axis))])  22.7 us
    ppermute x11, starting transfers between devices, swap(): lax.ppermute(x, axis, [(i, i ^ mask) for i in range(lax.axis_size(axis))])  17.2 us
    pallas_call x1, Pallas kernels, back(): pl.pallas_call(functools.partial(back_body, devices=len(pairs[0])), grid_...  15.7 us
  transfers between devices with their start and end apart: 27, of which 13 were waited for; matrix products, arithmetic and copies ran while one was open for 3% of the time, Pallas kernels for 27%

profile of v2, /device:TPU:0, one launch (start us, length us, event | category | flops | bytes accessed | tf_op | source)
XLA Modules:
  0.0 316.2 jit_solution(628000940960993146)
XLA Ops:
  11.3 11.2 %all_gather.9.small_ref = bf16[768,256]{1,0:T(8,128)(2,1)S(1)} all-gather(bf16[96,256]{1,0:T(8,128)(2,1)S(1)} %maximum_maximum_fusion), channel_id=1, replica_groups=mesh['batch'=8,'seq'=4] {'batch'}, dimensions={0}, use_global_device_ids=true | all-gather | bytes 442368 | tf_op jit(solution)/shard_map/all_gather | solution.py:886
  26.9 4.1 %shard_map.322 = (bf16[2,456,768]{2,1,0:T(8,128)(2,1)}, bf16[2,456,768]{2,1,0:T(8,128)(2,1)}, bf16[2,456,128]{2,1,0:T(8,128)(2,1)}) custom-call(bf16[2,456,768]{2,1,0:T(8,128)(2,1)S(1)} %copy-done.3, bf16[768,256]{1,0:T(8,128)(2,1)S(1)} %all_gather.9.small_ref, f32[456,128]{1,0:T(8,128)S(1)} %pad_maximum_fusion.1.cos_ref, ...), custom_call_target="tpu_custom_call" | custom-call | flops 179306496 | bytes 5603328 | tf_op jit(solution)/shard_map/pallas_call | solution.py:421
  32.7 4.1 %collective-permute-start.11 = (bf16[456,128]{1,0:T(8,128)(2,1)S(1)}, bf16[456,128]{1,0:T(8,128)(2,1)}, u32[]{:S(2)}, u32[]{:S(2)}) collective-permute-start(bf16[456,128]{1,0:T(8,128)(2,1)S(1)} %get-tuple-element.521.refs_0_), channel_id=1, source_target_pairs={{0,1},{1,2},{2,3},{4,5},{5,6},{6,7},{8,9},{9,10},{10,11},{12,13},{... | collective-permute-start | bytes 350216 | tf_op jit(solution)/shard_map/ppermute | solution.py:851
  36.8 4.5 %collective-permute-start.12 = (bf16[456,128]{1,0:T(8,128)(2,1)S(1)}, bf16[456,128]{1,0:T(8,128)(2,1)}, u32[]{:S(2)}, u32[]{:S(2)}) collective-permute-start(bf16[456,128]{1,0:T(8,128)(2,1)S(1)} %get-tuple-element.521.refs_0_), channel_id=1, source_target_pairs={{0,2},{1,3},{4,6},{5,7},{8,10},{9,11},{12,14},{13,15},{16,18},{17,... | collective-permute-start | bytes 350216 | tf_op jit(solution)/shard_map/ppermute | solution.py:851
  45.0 5.5 %shard_map.323 = (bf16[2,456,768]{2,1,0:T(8,128)(2,1)}, bf16[2,456,768]{2,1,0:T(8,128)(2,1)}) custom-call(bf16[2,456,768]{2,1,0:T(8,128)(2,1)S(1)} %copy-done.6, bf16[2,456,768]{2,1,0:T(8,128)(2,1)} %multiply_convert_fusion.dy_ref, bf16[768,1536]{1,0:T(8,128)(2,1)} %all-gather.3.cloned.1.call-done.weight_ref, f32[456,128]{1,0:T(8,128)} %copy-done.9, ...), custom_call_target="tpu_custom_call" | custom-call | flops 2151677952 | bytes 5603328 | tf_op jit(solution)/shard_map/pallas_call | solution.py:454
  52.5 3.7 %collective-permute-start.15 = (bf16[456,128]{1,0:T(8,128)(2,1)}, bf16[456,128]{1,0:T(8,128)(2,1)}, u32[]{:S(2)}, u32[]{:S(2)}) collective-permute-start(bf16[456,128]{1,0:T(8,128)(2,1)} %get-tuple-element.534.refs_0_), channel_id=1, source_target_pairs={{0,2},{1,3},{4,6},{5,7},{8,10},{9,11},{12,14},{13,15},{16,18},{17,... | collective-permute-start | bytes 350216 | tf_op jit(solution)/shard_map/ppermute | solution.py:851
  58.3 17.1 %shard_map.324 = (bf16[2,456,768]{2,1,0:T(8,128)(2,1)S(1)}, bf16[2,456,768]{2,1,0:T(8,128)(2,1)S(1)}, bf16[456,128]{1,0:T(8,128)(2,1)S(1)}, bf16[456,128]{1,0:T(...) custom-call(s32[1]{0:T(128)} %bitcast.5.place.seq_at, bf16[2,456,768]{2,1,0:T(8,128)(2,1)} %get-tuple-element.519.q_ref, ...), custom_call_target="tpu_custom_call" | custom-call | flops 7665352704 | bytes 2801664 | tf_op jit(solution)/shard_map/pallas_call | solution.py:212
  75.4 28.2 %all-gather.5.cloned.1.call-done = bf16[6144,768]{1,0:T(8,128)(2,1)} async-done(((bf16[768,768]{1,0:T(8,128)(2,1)}), bf16[6144,768]{1,0:T(8,128)(2,1)}) %all-gather.5.cloned.1.call-update) | async-done | bytes 9437200 | tf_op jit(solution)/shard_map/all_gather | solution.py:891
  103.6 26.0 %shard_map.325 = (bf16[912,3072]{1,0:T(8,128)(2,1)}, bf16[912,3072]{1,0:T(8,128)(2,1)}, bf16[8,768,768]{2,1,0:T(8,128)(2,1)}) custom-call(bf16[912,768]{1,0:T(8,128)(2,1)} %bitcast.39, bf16[912,768]{1,0:T(8,128)(2,1)} %bitcast.37, bf16[8,768,768]{2,1,0:T(8,128)(2,1)} %bitcast.25, bf16[8,768,768]{2,1,0:T(8,128)(2,1)} %bitcast.26), custom_call_target="tpu_custom_call" | custom-call | flops 17213423616 | bytes 37601280 | tf_op jit(solution)/shard_map/pallas_call | solution.py:337
  134.5 17.5 %shard_map.326 = (bf16[2,456,768]{2,1,0:T(8,128)(2,1)S(1)}, bf16[2,456,768]{2,1,0:T(8,128)(2,1)S(1)}, bf16[456,128]{1,0:T(8,128)(2,1)}, bf16[456,128]{1,0:T(8,12...) custom-call(s32[1]{0:T(128)} %bitcast.5.place.seq_at, ...), custom_call_target="tpu_custom_call", output_to_operand_aliasing={{0}: (7, {}), {1}: (8, {})} | custom-call | flops 7665352704 | bytes 2801664 | tf_op jit(solution)/shard_map/pallas_call | solution.py:212
  155.9 9.6 %shard_map.327 = f32[912,768]{1,0:T(8,128)} custom-call(bf16[912,3072]{1,0:T(8,128)(2,1)} %get-tuple-element.550.a_ref, bf16[8,768,768]{2,1,0:T(8,128)(2,1)} %bitcast.27), custom_call_target="tpu_custom_call" | custom-call | flops 4303355904 | bytes 13123584 | tf_op jit(solution)/shard_map/pallas_call | solution.py:600
  165.6 4.4 %collective-permute-done.20 = bf16[456,128]{1,0:T(8,128)(2,1)} collective-permute-done((bf16[456,128]{1,0:T(8,128)(2,1)}, bf16[456,128]{1,0:T(8,128)(2,1)}, u32[]{:S(2)}, u32[]{:S(2)}) %collective-permute-start.20) | collective-permute-done | bytes 116768 | tf_op jit(solution)/shard_map/ppermute | solution.py:851
  170.0 14.0 %collective-permute-done.21 = bf16[456,128]{1,0:T(8,128)(2,1)} collective-permute-done((bf16[456,128]{1,0:T(8,128)(2,1)}, bf16[456,128]{1,0:T(8,128)(2,1)}, u32[]{:S(2)}, u32[]{:S(2)}) %collective-permute-start.21) | collective-permute-done | bytes 116768 | tf_op jit(solution)/shard_map/ppermute | solution.py:851
  184.0 13.1 %collective-permute-done.22 = bf16[456,128]{1,0:T(8,128)(2,1)} collective-permute-done((bf16[456,128]{1,0:T(8,128)(2,1)}, bf16[456,128]{1,0:T(8,128)(2,1)}, u32[]{:S(2)}, u32[]{:S(2)}) %collective-permute-start.22) | collective-permute-done | bytes 116768 | tf_op jit(solution)/shard_map/ppermute | solution.py:851
  197.1 9.2 %reduce-scatter.2.cloned.1.call-done = bf16[768,768]{1,0:T(8,128)(2,1)} async-done(((bf16[6144,768]{1,0:T(8,128)(2,1)}), bf16[768,768]{1,0:T(8,128)(2,1)}) %reduce-scatter.2.cloned.1.call-update) | async-done | bytes 1179664 | tf_op jit(solution)/shard_map/reduce_scatter | solution.py:917
  208.9 72.2 %while.22 = (s32[]{:T(128)}, bf16[2,456,768]{2,1,0:T(8,128)(2,1)}, bf16[912,768]{1,0:T(8,128)(2,1)}, bf16[24,1920]{1,0:T(8,128)(2,1)}, bf16[24,1920]{1,0:T(8,128...) while((s32[]{:T(128)}, bf16[2,456,768]{2,1,0:T(8,128)(2,1)}, ...), condition=%wide.region_3.4_spmd, body=%wide.region_2.3_spmd.sunk | while | flops 8606711808 | bytes 48882624 | solution.py:975
  209.1 15.7 %body.24 = (bf16[2,456,768]{2,1,0:T(8,128)(2,1)}, bf16[4,96,1792]{2,1,0:T(8,128)(2,1)}, f32[4,96,1792]{2,1,0:T(8,128)}) custom-call(s32[1]{0:T(128)} %bitcast.23.core_of, f32[2]{0:T(128)S(1)} %get-tuple-element.1016.weight_of, bf16[2,456,768]{2,1,0:T(8,128)(2,1)} %bitcast.30, bf16[2,456,768]{2,1,0:T(8,128)(2,1)} %get-tuple-element.1018.cot_ref, ...), custom_call_target="tpu_custom_call" | custom-call | flops 3227516928 | bytes 11206656 | tf_op jit(solution)/shard_map/while/body/pallas_call | solution.py:551
  224.9 3.3 %collective-permute-done.came = bf16[4,96,1792]{2,1,0:T(8,128)(2,1)S(1)} collective-permute-done((bf16[4,96,1792]{2,1,0:T(8,128)(2,1)}, bf16[4,96,1792]{2,1,0:T(8,128)(2,1)S(1)}, u32[]{:S(2)}, u32[]{:S(2)}) %collective-permute-start) | collective-permute-done | bytes 1376288 | tf_op jit(solution)/shard_map/while/body/ppermute | solution.py:727
  232.9 8.1 %collective-permute-done.1.a = bf16[2,96,896]{2,1,0:T(8,128)(2,1)S(1)} collective-permute-done((bf16[2,96,896]{2,1,0:T(8,128)(2,1)S(1)}, bf16[2,96,896]{2,1,0:T(8,128)(2,1)S(1)}, u32[]{:S(2)}, u32[]{:S(2)}) %collective-permute-start.1) | collective-permute-done | bytes 344096 | tf_op jit(solution)/shard_map/while/body/ppermute | solution.py:727
  244.8 3.4 %collective-permute-done.3.a = bf16[96,896]{1,0:T(8,128)(2,1)S(1)} collective-permute-done((bf16[96,896]{1,0:T(8,128)(2,1)S(1)}, bf16[96,896]{1,0:T(8,128)(2,1)S(1)}, u32[]{:S(2)}, u32[]{:S(2)}) %collective-permute-start.3) | collective-permute-done | bytes 172064 | tf_op jit(solution)/shard_map/while/body/ppermute | solution.py:727
  253.9 11.3 %body.28 = bf16[912,768]{1,0:T(8,128)(2,1)} custom-call(bf16[912,768]{1,0:T(8,128)(2,1)} %get-tuple-element.916.x_ref, bf16[912,768]{1,0:T(8,128)(2,1)} %get-tuple-element.917.o_ref, bf16[768,1536]{1,0:T(8,128)(2,1)S(1)} %get-tuple-element.918.middle_ref.out_w_ref, bf16[912,3072]{1,0:T(8,128)(2,1)} %get-tuple-element.919.f_ref, ...), custom_call_target="tpu_custom_call" | custom-call | flops 5379194880 | bytes 14524416 | tf_op jit(solution)/shard_map/while/body/pallas_call | solution.py:640
  269.8 4.6 %collective-permute-start.8 = (bf16[24,1920]{1,0:T(8,128)(2,1)}, bf16[24,1920]{1,0:T(8,128)(2,1)S(1)}, u32[]{:S(2)}, u32[]{:S(2)}) collective-permute-start(bf16[24,1920]{1,0:T(8,128)(2,1)} %body.29), channel_id=1, source_target_pairs={{0,1},{1,0},{2,3},{3,2},{4,5},{5,4},{6,7},{7,6},{8,9},{9,8},{10,11... | collective-permute-start | bytes 276488 | tf_op jit(solution)/shard_map/while/body/ppermute | solution.py:727
  284.8 12.4 %psum.15 = f32[]{:T(128)} all-reduce(f32[]{:T(128)} %reduce_sum.19), channel_id=1, replica_groups=mesh['batch'=8,'seq'=4] {'batch'}, use_global_device_ids=true, to_apply=%region_6.7 | all-reduce | flops 1 | bytes 8 | tf_op jit(solution)/shard_map/psum | solution.py:978
  297.9 10.1 %shard_map.329 = (f32[96,896]{1,0:T(8,128)}, f32[96,896]{1,0:T(8,128)}, f32[96,896]{1,0:T(8,128)}, f32[96,768]{1,0:T(8,128)}, f32[96,768]{1,0:T(8,128)}, /*index...) custom-call(s32[1]{0:T(128)} %bitcast.5.place.seq_at, ...), custom_call_target="tpu_custom_call" | custom-call | tf_op jit(solution)/shard_map/pallas_call | solution.py:704
  (132 shorter events, 58.1 us)
Async XLA Ops:
  7.2 37.8 %all-gather.3.cloned.1.call-start = ((), (), s32[]{:S(2)}) async-start(), calls=%async_computation.1 | async-start | bytes 2654208 | tf_op jit(solution)/shard_map/all_gather | solution.py:888
  10.1 93.4 %all-gather.5.cloned.1.call-start = ((), (), s32[]{:S(2)}) async-start(), calls=%async_computation.2 | async-start | bytes 10616832 | tf_op jit(solution)/shard_map/all_gather | solution.py:891
  23.7 182.6 %reduce-scatter.2.cloned.1.call-start = ((), (), s32[]{:S(2)}) async-start(), calls=%async_computation.3 | async-start | bytes 10616832 | tf_op jit(solution)/shard_map/reduce_scatter | solution.py:917
  32.7 17.8 %collective-permute-start.11 = (bf16[456,128]{1,0:T(8,128)(2,1)S(1)}, bf16[456,128]{1,0:T(8,128)(2,1)}, u32[]{:S(2)}, u32[]{:S(2)}) collective-permute-start(bf16[456,128]{1,0:T(8,128)(2,1)S(1)} %get-tuple-element.521.refs_0_), channel_id=1, source_target_pairs={{0,1},{1,2},{2,3},{4,5},{5,6},{6,7},{8,9},{9,10},{10,11},{12,13},{... | collective-permute-start | bytes 350216 | tf_op jit(solution)/shard_map/ppermute | solution.py:851
  36.8 13.7 %collective-permute-start.12 = (bf16[456,128]{1,0:T(8,128)(2,1)S(1)}, bf16[456,128]{1,0:T(8,128)(2,1)}, u32[]{:S(2)}, u32[]{:S(2)}) collective-permute-start(bf16[456,128]{1,0:T(8,128)(2,1)S(1)} %get-tuple-element.521.refs_0_), channel_id=1, source_target_pairs={{0,2},{1,3},{4,6},{5,7},{8,10},{9,11},{12,14},{13,15},{16,18},{17,... | collective-permute-start | bytes 350216 | tf_op jit(solution)/shard_map/ppermute | solution.py:851
  41.3 9.2 %collective-permute-start.13 = (bf16[456,128]{1,0:T(8,128)(2,1)S(1)}, bf16[456,128]{1,0:T(8,128)(2,1)}, u32[]{:S(2)}, u32[]{:S(2)}) collective-permute-start(bf16[456,128]{1,0:T(8,128)(2,1)S(1)} %get-tuple-element.521.refs_0_), channel_id=1, source_target_pairs={{0,3},{4,7},{8,11},{12,15},{16,19},{20,23},{24,27},{28,31}} | collective-permute-start | bytes 350216 | tf_op jit(solution)/shard_map/ppermute | solution.py:851
  50.5 24.8 %collective-permute-start.14 = (bf16[456,128]{1,0:T(8,128)(2,1)}, bf16[456,128]{1,0:T(8,128)(2,1)}, u32[]{:S(2)}, u32[]{:S(2)}) collective-permute-start(bf16[456,128]{1,0:T(8,128)(2,1)} %get-tuple-element.534.refs_0_), channel_id=1, source_target_pairs={{0,1},{1,2},{2,3},{4,5},{5,6},{6,7},{8,9},{9,10},{10,11},{12,13},{... | collective-permute-start | bytes 350216 | tf_op jit(solution)/shard_map/ppermute | solution.py:851
  52.5 22.9 %collective-permute-start.15 = (bf16[456,128]{1,0:T(8,128)(2,1)}, bf16[456,128]{1,0:T(8,128)(2,1)}, u32[]{:S(2)}, u32[]{:S(2)}) collective-permute-start(bf16[456,128]{1,0:T(8,128)(2,1)} %get-tuple-element.534.refs_0_), channel_id=1, source_target_pairs={{0,2},{1,3},{4,6},{5,7},{8,10},{9,11},{12,14},{13,15},{16,18},{17,... | collective-permute-start | bytes 350216 | tf_op jit(solution)/shard_map/ppermute | solution.py:851
  56.2 19.2 %collective-permute-start.16 = (bf16[456,128]{1,0:T(8,128)(2,1)}, bf16[456,128]{1,0:T(8,128)(2,1)}, u32[]{:S(2)}, u32[]{:S(2)}) collective-permute-start(bf16[456,128]{1,0:T(8,128)(2,1)} %get-tuple-element.534.refs_0_), channel_id=1, source_target_pairs={{0,3},{4,7},{8,11},{12,15},{16,19},{20,23},{24,27},{28,31}} | collective-permute-start | bytes 350216 | tf_op jit(solution)/shard_map/ppermute | solution.py:851
  129.6 151.5 %all-reduce.2.cloned.1.call-start = ((), (), s32[]{:S(2)}) async-start(), calls=%async_computation.4 | async-start | bytes 2359296 | tf_op jit(solution)/shard_map/psum | solution.py:935
  130.4 24.2 %collective-permute-start.17 = (bf16[456,128]{1,0:T(8,128)(2,1)}, bf16[456,128]{1,0:T(8,128)(2,1)}, u32[]{:S(2)}, u32[]{:S(2)}) collective-permute-start(bf16[456,128]{1,0:T(8,128)(2,1)} %get-tuple-element.531), channel_id=1, source_target_pairs={{1,0},{2,1},{3,2},{5,4},{6,5},{7,6},{9,8},{10,9},{11,10},{13,12},{... | collective-permute-start | bytes 350216 | tf_op jit(solution)/shard_map/ppermute | solution.py:851
  131.7 33.9 %collective-permute-start.18 = (bf16[456,128]{1,0:T(8,128)(2,1)}, bf16[456,128]{1,0:T(8,128)(2,1)}, u32[]{:S(2)}, u32[]{:S(2)}) collective-permute-start(bf16[456,128]{1,0:T(8,128)(2,1)} %get-tuple-element.532), channel_id=1, source_target_pairs={{2,0},{3,1},{6,4},{7,5},{10,8},{11,9},{14,12},{15,13},{18,16},{19,... | collective-permute-start | bytes 350216 | tf_op jit(solution)/shard_map/ppermute | solution.py:851
  133.0 32.6 %collective-permute-start.19 = (bf16[456,128]{1,0:T(8,128)(2,1)}, bf16[456,128]{1,0:T(8,128)(2,1)}, u32[]{:S(2)}, u32[]{:S(2)}) collective-permute-start(bf16[456,128]{1,0:T(8,128)(2,1)} %get-tuple-element.533), channel_id=1, source_target_pairs={{3,0},{7,4},{11,8},{15,12},{19,16},{23,20},{27,24},{31,28}} | collective-permute-start | bytes 350216 | tf_op jit(solution)/shard_map/ppermute | solution.py:851
  152.0 18.0 %collective-permute-start.20 = (bf16[456,128]{1,0:T(8,128)(2,1)}, bf16[456,128]{1,0:T(8,128)(2,1)}, u32[]{:S(2)}, u32[]{:S(2)}) collective-permute-start(bf16[456,128]{1,0:T(8,128)(2,1)} %get-tuple-element.545), channel_id=1, source_target_pairs={{1,0},{2,1},{3,2},{5,4},{6,5},{7,6},{9,8},{10,9},{11,10},{13,12},{... | collective-permute-start | bytes 350216 | tf_op jit(solution)/shard_map/ppermute | solution.py:851
  153.3 30.7 %collective-permute-start.21 = (bf16[456,128]{1,0:T(8,128)(2,1)}, bf16[456,128]{1,0:T(8,128)(2,1)}, u32[]{:S(2)}, u32[]{:S(2)}) collective-permute-start(bf16[456,128]{1,0:T(8,128)(2,1)} %get-tuple-element.546), channel_id=1, source_target_pairs={{2,0},{3,1},{6,4},{7,5},{10,8},{11,9},{14,12},{15,13},{18,16},{19,... | collective-permute-start | bytes 350216 | tf_op jit(solution)/shard_map/ppermute | solution.py:851
  154.6 42.5 %collective-permute-start.22 = (bf16[456,128]{1,0:T(8,128)(2,1)}, bf16[456,128]{1,0:T(8,128)(2,1)}, u32[]{:S(2)}, u32[]{:S(2)}) collective-permute-start(bf16[456,128]{1,0:T(8,128)(2,1)} %get-tuple-element.547), channel_id=1, source_target_pairs={{3,0},{7,4},{11,8},{15,12},{19,16},{23,20},{27,24},{31,28}} | collective-permute-start | bytes 350216 | tf_op jit(solution)/shard_map/ppermute | solution.py:851
  230.8 10.1 %collective-permute-start.1 = (bf16[2,96,896]{2,1,0:T(8,128)(2,1)S(1)}, bf16[2,96,896]{2,1,0:T(8,128)(2,1)S(1)}, u32[]{:S(2)}, u32[]{:S(2)}) collective-permute-start(bf16[2,96,896]{2,1,0:T(8,128)(2,1)S(1)} %get-tuple-element.898), channel_id=1, source_target_pairs={{0,8},{4,12},{8,0},{12,4},{16,24},{20,28},{24,16},{28,20},{1,9},{5... | collective-permute-start | bytes 1032200 | tf_op jit(solution)/shard_map/while/body/ppermute | solution.py:727
  232.2 9.8 %collective-permute-start.2 = (bf16[2,96,896]{2,1,0:T(8,128)(2,1)S(1)}, bf16[2,96,896]{2,1,0:T(8,128)(2,1)S(1)}, u32[]{:S(2)}, u32[]{:S(2)}) collective-permute-start(bf16[2,96,896]{2,1,0:T(8,128)(2,1)S(1)} %get-tuple-element.899), channel_id=1, source_target_pairs={{0,16},{4,20},{8,24},{12,28},{16,0},{20,4},{24,8},{28,12},{1,17},{... | collective-permute-start | bytes 1032200 | tf_op jit(solution)/shard_map/while/body/ppermute | solution.py:727
  249.5 15.7 %collective-permute-start.5 = (bf16[24,1792]{1,0:T(8,128)(2,1)S(1)}, bf16[24,1792]{1,0:T(8,128)(2,1)S(1)}, u32[]{:S(2)}, u32[]{:S(2)}) collective-permute-start(bf16[24,1792]{1,0:T(8,128)(2,1)S(1)} %get-tuple-element.913), channel_id=1, source_target_pairs={{0,1},{1,0},{2,3},{3,2},{4,5},{5,4},{6,7},{7,6},{8,9},{9,8},{10,11... | collective-permute-start | bytes 258056 | tf_op jit(solution)/shard_map/while/body/ppermute | solution.py:727
  251.0 14.7 %collective-permute-start.6 = (bf16[24,1792]{1,0:T(8,128)(2,1)S(1)}, bf16[24,1792]{1,0:T(8,128)(2,1)S(1)}, u32[]{:S(2)}, u32[]{:S(2)}) collective-permute-start(bf16[24,1792]{1,0:T(8,128)(2,1)S(1)} %get-tuple-element.914), channel_id=1, source_target_pairs={{0,2},{1,3},{2,0},{3,1},{4,6},{5,7},{6,4},{7,5},{8,10},{9,11},{10,... | collective-permute-start | bytes 258056 | tf_op jit(solution)/shard_map/while/body/ppermute | solution.py:727
  253.4 12.3 %collective-permute-start.7 = (bf16[24,1792]{1,0:T(8,128)(2,1)S(1)}, bf16[24,1792]{1,0:T(8,128)(2,1)S(1)}, u32[]{:S(2)}, u32[]{:S(2)}) collective-permute-start(bf16[24,1792]{1,0:T(8,128)(2,1)S(1)} %get-tuple-element.915), channel_id=1, source_target_pairs={{0,3},{1,2},{2,1},{3,0},{4,7},{5,6},{6,5},{7,4},{8,11},{9,10},{10,... | collective-permute-start | bytes 258056 | tf_op jit(solution)/shard_map/while/body/ppermute | solution.py:727
  267.0 8.5 %collective-permute-start.10 = (bf16[24,1920]{1,0:T(8,128)(2,1)}, bf16[24,1920]{1,0:T(8,128)(2,1)}, u32[]{:S(2)}, u32[]{:S(2)}) collective-permute-start(bf16[24,1920]{1,0:T(8,128)(2,1)} %body.29), channel_id=1, source_target_pairs={{0,3},{1,2},{2,1},{3,0},{4,7},{5,6},{6,5},{7,4},{8,11},{9,10},{10,... | collective-permute-start | bytes 276488 | tf_op jit(solution)/shard_map/while/body/ppermute | solution.py:727
  269.8 8.2 %collective-permute-start.8 = (bf16[24,1920]{1,0:T(8,128)(2,1)}, bf16[24,1920]{1,0:T(8,128)(2,1)S(1)}, u32[]{:S(2)}, u32[]{:S(2)}) collective-permute-start(bf16[24,1920]{1,0:T(8,128)(2,1)} %body.29), channel_id=1, source_target_pairs={{0,1},{1,0},{2,3},{3,2},{4,5},{5,4},{6,7},{7,6},{8,9},{9,8},{10,11... | collective-permute-start | bytes 276488 | tf_op jit(solution)/shard_map/while/body/ppermute | solution.py:727
  274.4 6.8 %collective-permute-start.9 = (bf16[24,1920]{1,0:T(8,128)(2,1)}, bf16[24,1920]{1,0:T(8,128)(2,1)}, u32[]{:S(2)}, u32[]{:S(2)}) collective-permute-start(bf16[24,1920]{1,0:T(8,128)(2,1)} %body.29), channel_id=1, source_target_pairs={{0,2},{1,3},{2,0},{3,1},{4,6},{5,7},{6,4},{7,5},{8,10},{9,11},{10,... | collective-permute-start | bytes 276488 | tf_op jit(solution)/shard_map/while/body/ppermute | solution.py:727
  (24 other events, 237.9 us)
Sparse Core Ops, SparseCore 0:
  10.5 31.7 all-gather.2
  44.7 58.8 all-gather.4
  129.7 76.4 reduce-scatter.1
  208.5 67.4 all-reduce.1

commit v3 on v2

--- a/solution.py
+++ b/solution.py
@@ -676,16 +676,22 @@
     adam_store(*up, up_grad_ref[...].astype(F32) * factor, up_out, RATE_SMALL, DECAY)
     adam_store(*down, down_grad_ref[...].astype(F32) * factor, down_out, RATE_SMALL, DECAY)
 
-    @pl.when(pl.program_id(0) == pl.num_programs(0) - 1)
+    step = pl.program_id(0)
+
+    @pl.when(step == 0)
     def _():
         for mask, ref in enumerate(parts):
             joined[seq_at[0] ^ mask] = unpack_quarter(ref)
-        rest = joined[...].reshape(-1, joined.shape[2])
-        wide = qkv[0].shape[1]
-        adam_store(*qkv, rest[:, :wide] * factor, qkv_out, RATE_SMALL, DECAY)
-        adam_store(*out, rest[:, wide : wide + D] * factor, out_out, RATE_LARGE, DECAY)
-        grad = rest[:, wide + D :].T[:4] * factor
-        adam_store(*norm, grad, norm_out, RATE_NORM, 0.0)
+
+    rest = joined[step]
+    wide = qkv[0].shape[1]
+    adam_store(*qkv, rest[:, :wide] * factor, qkv_out, RATE_SMALL, DECAY)
+    adam_store(*out, rest[:, wide : wide + D] * factor, out_out, RATE_LARGE, DECAY)
+
+    @pl.when(step == pl.num_programs(0) - 1)
+    def _():
+        norms = joined[:, :, pl.ds(wide + D, 2 * HD)].reshape(-1, 2 * HD)
+        adam_store(*norm, norms.T[:4] * factor, norm_out, RATE_NORM, 0.0)
 
 
 def adam_all(seq_at, factor, feed, rest, qkv, out, up, down, norm):
@@ -694,12 +700,15 @@
     column = pl.BlockSpec((part, width), lambda c, p: (0, c))
     row = pl.BlockSpec((part, width), lambda c, p: (c, 0))
 
+    def quarter(x):
+        return pl.BlockSpec((part // 4, x.shape[1]), lambda c, p: (c, 0))
+
     def whole(x):
         return pl.BlockSpec(x.shape, lambda c, p: (0, 0))
 
     states = [*qkv, *out, *up, *down, *norm]
     specs = (
-        [whole(x) for x in qkv + out] + [column] * 3 + [row] * 3 + [whole(x) for x in norm]
+        [quarter(x) for x in qkv + out] + [column] * 3 + [row] * 3 + [whole(x) for x in norm]
     )
     return pl.pallas_call(
         adam_body,
@@ -931,7 +940,9 @@
 
     grad_up_pre, heads = fence((grad_up_pre, heads))
     grad_second = up_back(grad_up_pre, weights, specs)
-    came, grad_second, feed_sum = fence((came, grad_second, feed_sum))
+    quarter = (-(-part // 4), w_qkv.shape[1] + D + 4 * HD)
+    blanks = [jnp.zeros(quarter, BF)] * 4
+    came, grad_second, feed_sum, blanks = fence((came, grad_second, feed_sum, blanks))
     feed_sum = lax.psum(feed_sum, "seq")
 
     def input_side():
@@ -965,17 +976,16 @@
             parts, layer_out = batch_sum(at, send, keep, output_side, output_inputs)
             return input_grad, layer_out, parts
 
-        quarter = (part // 4, w_qkv.shape[1] + D + 4 * HD)
         unused = (
             second_low,
             query.reshape(count, D),
-            [jnp.zeros(quarter, BF)] * 4,
+            blanks,
         )
         once = 1 + jnp.minimum(tags[0], 0)
         input_grad, layer_out, rest = lax.fori_loop(0, once, rest_of_layer, unused)
         feed_sum, rest = fence((feed_sum, rest))
         (squares,) = local_call(add_squares, at, [*rest, feed_sum], [((1, 2 * HD), F32)])
-        total_squares = lax.psum(jnp.sum(squares), "batch")
+        total_squares = jnp.sum(lax.all_gather(squares, "batch"))
     else:
         input_grad, rest = input_side()
         layer_out = output_side(*output_inputs)

time: 322 us -> 315 us (0.978)
  blocking collectives: 23.6 us -> 20 us
    psum x1 -> x0, blocking collectives: 12.4 us -> none  [shards(): total_squares = lax.psum(jnp.sum(squares), 'batch')]
    all_gather x0 -> x1, blocking collectives: none -> 8.84 us  [shards(): total_squares = jnp.sum(lax.all_gather(squares, 'batch'))]
  transfers between devices with their start and end apart: 27 -> 27, of which waited for: 13 -> 12; matrix products, arithmetic and copies ran while one was open for 3% -> 3% of each run, Pallas kernels for 27% -> 27%
where the time goes in v3:
time: 315 us; the launch traced here: 310 us
  Pallas kernels  121 us (38%)
  waiting for transfers between devices  89.8 us (29%)
  starting transfers between devices  44 us (14%)
  blocking collectives  20 us (6%)
  between operations  16.6 us (5%)
  local copies, waits for them, and re-layouts  11.8 us (4%)
  other arithmetic  6.75 us (2%)
    pallas_call x2, Pallas kernels, attention(): pl.pallas_call(functools.partial(attention_body, local=local, devices=dev...  34.4 us
    ppermute x12, waiting for transfers between devices, shift(): lax.ppermute(x, 'seq', [(s, s + by) for s in range(count) if 0 <= s + by...  31.2 us
    all_gather x1, waiting for transfers between devices, shards(): lax.all_gather(packed, 'batch', axis=0, tiled=True)  27.9 us
    pallas_call x1, Pallas kernels, feed_forward(): pl.pallas_call(functools.partial(feed_body, block=count // 3, direct=dire...  26 us
    ppermute x12, starting transfers between devices, shift(): lax.ppermute(x, 'seq', [(s, s + by) for s in range(count) if 0 <= s + by...  25.1 us
    ppermute x11, waiting for transfers between devices, swap(): lax.ppermute(x, axis, [(i, i ^ mask) for i in range(lax.axis_size(axis))])  20.7 us
    ppermute x11, starting transfers between devices, swap(): lax.ppermute(x, axis, [(i, i ^ mask) for i in range(lax.axis_size(axis))])  18.7 us
    pallas_call x1, Pallas kernels, back(): pl.pallas_call(functools.partial(back_body, devices=len(pairs[0])), grid_...  15.7 us
  transfers between devices with their start and end apart: 27, of which 12 were waited for; matrix products, arithmetic and copies ran while one was open for 3% of the time, Pallas kernels for 27%

profile of v3, /device:TPU:0, one launch (start us, length us, event | category | flops | bytes accessed | tf_op | source)
XLA Modules:
  0.0 309.8 jit_solution(12555711470026228470)
XLA Ops:
  11.3 11.2 %all_gather.15.small_ref = bf16[768,256]{1,0:T(8,128)(2,1)S(1)} all-gather(bf16[96,256]{1,0:T(8,128)(2,1)S(1)} %maximum_maximum_fusion), channel_id=1, replica_groups=mesh['batch'=8,'seq'=4] {'batch'}, dimensions={0}, use_global_device_ids=true | all-gather | bytes 442368 | tf_op jit(solution)/shard_map/all_gather | solution.py:895
  26.9 4.1 %shard_map.322 = (bf16[2,456,768]{2,1,0:T(8,128)(2,1)}, bf16[2,456,768]{2,1,0:T(8,128)(2,1)}, bf16[2,456,128]{2,1,0:T(8,128)(2,1)}) custom-call(bf16[2,456,768]{2,1,0:T(8,128)(2,1)S(1)} %copy-done.3, bf16[768,256]{1,0:T(8,128)(2,1)S(1)} %all_gather.15.small_ref, f32[456,128]{1,0:T(8,128)S(1)} %pad_maximum_fusion.1.cos_ref, ...), custom_call_target="tpu_custom_call" | custom-call | flops 179306496 | bytes 5603328 | tf_op jit(solution)/shard_map/pallas_call | solution.py:421
  32.7 4.1 %collective-permute-start.11 = (bf16[456,128]{1,0:T(8,128)(2,1)}, bf16[456,128]{1,0:T(8,128)(2,1)}, u32[]{:S(2)}, u32[]{:S(2)}) collective-permute-start(bf16[456,128]{1,0:T(8,128)(2,1)} %get-tuple-element.525.refs_0_), channel_id=1, source_target_pairs={{0,1},{1,2},{2,3},{4,5},{5,6},{6,7},{8,9},{9,10},{10,11},{12,13},{... | collective-permute-start | bytes 350216 | tf_op jit(solution)/shard_map/ppermute | solution.py:860
  36.8 4.5 %collective-permute-start.12 = (bf16[456,128]{1,0:T(8,128)(2,1)}, bf16[456,128]{1,0:T(8,128)(2,1)}, u32[]{:S(2)}, u32[]{:S(2)}) collective-permute-start(bf16[456,128]{1,0:T(8,128)(2,1)} %get-tuple-element.525.refs_0_), channel_id=1, source_target_pairs={{0,2},{1,3},{4,6},{5,7},{8,10},{9,11},{12,14},{13,15},{16,18},{17,... | collective-permute-start | bytes 350216 | tf_op jit(solution)/shard_map/ppermute | solution.py:860
  45.0 5.6 %shard_map.323 = (bf16[2,456,768]{2,1,0:T(8,128)(2,1)}, bf16[2,456,768]{2,1,0:T(8,128)(2,1)}) custom-call(bf16[2,456,768]{2,1,0:T(8,128)(2,1)S(1)} %copy-done.6, bf16[2,456,768]{2,1,0:T(8,128)(2,1)} %multiply_convert_fusion.dy_ref, bf16[768,1536]{1,0:T(8,128)(2,1)} %all-gather.5.cloned.1.call-done.weight_ref, f32[456,128]{1,0:T(8,128)} %copy-done.9, ...), custom_call_target="tpu_custom_call" | custom-call | flops 2151677952 | bytes 5603328 | tf_op jit(solution)/shard_map/pallas_call | solution.py:454
  51.9 3.8 %collective-permute-start.15 = (bf16[456,128]{1,0:T(8,128)(2,1)S(1)}, bf16[456,128]{1,0:T(8,128)(2,1)S(1)}, u32[]{:S(2)}, u32[]{:S(2)}) collective-permute-start(bf16[456,128]{1,0:T(8,128)(2,1)S(1)} %get-tuple-element.538.refs_0_), channel_id=1, source_target_pairs={{0,2},{1,3},{4,6},{5,7},{8,10},{9,11},{12,14},{13,15},{16,18},{17,... | collective-permute-start | bytes 350216 | tf_op jit(solution)/shard_map/ppermute | solution.py:860
  57.2 17.1 %shard_map.324 = (bf16[2,456,768]{2,1,0:T(8,128)(2,1)S(1)}, bf16[2,456,768]{2,1,0:T(8,128)(2,1)S(1)}, bf16[456,128]{1,0:T(8,128)(2,1)}, bf16[456,128]{1,0:T(8,12...) custom-call(s32[1]{0:T(128)} %bitcast.5.place.seq_at, bf16[2,456,768]{2,1,0:T(8,128)(2,1)} %get-tuple-element.523.q_ref, ...), custom_call_target="tpu_custom_call" | custom-call | flops 7665352704 | bytes 2801664 | tf_op jit(solution)/shard_map/pallas_call | solution.py:212
  75.7 27.9 %all-gather.7.cloned.1.call-done = bf16[6144,768]{1,0:T(8,128)(2,1)} async-done(((bf16[768,768]{1,0:T(8,128)(2,1)}), bf16[6144,768]{1,0:T(8,128)(2,1)}) %all-gather.7.cloned.1.call-update) | async-done | bytes 9437200 | tf_op jit(solution)/shard_map/all_gather | solution.py:900
  103.6 26.0 %shard_map.325 = (bf16[912,3072]{1,0:T(8,128)(2,1)}, bf16[912,3072]{1,0:T(8,128)(2,1)}, bf16[8,768,768]{2,1,0:T(8,128)(2,1)}) custom-call(bf16[912,768]{1,0:T(8,128)(2,1)} %bitcast.41, bf16[912,768]{1,0:T(8,128)(2,1)} %bitcast.39, bf16[8,768,768]{2,1,0:T(8,128)(2,1)} %bitcast.27, bf16[8,768,768]{2,1,0:T(8,128)(2,1)} %bitcast.28), custom_call_target="tpu_custom_call" | custom-call | flops 17213423616 | bytes 37601280 | tf_op jit(solution)/shard_map/pallas_call | solution.py:337
  133.9 17.2 %shard_map.326 = (bf16[2,456,768]{2,1,0:T(8,128)(2,1)S(1)}, bf16[2,456,768]{2,1,0:T(8,128)(2,1)S(1)}, bf16[456,128]{1,0:T(8,128)(2,1)}, bf16[456,128]{1,0:T(8,12...) custom-call(s32[1]{0:T(128)} %bitcast.5.place.seq_at, ...), custom_call_target="tpu_custom_call", output_to_operand_aliasing={{0}: (7, {}), {1}: (8, {})} | custom-call | flops 7665352704 | bytes 2801664 | tf_op jit(solution)/shard_map/pallas_call | solution.py:212
  155.1 10.1 %shard_map.327 = f32[912,768]{1,0:T(8,128)} custom-call(bf16[912,3072]{1,0:T(8,128)(2,1)} %get-tuple-element.554.a_ref, bf16[8,768,768]{2,1,0:T(8,128)(2,1)} %bitcast.29), custom_call_target="tpu_custom_call" | custom-call | flops 4303355904 | bytes 13123584 | tf_op jit(solution)/shard_map/pallas_call | solution.py:600
  165.2 4.4 %collective-permute-done.20 = bf16[456,128]{1,0:T(8,128)(2,1)} collective-permute-done((bf16[456,128]{1,0:T(8,128)(2,1)}, bf16[456,128]{1,0:T(8,128)(2,1)}, u32[]{:S(2)}, u32[]{:S(2)}) %collective-permute-start.20) | collective-permute-done | bytes 116768 | tf_op jit(solution)/shard_map/ppermute | solution.py:860
  169.6 13.8 %collective-permute-done.21 = bf16[456,128]{1,0:T(8,128)(2,1)} collective-permute-done((bf16[456,128]{1,0:T(8,128)(2,1)}, bf16[456,128]{1,0:T(8,128)(2,1)}, u32[]{:S(2)}, u32[]{:S(2)}) %collective-permute-start.21) | collective-permute-done | bytes 116768 | tf_op jit(solution)/shard_map/ppermute | solution.py:860
  183.4 13.0 %collective-permute-done.22 = bf16[456,128]{1,0:T(8,128)(2,1)} collective-permute-done((bf16[456,128]{1,0:T(8,128)(2,1)}, bf16[456,128]{1,0:T(8,128)(2,1)}, u32[]{:S(2)}, u32[]{:S(2)}) %collective-permute-start.22) | collective-permute-done | bytes 116768 | tf_op jit(solution)/shard_map/ppermute | solution.py:860
  196.4 9.9 %reduce-scatter.2.cloned.1.call-done = bf16[768,768]{1,0:T(8,128)(2,1)} async-done(((bf16[6144,768]{1,0:T(8,128)(2,1)}), bf16[768,768]{1,0:T(8,128)(2,1)}) %reduce-scatter.2.cloned.1.call-update) | async-done | bytes 1179664 | tf_op jit(solution)/shard_map/reduce_scatter | solution.py:926
  208.3 71.1 %while.22 = (s32[]{:T(128)}, bf16[2,456,768]{2,1,0:T(8,128)(2,1)}, bf16[912,768]{1,0:T(8,128)(2,1)}, bf16[24,1920]{1,0:T(8,128)(2,1)}, bf16[24,1920]{1,0:T(8,128...) while((s32[]{:T(128)}, bf16[2,456,768]{2,1,0:T(8,128)(2,1)}, ...), condition=%wide.region_3.4_spmd, body=%wide.region_2.3_spmd.sunk | while | flops 8606711808 | bytes 49251292 | solution.py:985
  208.6 15.7 %body.24 = (bf16[2,456,768]{2,1,0:T(8,128)(2,1)}, bf16[4,96,1792]{2,1,0:T(8,128)(2,1)}, f32[4,96,1792]{2,1,0:T(8,128)}) custom-call(s32[1]{0:T(128)} %bitcast.24.core_of, f32[2]{0:T(128)S(1)} %get-tuple-element.1024.weight_of, bf16[2,456,768]{2,1,0:T(8,128)(2,1)} %bitcast.32, bf16[2,456,768]{2,1,0:T(8,128)(2,1)} %get-tuple-element.1026.cot_ref, ...), custom_call_target="tpu_custom_call" | custom-call | flops 3227516928 | bytes 11206656 | tf_op jit(solution)/shard_map/while/body/pallas_call | solution.py:551
  232.3 8.1 %collective-permute-done.1.a = bf16[2,96,896]{2,1,0:T(8,128)(2,1)S(1)} collective-permute-done((bf16[2,96,896]{2,1,0:T(8,128)(2,1)S(1)}, bf16[2,96,896]{2,1,0:T(8,128)(2,1)S(1)}, u32[]{:S(2)}, u32[]{:S(2)}) %collective-permute-start.1) | collective-permute-done | bytes 344096 | tf_op jit(solution)/shard_map/while/body/ppermute | solution.py:736
  244.3 3.4 %collective-permute-done.3.a = bf16[96,896]{1,0:T(8,128)(2,1)S(1)} collective-permute-done((bf16[96,896]{1,0:T(8,128)(2,1)S(1)}, bf16[96,896]{1,0:T(8,128)(2,1)S(1)}, u32[]{:S(2)}, u32[]{:S(2)}) %collective-permute-start.3) | collective-permute-done | bytes 172064 | tf_op jit(solution)/shard_map/while/body/ppermute | solution.py:736
  253.4 11.2 %body.28 = bf16[912,768]{1,0:T(8,128)(2,1)} custom-call(bf16[912,768]{1,0:T(8,128)(2,1)} %get-tuple-element.924.x_ref, bf16[912,768]{1,0:T(8,128)(2,1)} %get-tuple-element.925.o_ref, bf16[768,1536]{1,0:T(8,128)(2,1)S(1)} %get-tuple-element.926.middle_ref.out_w_ref, bf16[912,3072]{1,0:T(8,128)(2,1)} %get-tuple-element.927.f_ref, ...), custom_call_target="tpu_custom_call" | custom-call | flops 5379194880 | bytes 14524416 | tf_op jit(solution)/shard_map/while/body/pallas_call | solution.py:640
  265.2 3.4 %collective-permute-start.10 = (bf16[24,1920]{1,0:T(8,128)(2,1)S(1)}, bf16[24,1920]{1,0:T(8,128)(2,1)}, u32[]{:S(2)}, u32[]{:S(2)}) collective-permute-start(bf16[24,1920]{1,0:T(8,128)(2,1)S(1)} %body.29), channel_id=1, source_target_pairs={{0,3},{1,2},{2,1},{3,0},{4,7},{5,6},{6,5},{7,4},{8,11},{9,10},{10,... | collective-permute-start | bytes 276488 | tf_op jit(solution)/shard_map/while/body/ppermute | solution.py:736
  268.6 5.2 %collective-permute-start.8 = (bf16[24,1920]{1,0:T(8,128)(2,1)S(1)}, bf16[24,1920]{1,0:T(8,128)(2,1)S(1)}, u32[]{:S(2)}, u32[]{:S(2)}) collective-permute-start(bf16[24,1920]{1,0:T(8,128)(2,1)S(1)} %body.29), channel_id=1, source_target_pairs={{0,1},{1,0},{2,3},{3,2},{4,5},{5,4},{6,7},{7,6},{8,9},{9,8},{10,11... | collective-permute-start | bytes 276488 | tf_op jit(solution)/shard_map/while/body/ppermute | solution.py:736
  282.5 8.8 %all-gather.1 = f32[8,1,128]{2,1,0:T(1,128)S(1)} all-gather(f32[1,1,128]{2,1,0:T(1,128)S(1)} %bitcast.26), channel_id=2, replica_groups=mesh['batch'=8,'seq'=4] {'batch'}, dimensions={0}, use_global_device_ids=true | all-gather | bytes 4608 | tf_op jit(solution)/shard_map/all_gather | solution.py:988
  292.7 9.1 %shard_map.329 = (f32[96,896]{1,0:T(8,128)}, f32[96,896]{1,0:T(8,128)}, f32[96,896]{1,0:T(8,128)}, f32[96,768]{1,0:T(8,128)}, f32[96,768]{1,0:T(8,128)}, /*index...) custom-call(s32[1]{0:T(128)} %bitcast.5.place.seq_at, ...), custom_call_target="tpu_custom_call" | custom-call | tf_op jit(solution)/shard_map/pallas_call | solution.py:713
  (142 shorter events, 55.2 us)
Async XLA Ops:
  7.2 37.8 %all-gather.5.cloned.1.call-start = ((), (), s32[]{:S(2)}) async-start(), calls=%async_computation.1 | async-start | bytes 2654208 | tf_op jit(solution)/shard_map/all_gather | solution.py:897
  10.1 93.4 %all-gather.7.cloned.1.call-start = ((), (), s32[]{:S(2)}) async-start(), calls=%async_computation.2 | async-start | bytes 10616832 | tf_op jit(solution)/shard_map/all_gather | solution.py:900
  23.7 182.6 %reduce-scatter.2.cloned.1.call-start = ((), (), s32[]{:S(2)}) async-start(), calls=%async_computation.3 | async-start | bytes 10616832 | tf_op jit(solution)/shard_map/reduce_scatter | solution.py:926
  32.7 17.9 %collective-permute-start.11 = (bf16[456,128]{1,0:T(8,128)(2,1)}, bf16[456,128]{1,0:T(8,128)(2,1)}, u32[]{:S(2)}, u32[]{:S(2)}) collective-permute-start(bf16[456,128]{1,0:T(8,128)(2,1)} %get-tuple-element.525.refs_0_), channel_id=1, source_target_pairs={{0,1},{1,2},{2,3},{4,5},{5,6},{6,7},{8,9},{9,10},{10,11},{12,13},{... | collective-permute-start | bytes 350216 | tf_op jit(solution)/shard_map/ppermute | solution.py:860
  36.8 13.8 %collective-permute-start.12 = (bf16[456,128]{1,0:T(8,128)(2,1)}, bf16[456,128]{1,0:T(8,128)(2,1)}, u32[]{:S(2)}, u32[]{:S(2)}) collective-permute-start(bf16[456,128]{1,0:T(8,128)(2,1)} %get-tuple-element.525.refs_0_), channel_id=1, source_target_pairs={{0,2},{1,3},{4,6},{5,7},{8,10},{9,11},{12,14},{13,15},{16,18},{17,... | collective-permute-start | bytes 350216 | tf_op jit(solution)/shard_map/ppermute | solution.py:860
  41.3 9.3 %collective-permute-start.13 = (bf16[456,128]{1,0:T(8,128)(2,1)}, bf16[456,128]{1,0:T(8,128)(2,1)}, u32[]{:S(2)}, u32[]{:S(2)}) collective-permute-start(bf16[456,128]{1,0:T(8,128)(2,1)} %get-tuple-element.525.refs_0_), channel_id=1, source_target_pairs={{0,3},{4,7},{8,11},{12,15},{16,19},{20,23},{24,27},{28,31}} | collective-permute-start | bytes 350216 | tf_op jit(solution)/shard_map/ppermute | solution.py:860
  50.6 23.8 %collective-permute-start.14 = (bf16[456,128]{1,0:T(8,128)(2,1)S(1)}, bf16[456,128]{1,0:T(8,128)(2,1)S(1)}, u32[]{:S(2)}, u32[]{:S(2)}) collective-permute-start(bf16[456,128]{1,0:T(8,128)(2,1)S(1)} %get-tuple-element.538.refs_0_), channel_id=1, source_target_pairs={{0,1},{1,2},{2,3},{4,5},{5,6},{6,7},{8,9},{9,10},{10,11},{12,13},{... | collective-permute-start | bytes 350216 | tf_op jit(solution)/shard_map/ppermute | solution.py:860
  51.9 22.5 %collective-permute-start.15 = (bf16[456,128]{1,0:T(8,128)(2,1)S(1)}, bf16[456,128]{1,0:T(8,128)(2,1)S(1)}, u32[]{:S(2)}, u32[]{:S(2)}) collective-permute-start(bf16[456,128]{1,0:T(8,128)(2,1)S(1)} %get-tuple-element.538.refs_0_), channel_id=1, source_target_pairs={{0,2},{1,3},{4,6},{5,7},{8,10},{9,11},{12,14},{13,15},{16,18},{17,... | collective-permute-start | bytes 350216 | tf_op jit(solution)/shard_map/ppermute | solution.py:860
  55.8 18.6 %collective-permute-start.16 = (bf16[456,128]{1,0:T(8,128)(2,1)S(1)}, bf16[456,128]{1,0:T(8,128)(2,1)S(1)}, u32[]{:S(2)}, u32[]{:S(2)}) collective-permute-start(bf16[456,128]{1,0:T(8,128)(2,1)S(1)} %get-tuple-element.538.refs_0_), channel_id=1, source_target_pairs={{0,3},{4,7},{8,11},{12,15},{16,19},{20,23},{24,27},{28,31}} | collective-permute-start | bytes 350216 | tf_op jit(solution)/shard_map/ppermute | solution.py:860
  129.6 149.8 %all-reduce.2.cloned.1.call-start = ((), (), s32[]{:S(2)}) async-start(), calls=%async_computation.4 | async-start | bytes 2359296 | tf_op jit(solution)/shard_map/psum | solution.py:946
  129.8 24.0 %collective-permute-start.17 = (bf16[456,128]{1,0:T(8,128)(2,1)}, bf16[456,128]{1,0:T(8,128)(2,1)}, u32[]{:S(2)}, u32[]{:S(2)}) collective-permute-start(bf16[456,128]{1,0:T(8,128)(2,1)} %get-tuple-element.535), channel_id=1, source_target_pairs={{1,0},{2,1},{3,2},{5,4},{6,5},{7,6},{9,8},{10,9},{11,10},{13,12},{... | collective-permute-start | bytes 350216 | tf_op jit(solution)/shard_map/ppermute | solution.py:860
  131.1 34.1 %collective-permute-start.18 = (bf16[456,128]{1,0:T(8,128)(2,1)}, bf16[456,128]{1,0:T(8,128)(2,1)}, u32[]{:S(2)}, u32[]{:S(2)}) collective-permute-start(bf16[456,128]{1,0:T(8,128)(2,1)} %get-tuple-element.536), channel_id=1, source_target_pairs={{2,0},{3,1},{6,4},{7,5},{10,8},{11,9},{14,12},{15,13},{18,16},{19,... | collective-permute-start | bytes 350216 | tf_op jit(solution)/shard_map/ppermute | solution.py:860
  132.4 32.8 %collective-permute-start.19 = (bf16[456,128]{1,0:T(8,128)(2,1)}, bf16[456,128]{1,0:T(8,128)(2,1)}, u32[]{:S(2)}, u32[]{:S(2)}) collective-permute-start(bf16[456,128]{1,0:T(8,128)(2,1)} %get-tuple-element.537), channel_id=1, source_target_pairs={{3,0},{7,4},{11,8},{15,12},{19,16},{23,20},{27,24},{31,28}} | collective-permute-start | bytes 350216 | tf_op jit(solution)/shard_map/ppermute | solution.py:860
  151.1 18.5 %collective-permute-start.20 = (bf16[456,128]{1,0:T(8,128)(2,1)}, bf16[456,128]{1,0:T(8,128)(2,1)}, u32[]{:S(2)}, u32[]{:S(2)}) collective-permute-start(bf16[456,128]{1,0:T(8,128)(2,1)} %get-tuple-element.549), channel_id=1, source_target_pairs={{1,0},{2,1},{3,2},{5,4},{6,5},{7,6},{9,8},{10,9},{11,10},{13,12},{... | collective-permute-start | bytes 350216 | tf_op jit(solution)/shard_map/ppermute | solution.py:860
  152.4 31.0 %collective-permute-start.21 = (bf16[456,128]{1,0:T(8,128)(2,1)}, bf16[456,128]{1,0:T(8,128)(2,1)}, u32[]{:S(2)}, u32[]{:S(2)}) collective-permute-start(bf16[456,128]{1,0:T(8,128)(2,1)} %get-tuple-element.550), channel_id=1, source_target_pairs={{2,0},{3,1},{6,4},{7,5},{10,8},{11,9},{14,12},{15,13},{18,16},{19,... | collective-permute-start | bytes 350216 | tf_op jit(solution)/shard_map/ppermute | solution.py:860
  153.8 42.7 %collective-permute-start.22 = (bf16[456,128]{1,0:T(8,128)(2,1)}, bf16[456,128]{1,0:T(8,128)(2,1)}, u32[]{:S(2)}, u32[]{:S(2)}) collective-permute-start(bf16[456,128]{1,0:T(8,128)(2,1)} %get-tuple-element.551), channel_id=1, source_target_pairs={{3,0},{7,4},{11,8},{15,12},{19,16},{23,20},{27,24},{31,28}} | collective-permute-start | bytes 350216 | tf_op jit(solution)/shard_map/ppermute | solution.py:860
  230.2 10.2 %collective-permute-start.1 = (bf16[2,96,896]{2,1,0:T(8,128)(2,1)S(1)}, bf16[2,96,896]{2,1,0:T(8,128)(2,1)S(1)}, u32[]{:S(2)}, u32[]{:S(2)}) collective-permute-start(bf16[2,96,896]{2,1,0:T(8,128)(2,1)S(1)} %get-tuple-element.906), channel_id=1, source_target_pairs={{0,8},{4,12},{8,0},{12,4},{16,24},{20,28},{24,16},{28,20},{1,9},{5... | collective-permute-start | bytes 1032200 | tf_op jit(solution)/shard_map/while/body/ppermute | solution.py:736
  231.7 9.8 %collective-permute-start.2 = (bf16[2,96,896]{2,1,0:T(8,128)(2,1)S(1)}, bf16[2,96,896]{2,1,0:T(8,128)(2,1)S(1)}, u32[]{:S(2)}, u32[]{:S(2)}) collective-permute-start(bf16[2,96,896]{2,1,0:T(8,128)(2,1)S(1)} %get-tuple-element.907), channel_id=1, source_target_pairs={{0,16},{4,20},{8,24},{12,28},{16,0},{20,4},{24,8},{28,12},{1,17},{... | collective-permute-start | bytes 1032200 | tf_op jit(solution)/shard_map/while/body/ppermute | solution.py:736
  249.0 15.6 %collective-permute-start.5 = (bf16[24,1792]{1,0:T(8,128)(2,1)S(1)}, bf16[24,1792]{1,0:T(8,128)(2,1)S(1)}, u32[]{:S(2)}, u32[]{:S(2)}) collective-permute-start(bf16[24,1792]{1,0:T(8,128)(2,1)S(1)} %get-tuple-element.921), channel_id=1, source_target_pairs={{0,1},{1,0},{2,3},{3,2},{4,5},{5,4},{6,7},{7,6},{8,9},{9,8},{10,11... | collective-permute-start | bytes 258056 | tf_op jit(solution)/shard_map/while/body/ppermute | solution.py:736
  250.5 14.1 %collective-permute-start.6 = (bf16[24,1792]{1,0:T(8,128)(2,1)S(1)}, bf16[24,1792]{1,0:T(8,128)(2,1)S(1)}, u32[]{:S(2)}, u32[]{:S(2)}) collective-permute-start(bf16[24,1792]{1,0:T(8,128)(2,1)S(1)} %get-tuple-element.922), channel_id=1, source_target_pairs={{0,2},{1,3},{2,0},{3,1},{4,6},{5,7},{6,4},{7,5},{8,10},{9,11},{10,... | collective-permute-start | bytes 258056 | tf_op jit(solution)/shard_map/while/body/ppermute | solution.py:736
  252.9 11.7 %collective-permute-start.7 = (bf16[24,1792]{1,0:T(8,128)(2,1)S(1)}, bf16[24,1792]{1,0:T(8,128)(2,1)S(1)}, u32[]{:S(2)}, u32[]{:S(2)}) collective-permute-start(bf16[24,1792]{1,0:T(8,128)(2,1)S(1)} %get-tuple-element.923), channel_id=1, source_target_pairs={{0,3},{1,2},{2,1},{3,0},{4,7},{5,6},{6,5},{7,4},{8,11},{9,10},{10,... | collective-permute-start | bytes 258056 | tf_op jit(solution)/shard_map/while/body/ppermute | solution.py:736
  265.2 10.0 %collective-permute-start.10 = (bf16[24,1920]{1,0:T(8,128)(2,1)S(1)}, bf16[24,1920]{1,0:T(8,128)(2,1)}, u32[]{:S(2)}, u32[]{:S(2)}) collective-permute-start(bf16[24,1920]{1,0:T(8,128)(2,1)S(1)} %body.29), channel_id=1, source_target_pairs={{0,3},{1,2},{2,1},{3,0},{4,7},{5,6},{6,5},{7,4},{8,11},{9,10},{10,... | collective-permute-start | bytes 276488 | tf_op jit(solution)/shard_map/while/body/ppermute | solution.py:736
  268.6 9.0 %collective-permute-start.8 = (bf16[24,1920]{1,0:T(8,128)(2,1)S(1)}, bf16[24,1920]{1,0:T(8,128)(2,1)S(1)}, u32[]{:S(2)}, u32[]{:S(2)}) collective-permute-start(bf16[24,1920]{1,0:T(8,128)(2,1)S(1)} %body.29), channel_id=1, source_target_pairs={{0,1},{1,0},{2,3},{3,2},{4,5},{5,4},{6,7},{7,6},{8,9},{9,8},{10,11... | collective-permute-start | bytes 276488 | tf_op jit(solution)/shard_map/while/body/ppermute | solution.py:736
  273.8 5.6 %collective-permute-start.9 = (bf16[24,1920]{1,0:T(8,128)(2,1)S(1)}, bf16[24,1920]{1,0:T(8,128)(2,1)}, u32[]{:S(2)}, u32[]{:S(2)}) collective-permute-start(bf16[24,1920]{1,0:T(8,128)(2,1)S(1)} %body.29), channel_id=1, source_target_pairs={{0,2},{1,3},{2,0},{3,1},{4,6},{5,7},{6,4},{7,5},{8,10},{9,11},{10,... | collective-permute-start | bytes 276488 | tf_op jit(solution)/shard_map/while/body/ppermute | solution.py:736
  (29 other events, 273.3 us)
Sparse Core Ops, SparseCore 0:
  10.5 31.7 all-gather.4
  44.7 58.8 all-gather.6
  129.7 76.5 reduce-scatter.1
  208.5 67.6 all-reduce.1

commit v4 on v3

--- a/solution.py
+++ b/solution.py
@@ -736,7 +736,7 @@
     return lax.ppermute(x, axis, [(i, i ^ mask) for i in range(lax.axis_size(axis))])
 
 
-def local_call(body, at, inputs, shapes, scratch=()):
+def local_call(body, at, inputs, shapes, scratch=(), room=VMEM_BYTES // 3):
     return pl.pallas_call(
         body,
         grid_spec=pltpu.PrefetchScalarGridSpec(
@@ -748,7 +748,7 @@
         ),
         out_shape=[jax.ShapeDtypeStruct(s, kind) for s, kind in shapes],
         compiler_params=pltpu.CompilerParams(
-            dimension_semantics=("arbitrary",), vmem_limit_bytes=VMEM_BYTES // 3
+            dimension_semantics=("arbitrary",), vmem_limit_bytes=room
         ),
     )(at, *inputs)
 
@@ -892,8 +892,9 @@
     small = jnp.concatenate(
         [w_qkv[:, D:], norm_params.T, jnp.zeros((part, 2 * HD - 4), F32)], 1
     ).astype(BF)
+    middle = jnp.concatenate([w_qkv[:, :D], w_out], 1).astype(BF)
+    middle, small = fence((middle, small))
     small = lax.all_gather(small, "batch", axis=0, tiled=True)
-    middle = jnp.concatenate([w_qkv[:, :D], w_out], 1).astype(BF)
     middle = lax.all_gather(middle, "batch", axis=0, tiled=True)
     packed = jnp.concatenate([w_down] + [w_up[:, D * i : D * (i + 1)] for i in range(4)], 0)
     packed, small = fence((packed.astype(BF), small))
@@ -984,7 +985,9 @@
         once = 1 + jnp.minimum(tags[0], 0)
         input_grad, layer_out, rest = lax.fori_loop(0, once, rest_of_layer, unused)
         feed_sum, rest = fence((feed_sum, rest))
-        (squares,) = local_call(add_squares, at, [*rest, feed_sum], [((1, 2 * HD), F32)])
+        (squares,) = local_call(
+            add_squares, at, [*rest, feed_sum], [((1, 2 * HD), F32)], room=VMEM_BYTES
+        )
         total_squares = jnp.sum(lax.all_gather(squares, "batch"))
     else:
         input_grad, rest = input_side()

time: 315 us -> 316 us (level)
  transfers between devices with their start and end apart: 27 -> 27, of which waited for: 12 -> 12; matrix products, arithmetic and copies ran while one was open for 3% -> 2% of each run, Pallas kernels for 27% -> 27%
where the time goes in v4:
time: 316 us; the launch traced here: 311 us
  Pallas kernels  121 us (38%)
  waiting for transfers between devices  90 us (28%)
  starting transfers between devices  44.6 us (14%)
  blocking collectives  20.6 us (7%)
  between operations  16.6 us (5%)
  local copies, waits for them, and re-layouts  10.5 us (3%)
  other arithmetic  6.58 us (2%)
    pallas_call x2, Pallas kernels, attention(): pl.pallas_call(functools.partial(attention_body, local=local, devices=dev...  34.4 us
    ppermute x12, waiting for transfers between devices, shift(): lax.ppermute(x, 'seq', [(s, s + by) for s in range(count) if 0 <= s + by...  31.3 us
    all_gather x1, waiting for transfers between devices, shards(): lax.all_gather(packed, 'batch', axis=0, tiled=True)  28.1 us
    pallas_call x1, Pallas kernels, feed_forward(): pl.pallas_call(functools.partial(feed_body, block=count // 3, direct=dire...  25.9 us
    ppermute x12, starting transfers between devices, shift(): lax.ppermute(x, 'seq', [(s, s + by) for s in range(count) if 0 <= s + by...  25.8 us
    ppermute x11, waiting for transfers between devices, swap(): lax.ppermute(x, axis, [(i, i ^ mask) for i in range(lax.axis_size(axis))])  20.7 us
    ppermute x11, starting transfers between devices, swap(): lax.ppermute(x, axis, [(i, i ^ mask) for i in range(lax.axis_size(axis))])  18.7 us
    pallas_call x1, Pallas kernels, back(): pl.pallas_call(functools.partial(back_body, devices=len(pairs[0])), grid_...  15.7 us
  transfers between devices with their start and end apart: 27, of which 12 were waited for; matrix products, arithmetic and copies ran while one was open for 2% of the time, Pallas kernels for 27%

profile of v4, /device:TPU:0, one launch (start us, length us, event | category | flops | bytes accessed | tf_op | source)
XLA Modules:
  0.0 310.7 jit_solution(11509522854189550452)
XLA Ops:
  11.2 11.2 %all_gather.15.small_ref = bf16[768,256]{1,0:T(8,128)(2,1)S(1)} all-gather(bf16[96,256]{1,0:T(8,128)(2,1)S(1)} %maximum_maximum_fusion), channel_id=1, replica_groups=mesh['batch'=8,'seq'=4] {'batch'}, dimensions={0}, use_global_device_ids=true | all-gather | bytes 442368 | tf_op jit(solution)/shard_map/all_gather | solution.py:897
  26.8 4.1 %shard_map.322 = (bf16[2,456,768]{2,1,0:T(8,128)(2,1)}, bf16[2,456,768]{2,1,0:T(8,128)(2,1)}, bf16[2,456,128]{2,1,0:T(8,128)(2,1)}) custom-call(bf16[2,456,768]{2,1,0:T(8,128)(2,1)S(1)} %copy-done.2, bf16[768,256]{1,0:T(8,128)(2,1)S(1)} %all_gather.15.small_ref, f32[456,128]{1,0:T(8,128)S(1)} %pad_maximum_fusion.1.cos_ref, ...), custom_call_target="tpu_custom_call" | custom-call | flops 179306496 | bytes 5603328 | tf_op jit(solution)/shard_map/pallas_call | solution.py:421
  32.5 4.1 %collective-permute-start.11 = (bf16[456,128]{1,0:T(8,128)(2,1)}, bf16[456,128]{1,0:T(8,128)(2,1)}, u32[]{:S(2)}, u32[]{:S(2)}) collective-permute-start(bf16[456,128]{1,0:T(8,128)(2,1)} %get-tuple-element.529.refs_0_), channel_id=1, source_target_pairs={{0,1},{1,2},{2,3},{4,5},{5,6},{6,7},{8,9},{9,10},{10,11},{12,13},{... | collective-permute-start | bytes 350216 | tf_op jit(solution)/shard_map/ppermute | solution.py:860
  36.6 4.5 %collective-permute-start.12 = (bf16[456,128]{1,0:T(8,128)(2,1)}, bf16[456,128]{1,0:T(8,128)(2,1)}, u32[]{:S(2)}, u32[]{:S(2)}) collective-permute-start(bf16[456,128]{1,0:T(8,128)(2,1)} %get-tuple-element.529.refs_0_), channel_id=1, source_target_pairs={{0,2},{1,3},{4,6},{5,7},{8,10},{9,11},{12,14},{13,15},{16,18},{17,... | collective-permute-start | bytes 350216 | tf_op jit(solution)/shard_map/ppermute | solution.py:860
  44.8 5.6 %shard_map.323 = (bf16[2,456,768]{2,1,0:T(8,128)(2,1)}, bf16[2,456,768]{2,1,0:T(8,128)(2,1)}) custom-call(bf16[2,456,768]{2,1,0:T(8,128)(2,1)S(1)} %copy-done.5, bf16[2,456,768]{2,1,0:T(8,128)(2,1)} %multiply_convert_fusion.dy_ref, bf16[768,1536]{1,0:T(8,128)(2,1)} %all-gather.5.cloned.1.call-done.weight_ref, f32[456,128]{1,0:T(8,128)} %copy-done.8, ...), custom_call_target="tpu_custom_call" | custom-call | flops 2151677952 | bytes 5603328 | tf_op jit(solution)/shard_map/pallas_call | solution.py:454
  51.9 4.3 %collective-permute-start.15 = (bf16[456,128]{1,0:T(8,128)(2,1)S(1)}, bf16[456,128]{1,0:T(8,128)(2,1)S(1)}, u32[]{:S(2)}, u32[]{:S(2)}) collective-permute-start(bf16[456,128]{1,0:T(8,128)(2,1)S(1)} %get-tuple-element.542.refs_0_), channel_id=1, source_target_pairs={{0,2},{1,3},{4,6},{5,7},{8,10},{9,11},{12,14},{13,15},{16,18},{17,... | collective-permute-start | bytes 350216 | tf_op jit(solution)/shard_map/ppermute | solution.py:860
  57.7 17.1 %shard_map.324 = (bf16[2,456,768]{2,1,0:T(8,128)(2,1)S(1)}, bf16[2,456,768]{2,1,0:T(8,128)(2,1)S(1)}, bf16[456,128]{1,0:T(8,128)(2,1)}, bf16[456,128]{1,0:T(8,12...) custom-call(s32[1]{0:T(128)} %bitcast.5.place.seq_at, bf16[2,456,768]{2,1,0:T(8,128)(2,1)} %get-tuple-element.527.q_ref, ...), custom_call_target="tpu_custom_call" | custom-call | flops 7665352704 | bytes 2801664 | tf_op jit(solution)/shard_map/pallas_call | solution.py:212
  76.1 28.1 %all-gather.7.cloned.1.call-done = bf16[6144,768]{1,0:T(8,128)(2,1)} async-done(((bf16[768,768]{1,0:T(8,128)(2,1)}), bf16[6144,768]{1,0:T(8,128)(2,1)}) %all-gather.7.cloned.1.call-update) | async-done | bytes 9437200 | tf_op jit(solution)/shard_map/all_gather | solution.py:901
  104.2 25.9 %shard_map.325 = (bf16[912,3072]{1,0:T(8,128)(2,1)}, bf16[912,3072]{1,0:T(8,128)(2,1)}, bf16[8,768,768]{2,1,0:T(8,128)(2,1)}) custom-call(bf16[912,768]{1,0:T(8,128)(2,1)} %bitcast.41, bf16[912,768]{1,0:T(8,128)(2,1)} %bitcast.38, bf16[8,768,768]{2,1,0:T(8,128)(2,1)} %bitcast.26, bf16[8,768,768]{2,1,0:T(8,128)(2,1)} %bitcast.27), custom_call_target="tpu_custom_call" | custom-call | flops 17213423616 | bytes 37601280 | tf_op jit(solution)/shard_map/pallas_call | solution.py:337
  134.5 17.2 %shard_map.326 = (bf16[2,456,768]{2,1,0:T(8,128)(2,1)S(1)}, bf16[2,456,768]{2,1,0:T(8,128)(2,1)S(1)}, bf16[456,128]{1,0:T(8,128)(2,1)}, bf16[456,128]{1,0:T(8,12...) custom-call(s32[1]{0:T(128)} %bitcast.5.place.seq_at, ...), custom_call_target="tpu_custom_call", output_to_operand_aliasing={{0}: (7, {}), {1}: (8, {})} | custom-call | flops 7665352704 | bytes 2801664 | tf_op jit(solution)/shard_map/pallas_call | solution.py:212
  155.7 10.1 %shard_map.327 = f32[912,768]{1,0:T(8,128)} custom-call(bf16[912,3072]{1,0:T(8,128)(2,1)} %get-tuple-element.558.a_ref, bf16[8,768,768]{2,1,0:T(8,128)(2,1)} %bitcast.28), custom_call_target="tpu_custom_call" | custom-call | flops 4303355904 | bytes 13123584 | tf_op jit(solution)/shard_map/pallas_call | solution.py:600
  165.8 4.5 %collective-permute-done.20 = bf16[456,128]{1,0:T(8,128)(2,1)} collective-permute-done((bf16[456,128]{1,0:T(8,128)(2,1)}, bf16[456,128]{1,0:T(8,128)(2,1)}, u32[]{:S(2)}, u32[]{:S(2)}) %collective-permute-start.20) | collective-permute-done | bytes 116768 | tf_op jit(solution)/shard_map/ppermute | solution.py:860
  170.3 13.8 %collective-permute-done.21 = bf16[456,128]{1,0:T(8,128)(2,1)} collective-permute-done((bf16[456,128]{1,0:T(8,128)(2,1)}, bf16[456,128]{1,0:T(8,128)(2,1)}, u32[]{:S(2)}, u32[]{:S(2)}) %collective-permute-start.21) | collective-permute-done | bytes 116768 | tf_op jit(solution)/shard_map/ppermute | solution.py:860
  184.0 13.0 %collective-permute-done.22 = bf16[456,128]{1,0:T(8,128)(2,1)} collective-permute-done((bf16[456,128]{1,0:T(8,128)(2,1)}, bf16[456,128]{1,0:T(8,128)(2,1)}, u32[]{:S(2)}, u32[]{:S(2)}) %collective-permute-start.22) | collective-permute-done | bytes 116768 | tf_op jit(solution)/shard_map/ppermute | solution.py:860
  197.1 9.8 %reduce-scatter.2.cloned.1.call-done = bf16[768,768]{1,0:T(8,128)(2,1)} async-done(((bf16[6144,768]{1,0:T(8,128)(2,1)}), bf16[768,768]{1,0:T(8,128)(2,1)}) %reduce-scatter.2.cloned.1.call-update) | async-done | bytes 1179664 | tf_op jit(solution)/shard_map/reduce_scatter | solution.py:927
  208.9 71.1 %while.22 = (s32[]{:T(128)}, bf16[2,456,768]{2,1,0:T(8,128)(2,1)}, bf16[912,768]{1,0:T(8,128)(2,1)}, bf16[24,1920]{1,0:T(8,128)(2,1)}, bf16[24,1920]{1,0:T(8,128...) while((s32[]{:T(128)}, bf16[2,456,768]{2,1,0:T(8,128)(2,1)}, ...), condition=%wide.region_3.4_spmd, body=%wide.region_2.3_spmd.sunk | while | flops 8606711808 | bytes 49251292 | solution.py:986
  209.2 15.7 %body.24 = (bf16[2,456,768]{2,1,0:T(8,128)(2,1)}, bf16[4,96,1792]{2,1,0:T(8,128)(2,1)}, f32[4,96,1792]{2,1,0:T(8,128)}) custom-call(s32[1]{0:T(128)} %bitcast.24.core_of, f32[2]{0:T(128)S(1)} %get-tuple-element.1028.weight_of, bf16[2,456,768]{2,1,0:T(8,128)(2,1)} %bitcast.31, bf16[2,456,768]{2,1,0:T(8,128)(2,1)} %get-tuple-element.1030.cot_ref, ...), custom_call_target="tpu_custom_call" | custom-call | flops 3227516928 | bytes 11206656 | tf_op jit(solution)/shard_map/while/body/pallas_call | solution.py:551
  233.0 8.1 %collective-permute-done.1.a = bf16[2,96,896]{2,1,0:T(8,128)(2,1)S(1)} collective-permute-done((bf16[2,96,896]{2,1,0:T(8,128)(2,1)S(1)}, bf16[2,96,896]{2,1,0:T(8,128)(2,1)S(1)}, u32[]{:S(2)}, u32[]{:S(2)}) %collective-permute-start.1) | collective-permute-done | bytes 344096 | tf_op jit(solution)/shard_map/while/body/ppermute | solution.py:736
  244.9 3.4 %collective-permute-done.3.a = bf16[96,896]{1,0:T(8,128)(2,1)S(1)} collective-permute-done((bf16[96,896]{1,0:T(8,128)(2,1)S(1)}, bf16[96,896]{1,0:T(8,128)(2,1)S(1)}, u32[]{:S(2)}, u32[]{:S(2)}) %collective-permute-start.3) | collective-permute-done | bytes 172064 | tf_op jit(solution)/shard_map/while/body/ppermute | solution.py:736
  254.0 11.2 %body.28 = bf16[912,768]{1,0:T(8,128)(2,1)} custom-call(bf16[912,768]{1,0:T(8,128)(2,1)} %get-tuple-element.928.x_ref, bf16[912,768]{1,0:T(8,128)(2,1)} %get-tuple-element.929.o_ref, bf16[768,1536]{1,0:T(8,128)(2,1)S(1)} %get-tuple-element.930.middle_ref.out_w_ref, bf16[912,3072]{1,0:T(8,128)(2,1)} %get-tuple-element.931.f_ref, ...), custom_call_target="tpu_custom_call" | custom-call | flops 5379194880 | bytes 14524416 | tf_op jit(solution)/shard_map/while/body/pallas_call | solution.py:640
  265.8 3.4 %collective-permute-start.10 = (bf16[24,1920]{1,0:T(8,128)(2,1)S(1)}, bf16[24,1920]{1,0:T(8,128)(2,1)}, u32[]{:S(2)}, u32[]{:S(2)}) collective-permute-start(bf16[24,1920]{1,0:T(8,128)(2,1)S(1)} %body.29), channel_id=1, source_target_pairs={{0,3},{1,2},{2,1},{3,0},{4,7},{5,6},{6,5},{7,4},{8,11},{9,10},{10,... | collective-permute-start | bytes 276488 | tf_op jit(solution)/shard_map/while/body/ppermute | solution.py:736
  269.2 5.2 %collective-permute-start.8 = (bf16[24,1920]{1,0:T(8,128)(2,1)S(1)}, bf16[24,1920]{1,0:T(8,128)(2,1)S(1)}, u32[]{:S(2)}, u32[]{:S(2)}) collective-permute-start(bf16[24,1920]{1,0:T(8,128)(2,1)S(1)} %body.29), channel_id=1, source_target_pairs={{0,1},{1,0},{2,3},{3,2},{4,5},{5,4},{6,7},{7,6},{8,9},{9,8},{10,11... | collective-permute-start | bytes 276488 | tf_op jit(solution)/shard_map/while/body/ppermute | solution.py:736
  282.8 9.4 %all-gather.1 = f32[8,1,128]{2,1,0:T(1,128)S(1)} all-gather(f32[1,1,128]{2,1,0:T(1,128)} %bitcast.40), channel_id=2, replica_groups=mesh['batch'=8,'seq'=4] {'batch'}, dimensions={0}, use_global_device_ids=true | all-gather | bytes 4608 | tf_op jit(solution)/shard_map/all_gather | solution.py:991
  293.6 9.1 %shard_map.329 = (f32[96,896]{1,0:T(8,128)}, f32[96,896]{1,0:T(8,128)}, f32[96,896]{1,0:T(8,128)}, f32[96,768]{1,0:T(8,128)}, f32[96,768]{1,0:T(8,128)}, /*index...) custom-call(s32[1]{0:T(128)} %bitcast.5.place.seq_at, ...), custom_call_target="tpu_custom_call" | custom-call | tf_op jit(solution)/shard_map/pallas_call | solution.py:713
  (136 shorter events, 54.9 us)
Async XLA Ops:
  7.2 37.6 %all-gather.5.cloned.1.call-start = ((), (), s32[]{:S(2)}) async-start(), calls=%async_computation.1 | async-start | bytes 2654208 | tf_op jit(solution)/shard_map/all_gather | solution.py:898
  11.0 93.2 %all-gather.7.cloned.1.call-start = ((), (), s32[]{:S(2)}) async-start(), calls=%async_computation.2 | async-start | bytes 10616832 | tf_op jit(solution)/shard_map/all_gather | solution.py:901
  23.5 183.4 %reduce-scatter.2.cloned.1.call-start = ((), (), s32[]{:S(2)}) async-start(), calls=%async_computation.3 | async-start | bytes 10616832 | tf_op jit(solution)/shard_map/reduce_scatter | solution.py:927
  32.5 17.9 %collective-permute-start.11 = (bf16[456,128]{1,0:T(8,128)(2,1)}, bf16[456,128]{1,0:T(8,128)(2,1)}, u32[]{:S(2)}, u32[]{:S(2)}) collective-permute-start(bf16[456,128]{1,0:T(8,128)(2,1)} %get-tuple-element.529.refs_0_), channel_id=1, source_target_pairs={{0,1},{1,2},{2,3},{4,5},{5,6},{6,7},{8,9},{9,10},{10,11},{12,13},{... | collective-permute-start | bytes 350216 | tf_op jit(solution)/shard_map/ppermute | solution.py:860
  36.6 13.7 %collective-permute-start.12 = (bf16[456,128]{1,0:T(8,128)(2,1)}, bf16[456,128]{1,0:T(8,128)(2,1)}, u32[]{:S(2)}, u32[]{:S(2)}) collective-permute-start(bf16[456,128]{1,0:T(8,128)(2,1)} %get-tuple-element.529.refs_0_), channel_id=1, source_target_pairs={{0,2},{1,3},{4,6},{5,7},{8,10},{9,11},{12,14},{13,15},{16,18},{17,... | collective-permute-start | bytes 350216 | tf_op jit(solution)/shard_map/ppermute | solution.py:860
  41.1 9.3 %collective-permute-start.13 = (bf16[456,128]{1,0:T(8,128)(2,1)}, bf16[456,128]{1,0:T(8,128)(2,1)}, u32[]{:S(2)}, u32[]{:S(2)}) collective-permute-start(bf16[456,128]{1,0:T(8,128)(2,1)} %get-tuple-element.529.refs_0_), channel_id=1, source_target_pairs={{0,3},{4,7},{8,11},{12,15},{16,19},{20,23},{24,27},{28,31}} | collective-permute-start | bytes 350216 | tf_op jit(solution)/shard_map/ppermute | solution.py:860
  50.4 24.4 %collective-permute-start.14 = (bf16[456,128]{1,0:T(8,128)(2,1)S(1)}, bf16[456,128]{1,0:T(8,128)(2,1)S(1)}, u32[]{:S(2)}, u32[]{:S(2)}) collective-permute-start(bf16[456,128]{1,0:T(8,128)(2,1)S(1)} %get-tuple-element.542.refs_0_), channel_id=1, source_target_pairs={{0,1},{1,2},{2,3},{4,5},{5,6},{6,7},{8,9},{9,10},{10,11},{12,13},{... | collective-permute-start | bytes 350216 | tf_op jit(solution)/shard_map/ppermute | solution.py:860
  51.9 22.9 %collective-permute-start.15 = (bf16[456,128]{1,0:T(8,128)(2,1)S(1)}, bf16[456,128]{1,0:T(8,128)(2,1)S(1)}, u32[]{:S(2)}, u32[]{:S(2)}) collective-permute-start(bf16[456,128]{1,0:T(8,128)(2,1)S(1)} %get-tuple-element.542.refs_0_), channel_id=1, source_target_pairs={{0,2},{1,3},{4,6},{5,7},{8,10},{9,11},{12,14},{13,15},{16,18},{17,... | collective-permute-start | bytes 350216 | tf_op jit(solution)/shard_map/ppermute | solution.py:860
  56.2 18.6 %collective-permute-start.16 = (bf16[456,128]{1,0:T(8,128)(2,1)S(1)}, bf16[456,128]{1,0:T(8,128)(2,1)S(1)}, u32[]{:S(2)}, u32[]{:S(2)}) collective-permute-start(bf16[456,128]{1,0:T(8,128)(2,1)S(1)} %get-tuple-element.542.refs_0_), channel_id=1, source_target_pairs={{0,3},{4,7},{8,11},{12,15},{16,19},{20,23},{24,27},{28,31}} | collective-permute-start | bytes 350216 | tf_op jit(solution)/shard_map/ppermute | solution.py:860
  130.2 149.8 %all-reduce.2.cloned.1.call-start = ((), (), s32[]{:S(2)}) async-start(), calls=%async_computation.4 | async-start | bytes 2359296 | tf_op jit(solution)/shard_map/psum | solution.py:947
  130.4 24.0 %collective-permute-start.17 = (bf16[456,128]{1,0:T(8,128)(2,1)}, bf16[456,128]{1,0:T(8,128)(2,1)}, u32[]{:S(2)}, u32[]{:S(2)}) collective-permute-start(bf16[456,128]{1,0:T(8,128)(2,1)} %get-tuple-element.539), channel_id=1, source_target_pairs={{1,0},{2,1},{3,2},{5,4},{6,5},{7,6},{9,8},{10,9},{11,10},{13,12},{... | collective-permute-start | bytes 350216 | tf_op jit(solution)/shard_map/ppermute | solution.py:860
  131.7 34.1 %collective-permute-start.18 = (bf16[456,128]{1,0:T(8,128)(2,1)}, bf16[456,128]{1,0:T(8,128)(2,1)}, u32[]{:S(2)}, u32[]{:S(2)}) collective-permute-start(bf16[456,128]{1,0:T(8,128)(2,1)} %get-tuple-element.540), channel_id=1, source_target_pairs={{2,0},{3,1},{6,4},{7,5},{10,8},{11,9},{14,12},{15,13},{18,16},{19,... | collective-permute-start | bytes 350216 | tf_op jit(solution)/shard_map/ppermute | solution.py:860
  133.0 32.8 %collective-permute-start.19 = (bf16[456,128]{1,0:T(8,128)(2,1)}, bf16[456,128]{1,0:T(8,128)(2,1)}, u32[]{:S(2)}, u32[]{:S(2)}) collective-permute-start(bf16[456,128]{1,0:T(8,128)(2,1)} %get-tuple-element.541), channel_id=1, source_target_pairs={{3,0},{7,4},{11,8},{15,12},{19,16},{23,20},{27,24},{31,28}} | collective-permute-start | bytes 350216 | tf_op jit(solution)/shard_map/ppermute | solution.py:860
  151.8 18.5 %collective-permute-start.20 = (bf16[456,128]{1,0:T(8,128)(2,1)}, bf16[456,128]{1,0:T(8,128)(2,1)}, u32[]{:S(2)}, u32[]{:S(2)}) collective-permute-start(bf16[456,128]{1,0:T(8,128)(2,1)} %get-tuple-element.553), channel_id=1, source_target_pairs={{1,0},{2,1},{3,2},{5,4},{6,5},{7,6},{9,8},{10,9},{11,10},{13,12},{... | collective-permute-start | bytes 350216 | tf_op jit(solution)/shard_map/ppermute | solution.py:860
  153.1 31.0 %collective-permute-start.21 = (bf16[456,128]{1,0:T(8,128)(2,1)}, bf16[456,128]{1,0:T(8,128)(2,1)}, u32[]{:S(2)}, u32[]{:S(2)}) collective-permute-start(bf16[456,128]{1,0:T(8,128)(2,1)} %get-tuple-element.554), channel_id=1, source_target_pairs={{2,0},{3,1},{6,4},{7,5},{10,8},{11,9},{14,12},{15,13},{18,16},{19,... | collective-permute-start | bytes 350216 | tf_op jit(solution)/shard_map/ppermute | solution.py:860
  154.4 42.7 %collective-permute-start.22 = (bf16[456,128]{1,0:T(8,128)(2,1)}, bf16[456,128]{1,0:T(8,128)(2,1)}, u32[]{:S(2)}, u32[]{:S(2)}) collective-permute-start(bf16[456,128]{1,0:T(8,128)(2,1)} %get-tuple-element.555), channel_id=1, source_target_pairs={{3,0},{7,4},{11,8},{15,12},{19,16},{23,20},{27,24},{31,28}} | collective-permute-start | bytes 350216 | tf_op jit(solution)/shard_map/ppermute | solution.py:860
  230.9 10.2 %collective-permute-start.1 = (bf16[2,96,896]{2,1,0:T(8,128)(2,1)S(1)}, bf16[2,96,896]{2,1,0:T(8,128)(2,1)S(1)}, u32[]{:S(2)}, u32[]{:S(2)}) collective-permute-start(bf16[2,96,896]{2,1,0:T(8,128)(2,1)S(1)} %get-tuple-element.910), channel_id=1, source_target_pairs={{0,8},{4,12},{8,0},{12,4},{16,24},{20,28},{24,16},{28,20},{1,9},{5... | collective-permute-start | bytes 1032200 | tf_op jit(solution)/shard_map/while/body/ppermute | solution.py:736
  232.3 9.8 %collective-permute-start.2 = (bf16[2,96,896]{2,1,0:T(8,128)(2,1)S(1)}, bf16[2,96,896]{2,1,0:T(8,128)(2,1)S(1)}, u32[]{:S(2)}, u32[]{:S(2)}) collective-permute-start(bf16[2,96,896]{2,1,0:T(8,128)(2,1)S(1)} %get-tuple-element.911), channel_id=1, source_target_pairs={{0,16},{4,20},{8,24},{12,28},{16,0},{20,4},{24,8},{28,12},{1,17},{... | collective-permute-start | bytes 1032200 | tf_op jit(solution)/shard_map/while/body/ppermute | solution.py:736
  249.6 15.6 %collective-permute-start.5 = (bf16[24,1792]{1,0:T(8,128)(2,1)S(1)}, bf16[24,1792]{1,0:T(8,128)(2,1)S(1)}, u32[]{:S(2)}, u32[]{:S(2)}) collective-permute-start(bf16[24,1792]{1,0:T(8,128)(2,1)S(1)} %get-tuple-element.925), channel_id=1, source_target_pairs={{0,1},{1,0},{2,3},{3,2},{4,5},{5,4},{6,7},{7,6},{8,9},{9,8},{10,11... | collective-permute-start | bytes 258056 | tf_op jit(solution)/shard_map/while/body/ppermute | solution.py:736
  251.1 14.1 %collective-permute-start.6 = (bf16[24,1792]{1,0:T(8,128)(2,1)S(1)}, bf16[24,1792]{1,0:T(8,128)(2,1)S(1)}, u32[]{:S(2)}, u32[]{:S(2)}) collective-permute-start(bf16[24,1792]{1,0:T(8,128)(2,1)S(1)} %get-tuple-element.926), channel_id=1, source_target_pairs={{0,2},{1,3},{2,0},{3,1},{4,6},{5,7},{6,4},{7,5},{8,10},{9,11},{10,... | collective-permute-start | bytes 258056 | tf_op jit(solution)/shard_map/while/body/ppermute | solution.py:736
  253.5 11.7 %collective-permute-start.7 = (bf16[24,1792]{1,0:T(8,128)(2,1)S(1)}, bf16[24,1792]{1,0:T(8,128)(2,1)S(1)}, u32[]{:S(2)}, u32[]{:S(2)}) collective-permute-start(bf16[24,1792]{1,0:T(8,128)(2,1)S(1)} %get-tuple-element.927), channel_id=1, source_target_pairs={{0,3},{1,2},{2,1},{3,0},{4,7},{5,6},{6,5},{7,4},{8,11},{9,10},{10,... | collective-permute-start | bytes 258056 | tf_op jit(solution)/shard_map/while/body/ppermute | solution.py:736
  265.8 10.0 %collective-permute-start.10 = (bf16[24,1920]{1,0:T(8,128)(2,1)S(1)}, bf16[24,1920]{1,0:T(8,128)(2,1)}, u32[]{:S(2)}, u32[]{:S(2)}) collective-permute-start(bf16[24,1920]{1,0:T(8,128)(2,1)S(1)} %body.29), channel_id=1, source_target_pairs={{0,3},{1,2},{2,1},{3,0},{4,7},{5,6},{6,5},{7,4},{8,11},{9,10},{10,... | collective-permute-start | bytes 276488 | tf_op jit(solution)/shard_map/while/body/ppermute | solution.py:736
  269.2 9.0 %collective-permute-start.8 = (bf16[24,1920]{1,0:T(8,128)(2,1)S(1)}, bf16[24,1920]{1,0:T(8,128)(2,1)S(1)}, u32[]{:S(2)}, u32[]{:S(2)}) collective-permute-start(bf16[24,1920]{1,0:T(8,128)(2,1)S(1)} %body.29), channel_id=1, source_target_pairs={{0,1},{1,0},{2,3},{3,2},{4,5},{5,4},{6,7},{7,6},{8,9},{9,8},{10,11... | collective-permute-start | bytes 276488 | tf_op jit(solution)/shard_map/while/body/ppermute | solution.py:736
  274.5 5.6 %collective-permute-start.9 = (bf16[24,1920]{1,0:T(8,128)(2,1)S(1)}, bf16[24,1920]{1,0:T(8,128)(2,1)}, u32[]{:S(2)}, u32[]{:S(2)}) collective-permute-start(bf16[24,1920]{1,0:T(8,128)(2,1)S(1)} %body.29), channel_id=1, source_target_pairs={{0,2},{1,3},{2,0},{3,1},{4,6},{5,7},{6,4},{7,5},{8,10},{9,11},{10,... | collective-permute-start | bytes 276488 | tf_op jit(solution)/shard_map/while/body/ppermute | solution.py:736
  (26 other events, 262.5 us)
Sparse Core Ops, SparseCore 0:
  11.2 31.7 all-gather.4
  45.4 58.8 all-gather.6
  130.3 76.4 reduce-scatter.1
  209.1 67.6 all-reduce.1
